TPU v7x, 32 devices: a whole 2x2x4 slice. The times are simulated.
32 devices in a mesh: tile: 8 (over z, y), mem: 4 (over x, core).
Axes of the slice: x: 2, y: 2, z: 4, core: 2. Of those that a mesh axis runs over, the one named last changes fastest.
Arguments:
- control: bfloat16 [32, 16, 24576], P('mem', None, 'tile'), may hold values from -6 to 6
- ensemble: bfloat16 [32, 16, 24576], P('mem', None, 'tile'), may hold values from -1 to 1
- vertical_loc: bfloat16 [16, 16], replicated, may hold values from -1.5 to 1.5
- blocks: bfloat16 [192, 7, 128, 128], P('tile'), as said below
- edge_mask: int32 [192, 7], P('tile'), may hold values from 0 to 1, as said below
- background: float32 [16, 24576], P(None, 'tile'), may hold values from -6 to 6
- obs_precision: float32 [16, 24576], P(None, 'tile'), may hold values from 1 to 10
Outputs:
- increment: float32 [16, 24576], P('mem', 'tile')
- gradient: float32 [32, 16, 24576], P('mem', None, 'tile')
Inputs may be any that keep to these rules, and one draw needn't show every extreme that they name: `edge_mask`: each entry is 0 or 1; slot 0 is 1 for every tile; slot 2d of tile (t + d) mod 192 equals slot 2d-1 of tile t. Slot 0 blocks are symmetric, and the block in slot 2d of tile (t + d) mod 192 is the transpose of the block in slot 2d-1 of tile t, so that Lh is symmetric.
All inputs are finite; a program needn't handle non-finite values.
Results may differ from a plain program's by a relative error of at most 0.011.
Values may be sent and summed in bfloat16 or wider, within the bound.
No kernel may reach another device: no remote copies, remote signals or barrier semaphores. Data moves between devices by JAX's collectives and lax.ppermute only.
A program may use at most 64 MiB of HBM per device.

v0:
```python
import jax
import jax.numpy as jnp
from jax import lax
from jax.sharding import PartitionSpec as P


def padded_2(value, sides, width):
    for axis, dim in sides:
        size, length = (lax.axis_size(axis), value.shape[dim])
        up = [(i, (i + 1) % size) for i in range(size)]
        down = [(j, i) for i, j in up]
        last = lax.slice_in_dim(value, length - width, length, axis=dim)
        first = lax.slice_in_dim(value, 0, width, axis=dim)
        before = lax.ppermute(last, axis, up)
        after = lax.ppermute(first, axis, down)
        value = jnp.concatenate([before, value, after], axis=dim)
    return value


def passed_along(value, axis, by):
    length = lax.axis_size(axis)
    return lax.ppermute(value, axis, [(i, (i + by) % length) for i in range(length)])


def slot_offset(slot_index):
    if slot_index == 0:
        return 0
    distance = (slot_index + 1) // 2
    if slot_index % 2 == 1:
        return distance
    return -distance


def apply_rows(padded, blocks, edge_mask, tile_count):
    member_count, level_count, padded_points = padded.shape
    block_width = blocks.shape[-1]
    padded_tiles = padded.reshape(
        member_count, level_count, padded_points // block_width, block_width
    )
    reach_tiles = (padded_points // block_width - tile_count) // 2
    mask_float = edge_mask.astype(jnp.float32)
    summed = jnp.zeros((member_count, level_count, tile_count, block_width), jnp.float32)
    for slot_index in range(blocks.shape[1]):
        offset = slot_offset(slot_index)
        source = padded_tiles[:, :, reach_tiles + offset : reach_tiles + offset + tile_count]
        product = jnp.einsum(
            "tab,kltb->klta", blocks[:, slot_index], source, preferred_element_type=jnp.float32
        )
        summed = summed + mask_float[None, None, :, slot_index, None] * product
    return summed


def on_device(control, ensemble, vertical_loc, blocks, edge_mask, background, obs_precision):
    member_count, level_count, point_count = control.shape
    block_width = blocks.shape[-1]
    tile_count = point_count // block_width
    reach_tiles = (blocks.shape[1] - 1) // 2
    vertical = jnp.einsum(
        "lm,kmh->klh", vertical_loc, control, preferred_element_type=jnp.float32
    ).astype(jnp.bfloat16)
    padded = padded_2(vertical, (("tile", 2),), reach_tiles * block_width)
    localized = apply_rows(padded, blocks, edge_mask, tile_count).reshape(
        member_count, level_count, point_count
    )
    partial_sum = jnp.sum(ensemble.astype(jnp.float32) * localized, axis=0)
    row_count = level_count // lax.axis_size("mem")
    first_row = lax.axis_index("mem") * row_count
    summed_total = lax.psum(partial_sum, "mem")
    increment = lax.dynamic_slice_in_dim(summed_total, first_row, row_count, 0)
    depart = (obs_precision * (summed_total - background)).astype(jnp.bfloat16)
    weighted = (ensemble.astype(jnp.float32) * depart.astype(jnp.float32)[None]).astype(
        jnp.bfloat16
    )
    weighted_tiles = weighted.reshape(member_count, level_count, tile_count, block_width)
    mask_float = edge_mask.astype(jnp.float32)
    extended = jnp.zeros(
        (member_count, level_count, tile_count + 2 * reach_tiles, block_width), jnp.float32
    )
    for slot_index in range(blocks.shape[1]):
        offset = slot_offset(slot_index)
        contrib = jnp.einsum(
            "tab,klta->kltb",
            blocks[:, slot_index],
            weighted_tiles,
            preferred_element_type=jnp.float32,
        )
        contrib = mask_float[None, None, :, slot_index, None] * contrib
        extended = extended.at[:, :, reach_tiles + offset : reach_tiles + offset + tile_count].add(
            contrib
        )
    left_rim = extended[:, :, :reach_tiles]
    right_rim = extended[:, :, reach_tiles + tile_count :]
    from_left = passed_along(right_rim, "tile", 1)
    from_right = passed_along(left_rim, "tile", -1)
    interior = extended[:, :, reach_tiles : reach_tiles + tile_count]
    interior = interior.at[:, :, :reach_tiles].add(from_left)
    interior = interior.at[:, :, tile_count - reach_tiles :].add(from_right)
    adjoint = interior.reshape(member_count, level_count, point_count)
    gradient = control.astype(jnp.float32) + jnp.einsum(
        "ml,kmh->klh", vertical_loc.astype(jnp.float32), adjoint, precision=lax.Precision.HIGHEST
    )
    return (increment, gradient)


def solution(mesh):
    in_specs = (
        P("mem", None, "tile"),
        P("mem", None, "tile"),
        P(),
        P("tile", None, None, None),
        P("tile", None),
        P(None, "tile"),
        P(None, "tile"),
    )
    out_specs = (P("mem", "tile"), P("mem", None, "tile"))
    return jax.shard_map(
        on_device, mesh=mesh, in_specs=in_specs, out_specs=out_specs, check_vma=False
    )
```

profile of v0, /device:TPU:0, one launch (start us, length us, event | category | flops | bytes accessed | tf_op | source)
XLA Modules:
  0.0 100.6 jit_solution(4137713650633322076)
XLA Ops:
  7.2 0.0 copy-start
  7.2 0.0 copy-start.5
  7.2 0.0 all-reduce.3.cloned.1.call-start
  7.2 0.6 copy-done
  7.9 1.5 %fusion.1 = bf16[8,16,3072]{2,1,0:T(8,128)(2,1)S(1)} fusion(bf16[8,16,3072]{2,1,0:T(8,128)(2,1)} %param.25, bf16[16,16]{1,0:T(8,128)(2,1)S(1)} %copy-done), kind=kOutput, calls=%fused_computation.3 | convolution fusion | flops 12976128 | bytes 1573376 | tf_op jit(solution)/shard_map/lm,kmh->klh/dot_general | solution.py:58
  9.4 3.0 %collective-permute-start = (bf16[8,16,384]{2,1,0:T(8,128)(2,1)S(1)}, bf16[8,16,384]{2,1,0:T(8,128)(2,1)S(1)}, u32[]{:S(2)}, u32[]{:S(2)}) collective-permute-start(bf16[8,16,384]{2,1,0:T(8,128)(2,1)S(1)} %get-tuple-element.119), channel_id=1, source_target_pairs={{0,4},{4,8},{8,12},{12,16},{16,20},{20,24},{24,28},{28,0},{1,5},{5... | collective-permute-start | bytes 294920 | tf_op jit(solution)/shard_map/ppermute | solution.py:14
  12.4 3.1 %collective-permute-start.1 = (bf16[8,16,384]{2,1,0:T(8,128)(2,1)S(1)}, bf16[8,16,384]{2,1,0:T(8,128)(2,1)S(1)}, u32[]{:S(2)}, u32[]{:S(2)}) collective-permute-start(bf16[8,16,384]{2,1,0:T(8,128)(2,1)S(1)} %get-tuple-element.120), channel_id=1, source_target_pairs={{4,0},{8,4},{12,8},{16,12},{20,16},{24,20},{28,24},{0,28},{5,1},{9... | collective-permute-start | bytes 294920 | tf_op jit(solution)/shard_map/ppermute | solution.py:15
  15.5 0.0 copy-done.5
  15.5 2.8 %collective-permute-done = bf16[8,16,384]{2,1,0:T(8,128)(2,1)S(1)} collective-permute-done((bf16[8,16,384]{2,1,0:T(8,128)(2,1)S(1)}, bf16[8,16,384]{2,1,0:T(8,128)(2,1)S(1)}, u32[]{:S(2)}, u32[]{:S(2)}) %collective-permute-start) | collective-permute-done | bytes 98336 | tf_op jit(solution)/shard_map/ppermute | solution.py:14
  18.3 0.8 collective-permute-done.1
  19.1 0.1 pad_maximum_fusion
  19.2 0.6 reshape.325
  19.8 1.4 %fusion.73 = (bf16[8,16,24,128]{3,2,1,0:T(8,128)(2,1)S(1)}, bf16[8,16,24,128]{3,2,1,0:T(8,128)(2,1)S(1)}, bf16[8,16,24,128]{3,2,1,0:T(8,128)(2,1)S(1)}, bf16[8,1...) fusion(bf16[8,16,30,128]{3,2,1,0:T(8,128)(2,1)S(1)} %reshape.325), kind=kLoop, calls=%fused_computation.98 | loop fusion | bytes 11010048 | tf_op jit(solution)/shard_map/slice | solution.py:45
  21.2 1.8 %fusion.22 = f32[24,8,16,128]{3,2,1,0:T(8,128)S(1)} fusion(bf16[8,16,24,128]{3,2,1,0:T(8,128)(2,1)S(1)} %get-tuple-element.113, bf16[24,7,128,128]{3,2,1,0:T(8,128)(2,1)} %param.28), kind=kOutput, calls=%fused_computation.35 | convolution fusion | flops 100663296 | bytes 3145728 | tf_op jit(solution)/shard_map/tab,kltb->klta/dot_general | solution.py:46
  23.0 1.8 %fusion.25 = f32[24,8,16,128]{3,2,1,0:T(8,128)S(1)} fusion(bf16[8,16,24,128]{3,2,1,0:T(8,128)(2,1)S(1)} %get-tuple-element.114, bf16[24,7,128,128]{3,2,1,0:T(8,128)(2,1)} %param.28), kind=kOutput, calls=%fused_computation.38 | convolution fusion | flops 100663296 | bytes 3145728 | tf_op jit(solution)/shard_map/tab,kltb->klta/dot_general | solution.py:46
  24.8 1.8 %fusion.28 = f32[24,8,16,128]{3,2,1,0:T(8,128)S(1)} fusion(bf16[8,16,24,128]{3,2,1,0:T(8,128)(2,1)S(1)} %get-tuple-element.115, bf16[24,7,128,128]{3,2,1,0:T(8,128)(2,1)} %param.28), kind=kOutput, calls=%fused_computation.41 | convolution fusion | flops 100663296 | bytes 3145728 | tf_op jit(solution)/shard_map/tab,kltb->klta/dot_general | solution.py:46
  26.6 1.8 %fusion.31 = f32[24,8,16,128]{3,2,1,0:T(8,128)S(1)} fusion(bf16[8,16,24,128]{3,2,1,0:T(8,128)(2,1)S(1)} %get-tuple-element.116, bf16[24,7,128,128]{3,2,1,0:T(8,128)(2,1)} %param.28), kind=kOutput, calls=%fused_computation.44 | convolution fusion | flops 100663296 | bytes 3145728 | tf_op jit(solution)/shard_map/tab,kltb->klta/dot_general | solution.py:46
  28.4 1.8 %fusion.34 = f32[24,8,16,128]{3,2,1,0:T(8,128)S(1)} fusion(bf16[8,16,24,128]{3,2,1,0:T(8,128)(2,1)S(1)} %get-tuple-element.117, bf16[24,7,128,128]{3,2,1,0:T(8,128)(2,1)} %param.28), kind=kOutput, calls=%fused_computation.47 | convolution fusion | flops 100663296 | bytes 3145728 | tf_op jit(solution)/shard_map/tab,kltb->klta/dot_general | solution.py:46
  30.2 1.8 %fusion.37 = f32[24,8,16,128]{3,2,1,0:T(8,128)S(1)} fusion(bf16[8,16,24,128]{3,2,1,0:T(8,128)(2,1)S(1)} %get-tuple-element.118, bf16[24,7,128,128]{3,2,1,0:T(8,128)(2,1)} %param.28), kind=kOutput, calls=%fused_computation.50 | convolution fusion | flops 100663296 | bytes 3145728 | tf_op jit(solution)/shard_map/tab,kltb->klta/dot_general | solution.py:46
  32.0 0.0 copy-start.1
  32.0 2.3 %add_bitcast_fusion = f32[24,8,2,8,128]{4,3,2,1,0:T(8,128)S(1)} fusion(f32[24,8,16,128]{3,2,1,0:T(8,128)S(1)} %fusion.22, f32[24,8,16,128]{3,2,1,0:T(8,128)S(1)} %fusion.25, f32[24,8,16,128]{3,2,1,0:T(8,128)S(1)} %fusion.28, f32[24,8,16,128]{3,2,1,0:T(8,128)S(1)} %fusion.31, f32[24,8,16,128]{3,2,1,0:T(8,128)S(1)} %fusion.34, ...), kind=kOutput, calls=%fused_computation.21 | convolution fusion | flops 105775104 | bytes 12583584 | tf_op jit(solution)/shard_map/tab,kltb->klta/dot_general | solution.py:46
  34.3 0.0 copy-done.1
  34.3 0.0 copy-start.3
  34.4 0.0 copy-start.4
  34.4 0.9 fusion.2
  35.3 0.0 all-reduce.3.cloned.1.call-update
  35.3 32.3 %all-reduce.3.cloned.1.call-done = f32[16,3072]{1,0:T(8,128)} async-done(((f32[16,3072]{1,0:T(8,128)}), f32[16,3072]{1,0:T(8,128)}) %all-reduce.3.cloned.1.call-update) | async-done | bytes 196624 | tf_op jit(solution)/shard_map/psum | solution.py:68
  67.6 0.0 copy-done.3
  67.6 0.0 copy-done.4
  67.6 1.0 fusion.69
  68.6 1.7 %multiply_bitcast_fusion = f32[8,16,24,128]{3,1,0,2:T(8,128)S(1)} fusion(f32[24]{0:T(128)S(1)} %get-tuple-element.121, bf16[24,7,128,128]{3,2,1,0:T(8,128)(2,1)} %param.28, bf16[8,16,3072]{2,1,0:T(8,128)(2,1)S(1)} %copy-done.1, f32[16,3072]{1,0:T(8,128)S(1)} %fusion.69), kind=kOutput, calls=%fused_computation.22 | convolution fusion | flops 102236160 | bytes 3342432 | tf_op jit(solution)/shard_map/tab,klta->kltb/dot_general | solution.py:81
  70.3 0.0 slice-start.1
  70.3 0.2 scatter-add.30
  70.5 1.8 %fusion.10 = f32[8,16,30,128]{3,1,0,2:T(8,128)S(1)} fusion(f32[8,16,30,128]{3,1,0,2:T(8,128)S(1)} %scatter-add.30, f32[24]{0:T(128)S(1)} %get-tuple-element.127, bf16[24,7,128,128]{3,2,1,0:T(8,128)(2,1)} %param.28, bf16[8,16,3072]{2,1,0:T(8,128)(2,1)S(1)} %copy-done.1, f32[16,3072]{1,0:T(8,128)S(1)} %fusion.69), kind=kOutput, calls=%fused_computation.20 | convolution fusion | flops 102629376 | bytes 4915712 | tf_op jit(solution)/shard_map/tab,klta->kltb/dot_general | solution.py:81
  72.3 0.5 fusion.9
  72.9 0.5 fusion.8
  73.4 0.5 fusion.7
  74.0 0.5 fusion.6
  74.5 1.8 %constant_dynamic-update-slice_fusion = (f32[8,16,30,128]{3,1,0,2:T(8,128)S(1)}, f32[8,16,24,128]{3,1,0,2:T(8,128)}) fusion(f32[8,16,30,128]{3,1,0,2:T(8,128)S(1)} %fusion.6, bf16[24,7,128,128]{3,2,1,0:T(8,128)(2,1)S(1)} %bitcast.161, f32[24]{0:T(128)S(1)} %get-tuple-element.122, bf16[8,16,3072]{2,1,0:T(8,128)(2,1)S(1)} %copy-done.1, f32[16,3072]{1,0:T(8,128)S(1)} %fusion.69), kind=kOutput, calls=%fused_computation.88 | convolution fusion | flops 102629376 | bytes 6488576 | tf_op jit(solution)/shard_map/tab,klta->kltb/dot_general | solution.py:81
  76.3 1.5 %collective-permute-start.2 = (f32[8,16,3,128]{3,1,0,2:T(8,128)S(1)}, f32[8,16,3,128]{3,1,0,2:T(8,128)S(1)}, u32[]{:S(2)}, u32[]{:S(2)}) collective-permute-start(f32[8,16,3,128]{3,1,0,2:T(8,128)S(1)} %slice.403), channel_id=1, source_target_pairs={{0,4},{4,8},{8,12},{12,16},{16,20},{20,24},{24,28},{28,0},{1,5},{5... | collective-permute-start | bytes 589832 | tf_op jit(solution)/shard_map/ppermute | solution.py:22
  77.8 0.1 slice.401
  78.0 0.0 copy-start.2
  78.0 6.7 %collective-permute-done.2 = f32[8,16,3,128]{3,1,0,2:T(8,128)S(1)} collective-permute-done((f32[8,16,3,128]{3,1,0,2:T(8,128)S(1)}, f32[8,16,3,128]{3,1,0,2:T(8,128)S(1)}, u32[]{:S(2)}, u32[]{:S(2)}) %collective-permute-start.2) | collective-permute-done | bytes 196640 | tf_op jit(solution)/shard_map/ppermute | solution.py:22
  84.7 1.1 %fusion.72 = (f32[8,16,3,128]{3,1,0,2:T(8,128)S(1)}, f32[8,16,24,128]{3,1,0,2:T(8,128)S(1)}) fusion(f32[8,16,24,128]{3,1,0,2:T(8,128)} %get-tuple-element.129, f32[8,16,24,128]{3,1,0,2:T(8,128)S(1)} %slice.401, f32[8,16,3,128]{3,1,0,2:T(8,128)S(1)} %collective-permute-done.2), kind=kLoop, calls=%fused_computation.97 | loop fusion | flops 49152 | bytes 983040 | tf_op jit(solution)/shard_map/slice | solution.py:91
  85.8 1.6 %collective-permute-start.3 = (f32[8,16,3,128]{3,1,0,2:T(8,128)S(1)}, f32[8,16,3,128]{3,1,0,2:T(8,128)S(1)}, u32[]{:S(2)}, u32[]{:S(2)}) collective-permute-start(f32[8,16,3,128]{3,1,0,2:T(8,128)S(1)} %get-tuple-element.110), channel_id=1, source_target_pairs={{0,28},{4,0},{8,4},{12,8},{16,12},{20,16},{24,20},{28,24},{1,29},{... | collective-permute-start | bytes 589832 | tf_op jit(solution)/shard_map/ppermute | solution.py:22
  87.4 1.5 %constant_dynamic-slice_fusion = f32[4,3072]{1,0:T(4,128)} fusion(f32[16,3072]{1,0:T(8,128)} %all-reduce.3.cloned.1.call-done, s32[]{:T(128)S(6)} %select_n.3), kind=kLoop, calls=%fused_computation.89 | loop fusion | bytes 98308 | tf_op jit(solution)/shard_map/dynamic_slice | solution.py:69
  88.9 2.6 %collective-permute-done.3 = f32[8,16,3,128]{3,1,0,2:T(8,128)S(1)} collective-permute-done((f32[8,16,3,128]{3,1,0,2:T(8,128)S(1)}, f32[8,16,3,128]{3,1,0,2:T(8,128)S(1)}, u32[]{:S(2)}, u32[]{:S(2)}) %collective-permute-start.3) | collective-permute-done | bytes 196640 | tf_op jit(solution)/shard_map/ppermute | solution.py:22
  91.6 2.1 %fusion = f32[8,16,3072]{2,1,0:T(8,128)} fusion(bf16[8,16,3072]{2,1,0:T(8,128)(2,1)S(1)} %copy-done.2, bf16[16,16]{1,0:T(8,128)(2,1)S(1)} %copy-done, f32[8,16,24,128]{3,1,0,2:T(8,128)S(1)} %fusion.67), kind=kOutput, calls=%fused_computation.1 | convolution fusion | flops 76283904 | bytes 3932672 | tf_op jit(solution)/shard_map/ml,kmh->klh/dot_general | solution.py:99
  (10 shorter events, 0.1 us)
Async XLA Ops:
  7.2 0.7 copy-start
  7.2 8.3 %copy-start.5 = (s32[24,7]{0,1:T(8,128)S(1)}, s32[24,7]{0,1:T(8,128)}, u32[]{:S(2)}) copy-start(s32[24,7]{0,1:T(8,128)} %param.29) | copy-start | bytes 2020
  7.2 60.4 %all-reduce.3.cloned.1.call-start = ((), (), s32[]{:S(2)}) async-start(), calls=%async_computation | async-start | bytes 393216 | tf_op jit(solution)/shard_map/psum | solution.py:68
  9.4 9.0 %collective-permute-start = (bf16[8,16,384]{2,1,0:T(8,128)(2,1)S(1)}, bf16[8,16,384]{2,1,0:T(8,128)(2,1)S(1)}, u32[]{:S(2)}, u32[]{:S(2)}) collective-permute-start(bf16[8,16,384]{2,1,0:T(8,128)(2,1)S(1)} %get-tuple-element.119), channel_id=1, source_target_pairs={{0,4},{4,8},{8,12},{12,16},{16,20},{20,24},{24,28},{28,0},{1,5},{5... | collective-permute-start | bytes 294920 | tf_op jit(solution)/shard_map/ppermute | solution.py:14
  12.4 6.7 %collective-permute-start.1 = (bf16[8,16,384]{2,1,0:T(8,128)(2,1)S(1)}, bf16[8,16,384]{2,1,0:T(8,128)(2,1)S(1)}, u32[]{:S(2)}, u32[]{:S(2)}) collective-permute-start(bf16[8,16,384]{2,1,0:T(8,128)(2,1)S(1)} %get-tuple-element.120), channel_id=1, source_target_pairs={{4,0},{8,4},{12,8},{16,12},{20,16},{24,20},{28,24},{0,28},{5,1},{9... | collective-permute-start | bytes 294920 | tf_op jit(solution)/shard_map/ppermute | solution.py:15
  32.0 2.3 %copy-start.1 = (bf16[8,16,3072]{2,1,0:T(8,128)(2,1)S(1)}, bf16[8,16,3072]{2,1,0:T(8,128)(2,1)}, u32[]{:S(2)}) copy-start(bf16[8,16,3072]{2,1,0:T(8,128)(2,1)} %param.26) | copy-start | bytes 2359300
  34.3 33.2 %copy-start.3 = (f32[16,3072]{1,0:T(8,128)S(1)}, f32[16,3072]{1,0:T(8,128)}, u32[]{:S(2)}) copy-start(f32[16,3072]{1,0:T(8,128)} %param.31) | copy-start | bytes 589828
  34.4 33.2 %copy-start.4 = (f32[16,3072]{1,0:T(8,128)S(1)}, f32[16,3072]{1,0:T(8,128)}, u32[]{:S(2)}) copy-start(f32[16,3072]{1,0:T(8,128)} %param.30) | copy-start | bytes 589828
  68.6 3.7 %slice-start = ((s8[5505024]{0:T(1024)(128)(4,1)}), s8[4194304]{0:T(1024)(128)(4,1)S(1)}, s32[]{:S(2)}) async-start(s8[5505024]{0:T(1024)(128)(4,1)} %bitcast.160), calls=%async_computation.1 | async-start | bytes 8388608
  70.3 2.0 %slice-start.1 = ((s8[5505024]{0:T(1024)(128)(4,1)}), s8[1310720]{0:T(1024)(128)(4,1)S(1)}, s32[]{:S(2)}) async-start(s8[5505024]{0:T(1024)(128)(4,1)} %bitcast.160), calls=%async_computation.2 | async-start | bytes 2621440
  76.3 8.4 %collective-permute-start.2 = (f32[8,16,3,128]{3,1,0,2:T(8,128)S(1)}, f32[8,16,3,128]{3,1,0,2:T(8,128)S(1)}, u32[]{:S(2)}, u32[]{:S(2)}) collective-permute-start(f32[8,16,3,128]{3,1,0,2:T(8,128)S(1)} %slice.403), channel_id=1, source_target_pairs={{0,4},{4,8},{8,12},{12,16},{16,20},{20,24},{24,28},{28,0},{1,5},{5... | collective-permute-start | bytes 589832 | tf_op jit(solution)/shard_map/ppermute | solution.py:22
  78.0 13.6 %copy-start.2 = (bf16[8,16,3072]{2,1,0:T(8,128)(2,1)S(1)}, bf16[8,16,3072]{2,1,0:T(8,128)(2,1)}, u32[]{:S(2)}) copy-start(bf16[8,16,3072]{2,1,0:T(8,128)(2,1)} %param.25) | copy-start | bytes 2359300
  85.8 5.7 %collective-permute-start.3 = (f32[8,16,3,128]{3,1,0,2:T(8,128)S(1)}, f32[8,16,3,128]{3,1,0,2:T(8,128)S(1)}, u32[]{:S(2)}, u32[]{:S(2)}) collective-permute-start(f32[8,16,3,128]{3,1,0,2:T(8,128)S(1)} %get-tuple-element.110), channel_id=1, source_target_pairs={{0,28},{4,0},{8,4},{12,8},{16,12},{20,16},{24,20},{28,24},{1,29},{... | collective-permute-start | bytes 589832 | tf_op jit(solution)/shard_map/ppermute | solution.py:22
Sparse Core Ops, SparseCore 0:
  35.4 32.1 all-reduce.2
where the time goes:
time: 101 us
  waiting for transfers between devices  45.3 us (45%)
  matrix products  24.1 us (24%)
  between operations  14.3 us (14%)
  starting transfers between devices  9.29 us (9%)
  local copies, waits for them, and re-layouts  4.6 us (5%)
  other arithmetic  3.06 us (3%)
    psum x1, waiting for transfers between devices, on_device(): summed_total = lax.psum(partial_sum, 'mem')  32.3 us
    dot_general x7, matrix products, apply_rows(): jnp.einsum('tab,kltb->klta', blocks[:, slot_index], source, preferred_ele...  13.1 us
    ppermute x2, waiting for transfers between devices, passed_along(): lax.ppermute(value, axis, [(i, (i + by) % length) for i in range(length)])  9.32 us
    dot_general x7, matrix products, on_device(): jnp.einsum('tab,klta->kltb', blocks[:, slot_index], weighted_tiles, prefe...  7.37 us
    ppermute x2, starting transfers between devices, passed_along(): lax.ppermute(value, axis, [(i, (i + by) % length) for i in range(length)])  3.13 us
    ppermute x1, starting transfers between devices, padded_2(): after = lax.ppermute(first, axis, down)  3.1 us
    ppermute x1, starting transfers between devices, padded_2(): before = lax.ppermute(last, axis, up)  3.02 us
    ppermute x1, waiting for transfers between devices, padded_2(): before = lax.ppermute(last, axis, up)  2.82 us
  transfers between devices with their start and end apart: 5, of which 5 were waited for; matrix products, arithmetic and copies ran while one was open for 2% of the time, Pallas kernels for 0%

commit v1 on v0

v1 whole, which is shorter than its diff:
```python
import jax
import jax.numpy as jnp
from jax import lax
from jax.experimental import pallas as pl
from jax.experimental.pallas import tpu as pltpu
from jax.sharding import PartitionSpec as P


def slot_offset(slot_index):
    distance = (slot_index + 1) // 2
    return distance if slot_index % 2 == 1 else -distance


def slot_order(slot_count):
    return sorted(range(slot_count), key=slot_offset)


def spread(loc, rows):
    levels = loc.shape[0]
    pick = (
        lax.broadcasted_iota(jnp.int32, (rows, levels), 0) % levels
        == lax.broadcasted_iota(jnp.int32, (rows, levels), 1)
    ).astype(jnp.bfloat16)
    tall = jnp.dot(pick, loc, preferred_element_type=jnp.float32).astype(jnp.bfloat16)
    wide = lax.dot_general(
        tall, pick, (((1,), (1,)), ((), ())), preferred_element_type=jnp.float32
    )
    same = (
        lax.broadcasted_iota(jnp.int32, (rows, rows), 0) // levels
        == lax.broadcasted_iota(jnp.int32, (rows, rows), 1) // levels
    )
    return jnp.where(same, wide, 0.0).astype(jnp.bfloat16)


def tile_row(field_ref, blocks_ref, mask_ref, tile):
    slots, width = blocks_ref.shape[1], blocks_ref.shape[2]
    parts = []
    for slot in slot_order(slots):
        block = blocks_ref[tile, slot]
        keep = mask_ref[tile, slot].astype(jnp.float32).astype(jnp.bfloat16)
        parts.append(block * keep)
    row = jnp.concatenate(parts, axis=1)
    start = pl.multiple_of(tile * width, width)
    source = field_ref[:, pl.ds(start, slots * width)]
    return lax.dot_general(
        source, row, (((1,), (1,)), ((), ())), preferred_element_type=jnp.float32
    )


def forward_kernel(even_ref, mask_ref, loc_ref, control_ref, near_ref, far_ref, ensemble_ref,
                   blocks_ref, partial_ref, field_ref):
    members, levels, points = control_ref.shape
    rows, width = members * levels, blocks_ref.shape[2]
    rim = near_ref.shape[2]
    up = spread(loc_ref[...], rows)

    def vertical(value):
        return jnp.dot(
            up, value.reshape(rows, value.shape[2]), preferred_element_type=jnp.float32
        ).astype(jnp.bfloat16)

    even = even_ref[0]
    near_at = pl.multiple_of(even * (points + rim), width)
    far_at = pl.multiple_of((1 - even) * (points + rim), width)
    field_ref[:, pl.ds(near_at, rim)] = vertical(near_ref[...])
    field_ref[:, pl.ds(far_at, rim)] = vertical(far_ref[...])
    field_ref[:, rim : rim + points] = vertical(control_ref[...])

    def step(tile, carry):
        localized = tile_row(field_ref, blocks_ref, mask_ref, tile)
        at = pl.multiple_of(tile * width, width)
        weight = ensemble_ref[:, :, pl.ds(at, width)].astype(jnp.float32)
        total = jnp.sum(weight * localized.reshape(members, levels, width), axis=0)
        partial_ref[:, pl.ds(at, width)] = total.astype(jnp.bfloat16)
        return carry

    lax.fori_loop(0, points // width, step, 0, unroll=4)


def backward_kernel(even_ref, mask_ref, loc_ref, control_ref, depart_ref, depart_near_ref,
                    depart_far_ref, ensemble_ref, near_ref, far_ref, blocks_ref, gradient_ref,
                    field_ref):
    members, levels, points = control_ref.shape
    rows, width = members * levels, blocks_ref.shape[2]
    rim = near_ref.shape[2]
    down = spread(loc_ref[...].T, rows)

    def weighted(value, depart):
        product = value.astype(jnp.float32) * depart.astype(jnp.float32)[None]
        return product.astype(jnp.bfloat16).reshape(rows, value.shape[2])

    even = even_ref[0]
    near_at = pl.multiple_of(even * (points + rim), width)
    far_at = pl.multiple_of((1 - even) * (points + rim), width)
    field_ref[:, pl.ds(near_at, rim)] = weighted(near_ref[...], depart_near_ref[...])
    field_ref[:, pl.ds(far_at, rim)] = weighted(far_ref[...], depart_far_ref[...])
    field_ref[:, rim : rim + points] = weighted(ensemble_ref[...], depart_ref[...])

    def step(tile, carry):
        adjoint = tile_row(field_ref, blocks_ref, mask_ref, tile).astype(jnp.bfloat16)
        at = pl.multiple_of(tile * width, width)
        change = jnp.dot(down, adjoint, preferred_element_type=jnp.float32)
        gradient_ref[:, :, pl.ds(at, width)] = control_ref[:, :, pl.ds(at, width)].astype(
            jnp.float32
        ) + change.reshape(members, levels, width)
        return carry

    lax.fori_loop(0, points // width, step, 0, unroll=4)


def call(kernel, out, scratch, count, *operands):
    smem = pl.BlockSpec(memory_space=pltpu.SMEM)
    vmem = pl.BlockSpec(memory_space=pltpu.VMEM)
    return pl.pallas_call(
        kernel,
        out_shape=out,
        in_specs=[smem] * count + [vmem] * (len(operands) - count),
        out_specs=vmem,
        scratch_shapes=[scratch],
        compiler_params=pltpu.CompilerParams(vmem_limit_bytes=16 * 2**20),
    )(*operands)


def on_device(control, ensemble, vertical_loc, blocks, edge_mask, background, obs_precision):
    members, levels, points = control.shape
    tiles, slots, width, _ = blocks.shape
    rim = (slots - 1) // 2 * width
    ring, group = lax.axis_size("tile"), lax.axis_size("mem")
    even = 1 - lax.axis_index("tile") % 2
    even_ref = jnp.full((1,), even, jnp.int32)
    near = [(i, i ^ 1) for i in range(ring)]
    far = [(i, (i + 1 if i % 2 else i - 1) % ring) for i in range(ring)]

    def rims(value):
        axis = value.ndim - 1
        last = value.shape[axis] - rim
        to_near = lax.dynamic_slice_in_dim(value, even * last, rim, axis)
        to_far = lax.dynamic_slice_in_dim(value, (1 - even) * last, rim, axis)
        return lax.ppermute(to_near, "tile", near), lax.ppermute(to_far, "tile", far)

    control_near, control_far = rims(control)
    ensemble_near, ensemble_far = rims(ensemble)
    field = pltpu.VMEM((members * levels, points + 2 * rim), jnp.bfloat16)
    partial_sum = call(
        forward_kernel, jax.ShapeDtypeStruct((levels, points), jnp.bfloat16), field, 2,
        even_ref, edge_mask, vertical_loc, control, control_near, control_far, ensemble, blocks,
    )
    step = 1
    total = partial_sum
    while step < group:
        other = lax.ppermute(total, "mem", [(i, i ^ step) for i in range(group)])
        total = total.astype(jnp.float32) + other.astype(jnp.float32)
        step *= 2
        if step < group:
            total = total.astype(jnp.bfloat16)
    rows = levels // group
    increment = lax.dynamic_slice_in_dim(total, lax.axis_index("mem") * rows, rows, 0)
    depart = (obs_precision * (total - background)).astype(jnp.bfloat16)
    depart_near, depart_far = rims(depart)
    gradient = call(
        backward_kernel, jax.ShapeDtypeStruct((members, levels, points), jnp.float32), field, 2,
        even_ref, edge_mask, vertical_loc, control, depart, depart_near, depart_far, ensemble,
        ensemble_near, ensemble_far, blocks,
    )
    return increment, gradient


def solution(mesh):
    in_specs = (
        P("mem", None, "tile"),
        P("mem", None, "tile"),
        P(),
        P("tile", None, None, None),
        P("tile", None),
        P(None, "tile"),
        P(None, "tile"),
    )
    out_specs = (P("mem", "tile"), P("mem", None, "tile"))
    return jax.shard_map(
        on_device, mesh=mesh, in_specs=in_specs, out_specs=out_specs, check_vma=False
    )
```

time: 101 us -> 47.6 us (0.47)
  waiting for transfers between devices: 45.3 us -> 9.63 us
  matrix products: 24.1 us -> 0 us
  Pallas kernels: 0 us -> 13.6 us
  between operations: 14.3 us -> 0.75 us
  local copies, waits for them, and re-layouts: 4.6 us -> 10.6 us
  starting transfers between devices: 9.29 us -> 12.7 us
  other arithmetic: 3.06 us -> 0.07 us
    psum x1 -> x0, waiting for transfers between devices: 32.3 us -> none  [on_device(): summed_total = lax.psum(partial_sum, 'mem')]
    dot_general x16 -> x0, matrix products: 24.1 us -> none  [the longest x7 13.1 us: apply_rows(): jnp.einsum('tab,kltb->klta', blocks[:, slot_index], source, preferred_ele...]
    pallas_call x0 -> x2, Pallas kernels: none -> 13.6 us  [call(): pl.pallas_call(kernel, out_shape=out, in_specs=[smem] * count + [vmem] *...]
    unnamed x16 -> x21, local copies, waits for them, and re-layouts: 0.67 us -> 8.86 us
    ppermute x4 -> x8, starting transfers between devices: 9.25 us -> 12.7 us  [the longest x3 11 us: rims(): lax.ppermute(to_far, 'tile', far)]
    ppermute x4 -> x8, waiting for transfers between devices: 12.9 us -> 9.63 us  [the longest x3 3.74 us: rims(): lax.ppermute(to_near, 'tile', near)]
    slice x4 -> x0, local copies, waits for them, and re-layouts: 1.6 us -> none  [the longest x1 1.42 us: apply_rows(): padded_tiles[:, :, reach_tiles + offset:reach_tiles + offset + tile_count]]
    slice x1 -> x0, other arithmetic: 1.08 us -> none  [on_device(): left_rim = extended[:, :, :reach_tiles]]
  transfers between devices with their start and end apart: 5 -> 8, of which waited for: 5 -> 7; matrix products, arithmetic and copies ran while one was open for 2% -> 3% of each run, Pallas kernels for 0% -> 0%
where the time goes in v1:
time: 47.6 us; the launch traced here: 47.3 us
  Pallas kernels  13.6 us (29%)
  starting transfers between devices  12.7 us (27%)
  local copies, waits for them, and re-layouts  10.6 us (22%)
  waiting for transfers between devices  9.63 us (20%)
  between operations  0.75 us (2%)
    pallas_call x2, Pallas kernels, call(): pl.pallas_call(kernel, out_shape=out, in_specs=[smem] * count + [vmem] *...  13.6 us
    ppermute x3, starting transfers between devices, rims(): lax.ppermute(to_far, 'tile', far)  11 us
    unnamed x21, local copies, waits for them, and re-layouts  8.86 us
    ppermute x3, waiting for transfers between devices, rims(): lax.ppermute(to_near, 'tile', near)  3.74 us
    ppermute x3, waiting for transfers between devices, rims(): lax.ppermute(to_far, 'tile', far)  3.74 us
    ppermute x2, waiting for transfers between devices, on_device(): other = lax.ppermute(total, 'mem', [(i, i ^ step) for i in range(group)])  2.15 us
    ppermute x2, starting transfers between devices, on_device(): other = lax.ppermute(total, 'mem', [(i, i ^ step) for i in range(group)])  1.62 us
    dynamic_slice x3, local copies, waits for them, and re-layouts, rims(): to_far = lax.dynamic_slice_in_dim(value, (1 - even) * last, rim, axis)  1.08 us
  transfers between devices with their start and end apart: 8, of which 7 were waited for; matrix products, arithmetic and copies ran while one was open for 3% of the time, Pallas kernels for 0%

profile of v1, /device:TPU:0, one launch (start us, length us, event | category | flops | bytes accessed | tf_op | source)
XLA Modules:
  0.0 47.3 jit_solution(12375234876536610885)
XLA Ops:
  0.6 0.0 copy-start.7
  0.6 0.0 copy-start.8
  0.7 0.0 copy-start.9
  0.7 1.0 %constant_dynamic-slice_fusion.5 = (bf16[8,16,384]{2,1,0:T(8,128)(2,1)S(1)}, bf16[8,16,384]{2,1,0:T(8,128)(2,1)S(1)}) fusion(bf16[8,16,3072]{2,1,0:T(8,128)(2,1)} %control_ref.3, s32[]{:T(128)S(6)} %select_n.22, s32[]{:T(128)S(6)} %select_n.21), kind=kLoop, calls=%fused_computation.8 | loop fusion | bytes 393224 | tf_op jit(solution)/shard_map/dynamic_slice | solution.py:138
  1.7 6.1 %collective-permute-start.1 = (bf16[8,16,384]{2,1,0:T(8,128)(2,1)S(1)}, bf16[8,16,384]{2,1,0:T(8,128)(2,1)S(1)}, u32[]{:S(2)}, u32[]{:S(2)}) collective-permute-start(bf16[8,16,384]{2,1,0:T(8,128)(2,1)S(1)} %get-tuple-element.4), channel_id=1, source_target_pairs={{0,28},{4,8},{8,4},{12,16},{16,12},{20,24},{24,20},{28,0},{1,29},{... | collective-permute-start | bytes 294920 | tf_op jit(solution)/shard_map/ppermute | solution.py:139
  7.8 0.0 collective-permute-start
  7.8 0.8 %copy.9.mask_ref = s32[24,7]{1,0:T(8,128)S(1)} copy(s32[24,7]{0,1:T(8,128)} %param.11) | data formatting | bytes 1344 | tf_op args[4]
  8.6 2.1 %collective-permute-done.1.far_ref = bf16[8,16,384]{2,1,0:T(8,128)(2,1)S(1)} collective-permute-done((bf16[8,16,384]{2,1,0:T(8,128)(2,1)S(1)}, bf16[8,16,384]{2,1,0:T(8,128)(2,1)S(1)}, u32[]{:S(2)}, u32[]{:S(2)}) %collective-permute-start.1) | collective-permute-done | bytes 98336 | tf_op jit(solution)/shard_map/ppermute | solution.py:139
  10.7 2.0 %collective-permute-done.near_ref = bf16[8,16,384]{2,1,0:T(8,128)(2,1)S(1)} collective-permute-done((bf16[8,16,384]{2,1,0:T(8,128)(2,1)S(1)}, bf16[8,16,384]{2,1,0:T(8,128)(2,1)S(1)}, u32[]{:S(2)}, u32[]{:S(2)}) %collective-permute-start) | collective-permute-done | bytes 98336 | tf_op jit(solution)/shard_map/ppermute | solution.py:139
  12.7 0.0 copy-start
  12.7 2.6 %copy-done = bf16[24,7,128,128]{3,2,1,0:T(8,128)(2,1)S(1)} copy-done((bf16[24,7,128,128]{3,2,1,0:T(8,128)(2,1)S(1)}, bf16[24,7,128,128]{3,2,1,0:T(8,128)(2,1)}, u32[]{:S(2)}) %copy-start) | copy-done | bytes 5505048
  15.3 0.0 copy-start.2
  15.3 1.1 %copy-done.2 = bf16[8,16,3072]{2,1,0:T(8,128)(2,1)S(1)} copy-done((bf16[8,16,3072]{2,1,0:T(8,128)(2,1)S(1)}, bf16[8,16,3072]{2,1,0:T(8,128)(2,1)}, u32[]{:S(2)}) %copy-start.2) | copy-done | bytes 786456
  16.4 0.0 copy-start.4
  16.4 1.1 %copy-done.4 = bf16[8,16,3072]{2,1,0:T(8,128)(2,1)S(1)} copy-done((bf16[8,16,3072]{2,1,0:T(8,128)(2,1)S(1)}, bf16[8,16,3072]{2,1,0:T(8,128)(2,1)}, u32[]{:S(2)}) %copy-start.4) | copy-done | bytes 786456
  17.5 0.0 copy-start.6
  17.5 0.7 %copy-done.6 = bf16[16,16]{1,0:T(8,128)(2,1)S(1)} copy-done((bf16[16,16]{1,0:T(8,128)(2,1)S(1)}, bf16[16,16]{1,0:T(8,128)(2,1)}, u32[]{:S(2)}) %copy-start.6) | copy-done | bytes 536
  18.2 0.0 copy-start.3
  18.2 0.0 copy-start.5
  18.2 4.2 %shard_map.86 = bf16[16,3072]{1,0:T(8,128)(2,1)S(1)} custom-call(s32[1]{0:T(128)} %bitcast.even_ref, s32[24,7]{1,0:T(8,128)S(1)} %copy.9.mask_ref, bf16[16,16]{1,0:T(8,128)(2,1)S(1)} %copy-done.6, bf16[8,16,3072]{2,1,0:T(8,128)(2,1)S(1)} %copy-done.2, bf16[8,16,384]{2,1,0:T(8,128)(2,1)S(1)} %collective-permute-done.near_ref, ...), custom_call_target="tpu_custom_call" | custom-call | tf_op jit(solution)/shard_map/pallas_call | solution.py:114
  22.4 0.1 collective-permute-start.2
  22.5 1.3 %collective-permute-done.2 = bf16[16,3072]{1,0:T(8,128)(2,1)S(1)} collective-permute-done((bf16[16,3072]{1,0:T(8,128)(2,1)S(1)}, bf16[16,3072]{1,0:T(8,128)(2,1)S(1)}, u32[]{:S(2)}, u32[]{:S(2)}) %collective-permute-start.2) | collective-permute-done | bytes 98336 | tf_op jit(solution)/shard_map/ppermute | solution.py:151
  23.8 1.6 %collective-permute-start.3 = (bf16[16,3072]{1,0:T(8,128)(2,1)S(1)}, bf16[16,3072]{1,0:T(8,128)(2,1)S(1)}, u32[]{:S(2)}, u32[]{:S(2)}) collective-permute-start(bf16[16,3072]{1,0:T(8,128)(2,1)S(1)} %add_convert_fusion), channel_id=1, source_target_pairs={{0,2},{1,3},{2,0},{3,1},{4,6},{5,7},{6,4},{7,5},{8,10},{9,11},{10,... | collective-permute-start | bytes 294920 | tf_op jit(solution)/shard_map/ppermute | solution.py:151
  25.4 2.5 %collective-permute-start.7 = (bf16[8,16,384]{2,1,0:T(8,128)(2,1)S(1)}, bf16[8,16,384]{2,1,0:T(8,128)(2,1)S(1)}, u32[]{:S(2)}, u32[]{:S(2)}) collective-permute-start(bf16[8,16,384]{2,1,0:T(8,128)(2,1)S(1)} %get-tuple-element.2), channel_id=1, source_target_pairs={{0,28},{4,8},{8,4},{12,16},{16,12},{20,24},{24,20},{28,0},{1,29},{... | collective-permute-start | bytes 294920 | tf_op jit(solution)/shard_map/ppermute | solution.py:139
  27.9 0.0 collective-permute-start.6
  27.9 0.9 %collective-permute-done.3 = bf16[16,3072]{1,0:T(8,128)(2,1)S(1)} collective-permute-done((bf16[16,3072]{1,0:T(8,128)(2,1)S(1)}, bf16[16,3072]{1,0:T(8,128)(2,1)S(1)}, u32[]{:S(2)}, u32[]{:S(2)}) %collective-permute-start.3) | collective-permute-done | bytes 98336 | tf_op jit(solution)/shard_map/ppermute | solution.py:151
  28.7 0.0 copy-done.8
  28.7 0.0 copy-done.9
  28.8 2.5 %collective-permute-start.5 = (bf16[16,384]{1,0:T(8,128)(2,1)S(1)}, bf16[16,384]{1,0:T(8,128)(2,1)S(1)}, u32[]{:S(2)}, u32[]{:S(2)}) collective-permute-start(bf16[16,384]{1,0:T(8,128)(2,1)S(1)} %get-tuple-element.8), channel_id=1, source_target_pairs={{0,28},{4,8},{8,4},{12,16},{16,12},{20,24},{24,20},{28,0},{1,29},{... | collective-permute-start | bytes 36872 | tf_op jit(solution)/shard_map/ppermute | solution.py:139
  31.3 0.0 collective-permute-start.4
  31.3 0.6 %constant_dynamic-slice_fusion.4 = f32[4,3072]{1,0:T(4,128)} fusion(f32[16,3072]{1,0:T(8,128)S(1)} %get-tuple-element.7, s32[]{:T(128)S(6)} %select_n.23), kind=kLoop, calls=%fused_computation.7 | loop fusion | bytes 98308 | tf_op jit(solution)/shard_map/dynamic_slice | solution.py:157
  31.9 0.9 %collective-permute-done.7.far_ref = bf16[8,16,384]{2,1,0:T(8,128)(2,1)S(1)} collective-permute-done((bf16[8,16,384]{2,1,0:T(8,128)(2,1)S(1)}, bf16[8,16,384]{2,1,0:T(8,128)(2,1)S(1)}, u32[]{:S(2)}, u32[]{:S(2)}) %collective-permute-start.7) | collective-permute-done | bytes 98336 | tf_op jit(solution)/shard_map/ppermute | solution.py:139
  32.8 1.7 %collective-permute-done.6.near_ref = bf16[8,16,384]{2,1,0:T(8,128)(2,1)S(1)} collective-permute-done((bf16[8,16,384]{2,1,0:T(8,128)(2,1)S(1)}, bf16[8,16,384]{2,1,0:T(8,128)(2,1)S(1)}, u32[]{:S(2)}, u32[]{:S(2)}) %collective-permute-start.6) | collective-permute-done | bytes 98336 | tf_op jit(solution)/shard_map/ppermute | solution.py:139
  34.5 0.7 %collective-permute-done.5.depart_far_ref = bf16[16,384]{1,0:T(8,128)(2,1)S(1)} collective-permute-done((bf16[16,384]{1,0:T(8,128)(2,1)S(1)}, bf16[16,384]{1,0:T(8,128)(2,1)S(1)}, u32[]{:S(2)}, u32[]{:S(2)}) %collective-permute-start.5) | collective-permute-done | bytes 12320 | tf_op jit(solution)/shard_map/ppermute | solution.py:139
  35.3 0.0 collective-permute-done.4.depart_near_ref
  35.3 0.0 copy-done.7
  35.3 0.0 copy-done.3
  35.3 0.0 copy-done.5
  35.3 0.0 copy-start.1
  35.3 2.6 %copy-done.1 = bf16[24,7,128,128]{3,2,1,0:T(8,128)(2,1)S(1)} copy-done((bf16[24,7,128,128]{3,2,1,0:T(8,128)(2,1)S(1)}, bf16[24,7,128,128]{3,2,1,0:T(8,128)(2,1)}, u32[]{:S(2)}) %copy-start.1) | copy-done | bytes 5505048
  37.8 9.4 %shard_map.87 = f32[8,16,3072]{2,1,0:T(8,128)} custom-call(s32[1]{0:T(128)} %bitcast.even_ref, s32[24,7]{1,0:T(8,128)S(1)} %copy.9.mask_ref, bf16[16,16]{1,0:T(8,128)(2,1)S(1)} %copy-done.7, bf16[8,16,3072]{2,1,0:T(8,128)(2,1)S(1)} %copy-done.3, bf16[16,3072]{1,0:T(8,128)(2,1)S(1)} %get-tuple-element.6.depart_ref, ...), custom_call_target="tpu_custom_call" | custom-call | tf_op jit(solution)/shard_map/pallas_call | solution.py:114
  (4 shorter events, 0.1 us)
Async XLA Ops:
  0.6 34.6 %copy-start.7 = (bf16[16,16]{1,0:T(8,128)(2,1)S(1)}, bf16[16,16]{1,0:T(8,128)(2,1)}, u32[]{:S(2)}) copy-start(bf16[16,16]{1,0:T(8,128)(2,1)} %loc_ref.3) | copy-start | bytes 1540
  0.6 28.1 %copy-start.8 = (f32[16,3072]{1,0:T(8,128)S(1)}, f32[16,3072]{1,0:T(8,128)}, u32[]{:S(2)}) copy-start(f32[16,3072]{1,0:T(8,128)} %param.13) | copy-start | bytes 589828
  0.7 28.1 %copy-start.9 = (f32[16,3072]{1,0:T(8,128)S(1)}, f32[16,3072]{1,0:T(8,128)}, u32[]{:S(2)}) copy-start(f32[16,3072]{1,0:T(8,128)} %param.12) | copy-start | bytes 589828
  1.7 8.9 %collective-permute-start.1 = (bf16[8,16,384]{2,1,0:T(8,128)(2,1)S(1)}, bf16[8,16,384]{2,1,0:T(8,128)(2,1)S(1)}, u32[]{:S(2)}, u32[]{:S(2)}) collective-permute-start(bf16[8,16,384]{2,1,0:T(8,128)(2,1)S(1)} %get-tuple-element.4), channel_id=1, source_target_pairs={{0,28},{4,8},{8,4},{12,16},{16,12},{20,24},{24,20},{28,0},{1,29},{... | collective-permute-start | bytes 294920 | tf_op jit(solution)/shard_map/ppermute | solution.py:139
  7.8 4.9 %collective-permute-start = (bf16[8,16,384]{2,1,0:T(8,128)(2,1)S(1)}, bf16[8,16,384]{2,1,0:T(8,128)(2,1)S(1)}, u32[]{:S(2)}, u32[]{:S(2)}) collective-permute-start(bf16[8,16,384]{2,1,0:T(8,128)(2,1)S(1)} %get-tuple-element.5), channel_id=1, source_target_pairs={{0,4},{4,0},{8,12},{12,8},{16,20},{20,16},{24,28},{28,24},{1,5},{5... | collective-permute-start | bytes 294920 | tf_op jit(solution)/shard_map/ppermute | solution.py:139
  12.7 2.6 %copy-start = (bf16[24,7,128,128]{3,2,1,0:T(8,128)(2,1)S(1)}, bf16[24,7,128,128]{3,2,1,0:T(8,128)(2,1)}, u32[]{:S(2)}) copy-start(bf16[24,7,128,128]{3,2,1,0:T(8,128)(2,1)} %blocks_ref.3) | copy-start | bytes 16515076
  15.3 1.1 %copy-start.2 = (bf16[8,16,3072]{2,1,0:T(8,128)(2,1)S(1)}, bf16[8,16,3072]{2,1,0:T(8,128)(2,1)}, u32[]{:S(2)}) copy-start(bf16[8,16,3072]{2,1,0:T(8,128)(2,1)} %control_ref.3) | copy-start | bytes 2359300
  16.4 1.1 %copy-start.4 = (bf16[8,16,3072]{2,1,0:T(8,128)(2,1)S(1)}, bf16[8,16,3072]{2,1,0:T(8,128)(2,1)}, u32[]{:S(2)}) copy-start(bf16[8,16,3072]{2,1,0:T(8,128)(2,1)} %ensemble_ref.3) | copy-start | bytes 2359300
  17.5 0.7 %copy-start.6 = (bf16[16,16]{1,0:T(8,128)(2,1)S(1)}, bf16[16,16]{1,0:T(8,128)(2,1)}, u32[]{:S(2)}) copy-start(bf16[16,16]{1,0:T(8,128)(2,1)} %loc_ref.3) | copy-start | bytes 1540
  18.2 17.0 %copy-start.3 = (bf16[8,16,3072]{2,1,0:T(8,128)(2,1)S(1)}, bf16[8,16,3072]{2,1,0:T(8,128)(2,1)}, u32[]{:S(2)}) copy-start(bf16[8,16,3072]{2,1,0:T(8,128)(2,1)} %control_ref.3) | copy-start | bytes 2359300
  18.2 17.0 %copy-start.5 = (bf16[8,16,3072]{2,1,0:T(8,128)(2,1)S(1)}, bf16[8,16,3072]{2,1,0:T(8,128)(2,1)}, u32[]{:S(2)}) copy-start(bf16[8,16,3072]{2,1,0:T(8,128)(2,1)} %ensemble_ref.3) | copy-start | bytes 2359300
  22.4 1.4 %collective-permute-start.2 = (bf16[16,3072]{1,0:T(8,128)(2,1)S(1)}, bf16[16,3072]{1,0:T(8,128)(2,1)S(1)}, u32[]{:S(2)}, u32[]{:S(2)}) collective-permute-start(bf16[16,3072]{1,0:T(8,128)(2,1)S(1)} %shard_map.86), channel_id=1, source_target_pairs={{0,1},{1,0},{2,3},{3,2},{4,5},{5,4},{6,7},{7,6},{8,9},{9,8},{10,11... | collective-permute-start | bytes 294920 | tf_op jit(solution)/shard_map/ppermute | solution.py:151
  23.8 4.9 %collective-permute-start.3 = (bf16[16,3072]{1,0:T(8,128)(2,1)S(1)}, bf16[16,3072]{1,0:T(8,128)(2,1)S(1)}, u32[]{:S(2)}, u32[]{:S(2)}) collective-permute-start(bf16[16,3072]{1,0:T(8,128)(2,1)S(1)} %add_convert_fusion), channel_id=1, source_target_pairs={{0,2},{1,3},{2,0},{3,1},{4,6},{5,7},{6,4},{7,5},{8,10},{9,11},{10,... | collective-permute-start | bytes 294920 | tf_op jit(solution)/shard_map/ppermute | solution.py:151
  25.4 7.4 %collective-permute-start.7 = (bf16[8,16,384]{2,1,0:T(8,128)(2,1)S(1)}, bf16[8,16,384]{2,1,0:T(8,128)(2,1)S(1)}, u32[]{:S(2)}, u32[]{:S(2)}) collective-permute-start(bf16[8,16,384]{2,1,0:T(8,128)(2,1)S(1)} %get-tuple-element.2), channel_id=1, source_target_pairs={{0,28},{4,8},{8,4},{12,16},{16,12},{20,24},{24,20},{28,0},{1,29},{... | collective-permute-start | bytes 294920 | tf_op jit(solution)/shard_map/ppermute | solution.py:139
  27.9 6.7 %collective-permute-start.6 = (bf16[8,16,384]{2,1,0:T(8,128)(2,1)S(1)}, bf16[8,16,384]{2,1,0:T(8,128)(2,1)S(1)}, u32[]{:S(2)}, u32[]{:S(2)}) collective-permute-start(bf16[8,16,384]{2,1,0:T(8,128)(2,1)S(1)} %get-tuple-element.3), channel_id=1, source_target_pairs={{0,4},{4,0},{8,12},{12,8},{16,20},{20,16},{24,28},{28,24},{1,5},{5... | collective-permute-start | bytes 294920 | tf_op jit(solution)/shard_map/ppermute | solution.py:139
  28.8 6.5 %collective-permute-start.5 = (bf16[16,384]{1,0:T(8,128)(2,1)S(1)}, bf16[16,384]{1,0:T(8,128)(2,1)S(1)}, u32[]{:S(2)}, u32[]{:S(2)}) collective-permute-start(bf16[16,384]{1,0:T(8,128)(2,1)S(1)} %get-tuple-element.8), channel_id=1, source_target_pairs={{0,28},{4,8},{8,4},{12,16},{16,12},{20,24},{24,20},{28,0},{1,29},{... | collective-permute-start | bytes 36872 | tf_op jit(solution)/shard_map/ppermute | solution.py:139
  31.3 4.0 %collective-permute-start.4 = (bf16[16,384]{1,0:T(8,128)(2,1)S(1)}, bf16[16,384]{1,0:T(8,128)(2,1)S(1)}, u32[]{:S(2)}, u32[]{:S(2)}) collective-permute-start(bf16[16,384]{1,0:T(8,128)(2,1)S(1)} %get-tuple-element.9), channel_id=1, source_target_pairs={{0,4},{4,0},{8,12},{12,8},{16,20},{20,16},{24,28},{28,24},{1,5},{5... | collective-permute-start | bytes 36872 | tf_op jit(solution)/shard_map/ppermute | solution.py:139
  35.3 2.6 %copy-start.1 = (bf16[24,7,128,128]{3,2,1,0:T(8,128)(2,1)S(1)}, bf16[24,7,128,128]{3,2,1,0:T(8,128)(2,1)}, u32[]{:S(2)}) copy-start(bf16[24,7,128,128]{3,2,1,0:T(8,128)(2,1)} %blocks_ref.3) | copy-start | bytes 16515076

commit v2 on v1

v2 whole, which is shorter than its diff:
```python
import jax
import jax.numpy as jnp
from jax import lax
from jax.experimental import pallas as pl
from jax.experimental.pallas import tpu as pltpu
from jax.sharding import PartitionSpec as P

CHUNK = 4


def slot_of(offset):
    return 2 * offset - 1 if offset > 0 else -2 * offset


def spread(loc, rows):
    levels = loc.shape[0]
    pick = (
        lax.broadcasted_iota(jnp.int32, (rows, levels), 0) % levels
        == lax.broadcasted_iota(jnp.int32, (rows, levels), 1)
    ).astype(jnp.bfloat16)
    tall = jnp.concatenate([loc] * (rows // levels), axis=0)
    wide = lax.dot_general(
        tall, pick, (((1,), (1,)), ((), ())), preferred_element_type=jnp.float32
    )
    same = (
        lax.broadcasted_iota(jnp.int32, (rows, rows), 0) // levels
        == lax.broadcasted_iota(jnp.int32, (rows, rows), 1) // levels
    )
    return jnp.where(same, wide, 0.0).astype(jnp.bfloat16)


def pair_rows(source, blocks_ref, pair):
    tiles, slots, width, _ = blocks_ref.shape
    reach = (slots - 1) // 2
    empty = jnp.zeros((width, width), jnp.bfloat16)
    lines = []
    for tile in range(2 * pair - reach, 2 * pair + reach + 2):
        line = []
        for row in (2 * pair, 2 * pair + 1):
            if abs(row - tile) > reach:
                line.append(empty)
            elif 0 <= tile < tiles:
                line.append(blocks_ref[tile, slot_of(row - tile)])
            else:
                line.append(blocks_ref[row, slot_of(tile - row)].T)
        lines.append(jnp.concatenate(line, axis=1))
    return jnp.dot(source, jnp.concatenate(lines, axis=0), preferred_element_type=jnp.float32)


def interior_pairs(tiles, reach):
    first = (reach + 1) // 2
    return range(first, tiles // 2 - first)


def edge_pairs(tiles, reach):
    first = (reach + 1) // 2
    return [*range(first), *range(tiles // 2 - first, tiles // 2)]


def edge_source(field_ref, rims_ref, pair, width, reach, tiles):
    low, high = 2 * pair - reach, 2 * pair + reach + 2
    rim = reach * width
    parts = []
    if low < 0:
        parts.append(rims_ref[:, rim + low * width : rim])
    parts.append(field_ref[:, max(low, 0) * width : min(high, tiles) * width])
    if high > tiles:
        parts.append(rims_ref[:, rim : rim + (high - tiles) * width])
    return jnp.concatenate(parts, axis=1)


def place_rims(rims_ref, even, near, far):
    rim = near.shape[1]
    rims_ref[:, pl.ds(pl.multiple_of(even * rim, rim), rim)] = near
    rims_ref[:, pl.ds(pl.multiple_of((1 - even) * rim, rim), rim)] = far


def contribution(ensemble_ref, rows, columns):
    members, levels, _ = ensemble_ref.shape
    weight = ensemble_ref[:, :, columns].astype(jnp.float32)
    return jnp.sum(weight * rows.reshape(members, levels, rows.shape[1]), axis=0).astype(
        jnp.bfloat16
    )


def take_rims(where_ref, control_hbm, ensemble_hbm, *refs):
    outs, sems = refs[:4], refs[4]
    rim = outs[0].shape[2]
    last = control_hbm.shape[2] - rim
    even = where_ref[0]
    starts = [pl.multiple_of(even * last, 128), pl.multiple_of((1 - even) * last, 128)] * 2
    copies = [
        pltpu.make_async_copy(source.at[:, :, pl.ds(start, rim)], out, sems.at[i])
        for i, (source, start, out) in enumerate(
            zip([control_hbm] * 2 + [ensemble_hbm] * 2, starts, outs)
        )
    ]
    for copy in copies:
        copy.start()
    for copy in copies:
        copy.wait()


def take_depart(where_ref, mine_ref, other_ref, background_ref, precision_ref, depart_ref,
                near_ref, far_ref, increment_ref):
    total = mine_ref[...].astype(jnp.float32) + other_ref[...].astype(jnp.float32)
    depart_ref[...] = (precision_ref[...] * (total - background_ref[...])).astype(jnp.bfloat16)
    even, place = where_ref[0], where_ref[1]
    rim = near_ref.shape[1]
    last = depart_ref.shape[1] - rim
    near_ref[...] = depart_ref[:, pl.ds(pl.multiple_of(even * last, 128), rim)]
    far_ref[...] = depart_ref[:, pl.ds(pl.multiple_of((1 - even) * last, 128), rim)]
    per = increment_ref.shape[0]
    rows = total[:per]
    for at in range(per, total.shape[0], per):
        rows = jnp.where(place == at // per, total[at : at + per], rows)
    increment_ref[...] = rows


def forward_interior(loc_ref, mask_hbm, control_hbm, ensemble_hbm, blocks_hbm, partial_ref,
                     field_ref, control_ref, ensemble_ref, blocks_ref, mask_ref, few_sems,
                     block_sems):
    members, levels, points = control_ref.shape
    tiles, slots, width, _ = blocks_ref.shape
    rows, reach = members * levels, (slots - 1) // 2
    chunks = [pl.ds(at, min(CHUNK, tiles - at)) for at in range(0, tiles, CHUNK)]
    block_copies = [
        pltpu.make_async_copy(blocks_hbm.at[at], blocks_ref.at[at], block_sems.at[i])
        for i, at in enumerate(chunks)
    ]
    control_copy = pltpu.make_async_copy(control_hbm, control_ref, few_sems.at[0])
    mask_copy = pltpu.make_async_copy(mask_hbm, mask_ref, few_sems.at[1])
    ensemble_copy = pltpu.make_async_copy(ensemble_hbm, ensemble_ref, few_sems.at[2])
    mask_copy.start()
    control_copy.start()
    block_copies[0].start()
    ensemble_copy.start()
    for copy in block_copies[1:]:
        copy.start()
    up = spread(loc_ref[...], rows)
    control_copy.wait()
    field_ref[...] = jnp.dot(
        up, control_ref[...].reshape(rows, points), preferred_element_type=jnp.float32
    ).astype(jnp.bfloat16)
    mask_copy.wait()
    ready = 0

    def take(until, ready):
        while ready < until:
            block_copies[ready].wait()
            at = chunks[ready].start
            for tile in range(at, at + chunks[ready].size):
                for slot in range(slots):
                    keep = mask_ref[slot, tile].astype(jnp.float32).astype(jnp.bfloat16)
                    blocks_ref[tile, slot] = blocks_ref[tile, slot] * keep
            ready += 1
        return ready

    for pair in interior_pairs(tiles, reach):
        high = 2 * pair + reach + 2
        ready = take(pl.cdiv(high, CHUNK), ready)
        if pair == interior_pairs(tiles, reach)[0]:
            ensemble_copy.wait()
        source = field_ref[:, (2 * pair - reach) * width : high * width]
        columns = slice(2 * pair * width, (2 * pair + 2) * width)
        partial_ref[:, columns] = contribution(
            ensemble_ref, pair_rows(source, blocks_ref, pair), columns
        )
    take(len(chunks), ready)


def forward_edge(where_ref, loc_ref, near_ref, far_ref, field_ref, ensemble_ref, blocks_ref,
                 interior_ref, partial_ref, rims_ref):
    members, levels, points = ensemble_ref.shape
    tiles, slots, width, _ = blocks_ref.shape
    rows, reach = members * levels, (slots - 1) // 2
    up = spread(loc_ref[...], rows)

    def vertical(ref):
        value = ref[...].reshape(rows, ref.shape[2])
        return jnp.dot(up, value, preferred_element_type=jnp.float32).astype(jnp.bfloat16)

    place_rims(rims_ref, where_ref[0], vertical(near_ref), vertical(far_ref))
    edges = edge_pairs(tiles, reach)
    inner = interior_pairs(tiles, reach)
    columns = slice(2 * inner[0] * width, 2 * (inner[-1] + 1) * width)
    partial_ref[:, columns] = interior_ref[:, columns]
    for pair in edges:
        source = edge_source(field_ref, rims_ref, pair, width, reach, tiles)
        columns = slice(2 * pair * width, (2 * pair + 2) * width)
        partial_ref[:, columns] = contribution(
            ensemble_ref, pair_rows(source, blocks_ref, pair), columns
        )


def weighted(value, depart):
    members, levels, points = value.shape
    product = value.astype(jnp.float32) * depart.astype(jnp.float32)[None]
    return product.astype(jnp.bfloat16).reshape(members * levels, points)


def write_rows(pairs, sources, control_ref, blocks_ref, gradient_hbm, stage_ref, sems):
    members, levels, _ = control_ref.shape
    width = blocks_ref.shape[2]
    copies = []
    for i, pair in enumerate(pairs):
        change = pair_rows(sources(pair), blocks_ref, pair)
        columns = pl.ds(2 * pair * width, 2 * width)
        staged = stage_ref.at[:, :, pl.ds(2 * i * width, 2 * width)]
        staged[...] = control_ref[:, :, columns].astype(jnp.float32) + change.reshape(
            members, levels, 2 * width
        )
        copy = pltpu.make_async_copy(staged, gradient_hbm.at[:, :, columns], sems.at[i])
        copy.start()
        copies.append(copy)
    for copy in copies:
        copy.wait()


def backward_interior(loc_ref, depart_ref, ensemble_ref, control_ref, blocks_ref, gradient_hbm,
                      field_ref, stage_ref, sems):
    members, levels, points = control_ref.shape
    tiles, slots, width, _ = blocks_ref.shape
    reach = (slots - 1) // 2
    down = spread(loc_ref[...].T, members * levels)
    field_ref[...] = jnp.dot(
        down, weighted(ensemble_ref[...], depart_ref[...]), preferred_element_type=jnp.float32
    ).astype(jnp.bfloat16)
    write_rows(
        interior_pairs(tiles, reach),
        lambda pair: field_ref[:, (2 * pair - reach) * width : (2 * pair + reach + 2) * width],
        control_ref, blocks_ref, gradient_hbm, stage_ref, sems,
    )


def backward_edge(where_ref, loc_ref, depart_near_ref, depart_far_ref, near_ref, far_ref,
                  field_ref, control_ref, blocks_ref, begun_hbm, gradient_hbm, rims_ref,
                  stage_ref, sems):
    members, levels, points = control_ref.shape
    tiles, slots, width, _ = blocks_ref.shape
    reach = (slots - 1) // 2
    down = spread(loc_ref[...].T, members * levels)

    def lowered(value_ref, depart_ref):
        return jnp.dot(
            down, weighted(value_ref[...], depart_ref[...]), preferred_element_type=jnp.float32
        ).astype(jnp.bfloat16)

    place_rims(
        rims_ref, where_ref[0], lowered(near_ref, depart_near_ref),
        lowered(far_ref, depart_far_ref),
    )
    write_rows(
        edge_pairs(tiles, reach),
        lambda pair: edge_source(field_ref, rims_ref, pair, width, reach, tiles),
        control_ref, blocks_ref, gradient_hbm, stage_ref, sems,
    )


SMEM = pl.BlockSpec(memory_space=pltpu.SMEM)
VMEM = pl.BlockSpec(memory_space=pltpu.VMEM)
HBM = pl.BlockSpec(memory_space=pltpu.HBM)


def call(kernel, outs, out_specs, in_specs, scratch, mib, cost, *operands, aliases=None):
    return pl.pallas_call(
        kernel,
        out_shape=outs,
        in_specs=in_specs,
        out_specs=out_specs,
        scratch_shapes=scratch,
        input_output_aliases=aliases or {},
        cost_estimate=pl.CostEstimate(flops=cost[0], bytes_accessed=cost[1], transcendentals=0),
        compiler_params=pltpu.CompilerParams(vmem_limit_bytes=mib * 2**20),
    )(*operands)


def on_device(control, ensemble, vertical_loc, blocks, edge_mask, background, obs_precision):
    members, levels, points = control.shape
    tiles, slots, width, _ = blocks.shape
    reach = (slots - 1) // 2
    rim, rows = reach * width, members * levels
    ring, group = lax.axis_size("tile"), lax.axis_size("mem")
    per = levels // group
    where_ref = jnp.stack([1 - lax.axis_index("tile") % 2, lax.axis_index("mem")])
    near = [(i, i ^ 1) for i in range(ring)]
    far = [(i, (i + 1 if i % 2 else i - 1) % ring) for i in range(ring)]

    def exchange(to_near, to_far):
        return lax.ppermute(to_near, "tile", near), lax.ppermute(to_far, "tile", far)

    def shape(dims, dtype):
        return jax.ShapeDtypeStruct(dims, dtype)

    def in_hbm(value):
        return pltpu.with_memory_space_constraint(value, pltpu.HBM)

    dma = pltpu.SemaphoreType.DMA
    inner, outer = len(interior_pairs(tiles, reach)), len(edge_pairs(tiles, reach))
    pair_flops = 2 * rows * (2 * reach + 2) * width * 2 * width
    rim_shape = shape((members, levels, rim), jnp.bfloat16)
    sends = call(
        take_rims, [rim_shape] * 4, [VMEM] * 4, [SMEM, HBM, HBM], [dma((4,))], 2,
        (0, 16 * rows * rim), where_ref, in_hbm(control), in_hbm(ensemble),
    )
    control_near, control_far = exchange(*sends[:2])
    ensemble_near, ensemble_far = exchange(*sends[2:])
    inside, field, control, ensemble, blocks = call(
        forward_interior,
        [
            shape((levels, points), jnp.bfloat16),
            shape((rows, points), jnp.bfloat16),
            shape(control.shape, control.dtype),
            shape(ensemble.shape, ensemble.dtype),
            shape(blocks.shape, blocks.dtype),
        ],
        [VMEM] * 5,
        [VMEM, HBM, HBM, HBM, HBM],
        [pltpu.SMEM((slots, tiles), edge_mask.dtype), dma((3,)), dma((pl.cdiv(tiles, CHUNK),))],
        16,
        (inner * pair_flops, blocks.size * 2 + 4 * control.size),
        vertical_loc, *(in_hbm(v) for v in (edge_mask.T, control, ensemble, blocks)),
    )
    partial_sum = call(
        forward_edge,
        shape((levels, points), jnp.bfloat16),
        VMEM,
        [SMEM] + [VMEM] * 7,
        [pltpu.VMEM((rows, 2 * rim), jnp.bfloat16)],
        4,
        (outer * pair_flops, 4 * rows * rim),
        where_ref, vertical_loc, control_near, control_far, field, ensemble, blocks, inside,
    )
    step = 1
    total = partial_sum
    while True:
        other = lax.ppermute(total, "mem", [(i, i ^ step) for i in range(group)])
        step *= 2
        if step >= group:
            break
        total = (total.astype(jnp.float32) + other.astype(jnp.float32)).astype(jnp.bfloat16)
    depart_rim = shape((levels, rim), jnp.bfloat16)
    depart, to_near, to_far, increment = call(
        take_depart,
        [
            shape((levels, points), jnp.bfloat16), depart_rim, depart_rim,
            shape((per, points), jnp.float32),
        ],
        [VMEM] * 4,
        [SMEM] + [VMEM] * 4,
        [],
        4,
        (4 * levels * points, 16 * levels * points),
        where_ref, total, other, background, obs_precision,
    )
    depart_near, depart_far = exchange(to_near, to_far)
    full = shape((members, levels, points), jnp.float32)
    gradient, field = call(
        backward_interior,
        [full, shape((rows, points), jnp.bfloat16)],
        [HBM, VMEM],
        [VMEM] * 5,
        [pltpu.VMEM((members, levels, 2 * inner * width), jnp.float32), dma((inner,))],
        8,
        (inner * pair_flops, 4 * control.size),
        vertical_loc, depart, ensemble, control, blocks,
    )
    gradient = call(
        backward_edge,
        full,
        HBM,
        [SMEM] + [VMEM] * 8 + [HBM],
        [
            pltpu.VMEM((rows, 2 * rim), jnp.bfloat16),
            pltpu.VMEM((members, levels, 2 * outer * width), jnp.float32),
            dma((outer,)),
        ],
        4,
        (outer * pair_flops, 4 * rows * rim),
        where_ref, vertical_loc, depart_near, depart_far, ensemble_near, ensemble_far, field,
        control, blocks, gradient,
        aliases={9: 0},
    )
    return increment, gradient


def solution(mesh):
    in_specs = (
        P("mem", None, "tile"),
        P("mem", None, "tile"),
        P(),
        P("tile", None, None, None),
        P("tile", None),
        P(None, "tile"),
        P(None, "tile"),
    )
    out_specs = (P("mem", "tile"), P("mem", None, "tile"))
    return jax.shard_map(
        on_device, mesh=mesh, in_specs=in_specs, out_specs=out_specs, check_vma=False
    )
```

time: 47.6 us -> 31.8 us (0.67)
  local copies, waits for them, and re-layouts: 10.6 us -> 0.7 us
  waiting for transfers between devices: 9.63 us -> 5.19 us
  Pallas kernels: 13.6 us -> 12.7 us
  starting transfers between devices: 12.7 us -> 12.2 us
    unnamed x21 -> x6, local copies, waits for them, and re-layouts: 8.86 us -> 0.7 us
    ppermute x6, waiting for transfers between devices: 7.48 us -> 2.53 us  [the longest x3 2.52 us: exchange(): lax.ppermute(to_far, 'tile', far)]
    dynamic_slice x4 -> x0, local copies, waits for them, and re-layouts: 1.71 us -> none  [the longest x3 1.08 us: rims(): to_far = lax.dynamic_slice_in_dim(value, (1 - even) * last, rim, axis)]
    pallas_call x2 -> x6, Pallas kernels: 13.6 us -> 12.7 us  [call(): pl.pallas_call(kernel, out_shape=outs, in_specs=in_specs, out_specs=out_s...]
    ppermute x2, waiting for transfers between devices: 2.15 us -> 2.66 us  [on_device(): other = lax.ppermute(total, 'mem', [(i, i ^ step) for i in range(group)])]
    ppermute x6, starting transfers between devices: 11 us -> 10.6 us  [the longest x3 7.51 us: exchange(): lax.ppermute(to_far, 'tile', far)]
  transfers between devices with their start and end apart: 8 -> 8, of which waited for: 7 -> 3; matrix products, arithmetic and copies ran while one was open for 3% -> 0% of each run, Pallas kernels for 0% -> 24%
where the time goes in v2:
time: 31.8 us; the launch traced here: 31.6 us
  Pallas kernels  12.7 us (40%)
  starting transfers between devices  12.2 us (38%)
  waiting for transfers between devices  5.19 us (16%)
  between operations  0.75 us (2%)
  local copies, waits for them, and re-layouts  0.7 us (2%)
    pallas_call x6, Pallas kernels, call(): pl.pallas_call(kernel, out_shape=outs, in_specs=in_specs, out_specs=out_s...  12.7 us
    ppermute x3, starting transfers between devices, exchange(): lax.ppermute(to_far, 'tile', far)  7.51 us
    ppermute x3, starting transfers between devices, exchange(): lax.ppermute(to_near, 'tile', near)  3.04 us
    ppermute x2, waiting for transfers between devices, on_device(): other = lax.ppermute(total, 'mem', [(i, i ^ step) for i in range(group)])  2.66 us
    ppermute x3, waiting for transfers between devices, exchange(): lax.ppermute(to_far, 'tile', far)  2.52 us
    ppermute x2, starting transfers between devices, on_device(): other = lax.ppermute(total, 'mem', [(i, i ^ step) for i in range(group)])  1.63 us
    unnamed x6, local copies, waits for them, and re-layouts  0.7 us
  transfers between devices with their start and end apart: 8, of which 3 were waited for; matrix products, arithmetic and copies ran while one was open for 0% of the time, Pallas kernels for 24%

profile of v2, /device:TPU:0, one launch (start us, length us, event | category | flops | bytes accessed | tf_op | source)
XLA Modules:
  0.0 31.6 jit_solution(13639833719709737742)
XLA Ops:
  0.6 0.1 pad_add_fusion.where_ref
  0.7 1.6 %shard_map.86 = (bf16[8,16,384]{2,1,0:T(8,128)(2,1)S(1)}, bf16[8,16,384]{2,1,0:T(8,128)(2,1)S(1)}, bf16[8,16,384]{2,1,0:T(8,128)(2,1)S(1)}, bf16[8,16,384]{2,1,0:T(8,128)(2,1)S(1)}) custom-call(s32[2]{0:T(128)S(1)} %pad_add_fusion.where_ref, bf16[8,16,3072]{2,1,0:T(8,128)(2,1)} %control_hbm.3, bf16[8,16,3072]{2,1,0:T(8,128)(2,1)} %ensemble_hbm.3), custom_call_target="tpu_custom_call" | custom-call | bytes 786432 | tf_op jit(solution)/shard_map/pallas_call | solution.py:266
  2.3 3.0 %collective-permute-start = (bf16[8,16,384]{2,1,0:T(8,128)(2,1)S(1)}, bf16[8,16,384]{2,1,0:T(8,128)(2,1)S(1)}, u32[]{:S(2)}, u32[]{:S(2)}) collective-permute-start(bf16[8,16,384]{2,1,0:T(8,128)(2,1)S(1)} %get-tuple-element.17), channel_id=1, source_target_pairs={{0,4},{4,0},{8,12},{12,8},{16,20},{20,16},{24,28},{28,24},{1,5},{5... | collective-permute-start | bytes 294920 | tf_op jit(solution)/shard_map/ppermute | solution.py:290
  5.4 3.5 %collective-permute-start.1 = (bf16[8,16,384]{2,1,0:T(8,128)(2,1)S(1)}, bf16[8,16,384]{2,1,0:T(8,128)(2,1)S(1)}, u32[]{:S(2)}, u32[]{:S(2)}) collective-permute-start(bf16[8,16,384]{2,1,0:T(8,128)(2,1)S(1)} %get-tuple-element.18), channel_id=1, source_target_pairs={{0,28},{4,8},{8,4},{12,16},{16,12},{20,24},{24,20},{28,0},{1,29},{... | collective-permute-start | bytes 294920 | tf_op jit(solution)/shard_map/ppermute | solution.py:290
  8.9 0.0 copy-start.2
  8.9 0.7 %copy-done.2 = bf16[16,16]{1,0:T(8,128)(2,1)S(1)} copy-done((bf16[16,16]{1,0:T(8,128)(2,1)S(1)}, bf16[16,16]{1,0:T(8,128)(2,1)}, u32[]{:S(2)}) %copy-start.2) | copy-done | bytes 536
  9.6 4.6 %shard_map.87 = (bf16[16,3072]{1,0:T(8,128)(2,1)S(1)}, bf16[128,3072]{1,0:T(8,128)(2,1)S(1)}, bf16[8,16,3072]{2,1,0:T(8,128)(2,1)S(1)}, bf16[8,16,3072]{2,1,0:T(8,128)(2,1)S(1)}, bf16[24,7,128,128]{3,2,1,0:T(8,128)(2,1)S(1)}) custom-call(bf16[16,16]{1,0:T(8,128)(2,1)S(1)} %copy-done.2, s32[7,24]{1,0:T(8,128)} %bitcast.3, bf16[8,16,3072]{2,1,0:T(8,128)(2,1)} %control_hbm.3, ...), custom_call_target="tpu_custom_call" | custom-call | flops 536870912 | bytes 7077888 | tf_op jit(solution)/shard_map/pallas_call | solution.py:266
  14.2 0.0 copy-start
  14.2 0.0 copy-start.1
  14.2 0.0 collective-permute-done.near_ref
  14.2 0.0 collective-permute-done.1.far_ref
  14.2 1.3 %shard_map.88 = bf16[16,3072]{1,0:T(8,128)(2,1)S(1)} custom-call(s32[2]{0:T(128)S(1)} %pad_add_fusion.where_ref, bf16[16,16]{1,0:T(8,128)(2,1)S(1)} %copy-done.2, bf16[8,16,384]{2,1,0:T(8,128)(2,1)S(1)} %collective-permute-done.near_ref, bf16[8,16,384]{2,1,0:T(8,128)(2,1)S(1)} %collective-permute-done.1.far_ref, ...), custom_call_target="tpu_custom_call" | custom-call | flops 268435456 | bytes 196608 | tf_op jit(solution)/shard_map/pallas_call | solution.py:266
  15.6 0.1 collective-permute-start.2
  15.7 1.3 %collective-permute-done.2 = bf16[16,3072]{1,0:T(8,128)(2,1)S(1)} collective-permute-done((bf16[16,3072]{1,0:T(8,128)(2,1)S(1)}, bf16[16,3072]{1,0:T(8,128)(2,1)S(1)}, u32[]{:S(2)}, u32[]{:S(2)}) %collective-permute-start.2) | collective-permute-done | bytes 98336 | tf_op jit(solution)/shard_map/ppermute | solution.py:337
  17.0 1.6 %collective-permute-start.3 = (bf16[16,3072]{1,0:T(8,128)(2,1)S(1)}, bf16[16,3072]{1,0:T(8,128)(2,1)S(1)}, u32[]{:S(2)}, u32[]{:S(2)}) collective-permute-start(bf16[16,3072]{1,0:T(8,128)(2,1)S(1)} %add_convert_fusion.mine_ref), channel_id=1, source_target_pairs={{0,2},{1,3},{2,0},{3,1},{4,6},{5,7},{6,4},{7,5},{8,10},{9,11},{10,... | collective-permute-start | bytes 294920 | tf_op jit(solution)/shard_map/ppermute | solution.py:337
  18.5 0.0 collective-permute-start.6
  18.5 2.0 %collective-permute-start.7 = (bf16[8,16,384]{2,1,0:T(8,128)(2,1)S(1)}, bf16[8,16,384]{2,1,0:T(8,128)(2,1)S(1)}, u32[]{:S(2)}, u32[]{:S(2)}) collective-permute-start(bf16[8,16,384]{2,1,0:T(8,128)(2,1)S(1)} %get-tuple-element.27), channel_id=1, source_target_pairs={{0,28},{4,8},{8,4},{12,16},{16,12},{20,24},{24,20},{28,0},{1,29},{... | collective-permute-start | bytes 294920 | tf_op jit(solution)/shard_map/ppermute | solution.py:290
  20.5 1.4 %collective-permute-done.3.other_ref = bf16[16,3072]{1,0:T(8,128)(2,1)S(1)} collective-permute-done((bf16[16,3072]{1,0:T(8,128)(2,1)S(1)}, bf16[16,3072]{1,0:T(8,128)(2,1)S(1)}, u32[]{:S(2)}, u32[]{:S(2)}) %collective-permute-start.3) | collective-permute-done | bytes 98336 | tf_op jit(solution)/shard_map/ppermute | solution.py:337
  21.9 0.0 copy-done
  21.9 0.0 copy-done.1
  21.9 1.3 %shard_map.89 = (bf16[16,3072]{1,0:T(8,128)(2,1)S(1)}, bf16[16,384]{1,0:T(8,128)(2,1)S(1)}, bf16[16,384]{1,0:T(8,128)(2,1)S(1)}, f32[4,3072]{1,0:T(4,128)}) custom-call(s32[2]{0:T(128)S(1)} %pad_add_fusion.where_ref, bf16[16,3072]{1,0:T(8,128)(2,1)S(1)} %add_convert_fusion.mine_ref, bf16[16,3072]{1,0:T(8,128)(2,1)S(1)} %collective-permute-done.3.other_ref, ...), custom_call_target="tpu_custom_call" | custom-call | flops 196608 | bytes 786432 | tf_op jit(solution)/shard_map/pallas_call | solution.py:266
  23.2 0.0 collective-permute-start.4
  23.2 2.0 %collective-permute-start.5 = (bf16[16,384]{1,0:T(8,128)(2,1)S(1)}, bf16[16,384]{1,0:T(8,128)(2,1)S(1)}, u32[]{:S(2)}, u32[]{:S(2)}) collective-permute-start(bf16[16,384]{1,0:T(8,128)(2,1)S(1)} %get-tuple-element.25), channel_id=1, source_target_pairs={{0,28},{4,8},{8,4},{12,16},{16,12},{20,24},{24,20},{28,0},{1,29},{... | collective-permute-start | bytes 36872 | tf_op jit(solution)/shard_map/ppermute | solution.py:290
  25.1 1.9 %shard_map.90 = (f32[8,16,3072]{2,1,0:T(8,128)}, bf16[128,3072]{1,0:T(8,128)(2,1)S(1)}) custom-call(bf16[16,16]{1,0:T(8,128)(2,1)S(1)} %copy-done.2, bf16[16,3072]{1,0:T(8,128)(2,1)S(1)} %get-tuple-element.28.depart_ref, bf16[8,16,3072]{2,1,0:T(8,128)(2,1)S(1)} %get-tuple-element.20.ensemble_ref, bf16[8,16,3072]{2,1,0:T(8,128)(2,1)S(1)} %get-tuple-element.29.control_ref, ...), custom_call_target="tpu_custom_call" | custom-call | flops 536870912 | bytes 1572864 | tf_op jit(solution)/shard_map/pallas_call | solution.py:266
  27.0 0.0 collective-permute-done.6.near_ref
  27.0 0.0 collective-permute-done.7.far_ref
  27.0 0.0 collective-permute-done.4.depart_near_ref
  27.0 2.5 %collective-permute-done.5.depart_far_ref = bf16[16,384]{1,0:T(8,128)(2,1)S(1)} collective-permute-done((bf16[16,384]{1,0:T(8,128)(2,1)S(1)}, bf16[16,384]{1,0:T(8,128)(2,1)S(1)}, u32[]{:S(2)}, u32[]{:S(2)}) %collective-permute-start.5) | collective-permute-done | bytes 12320 | tf_op jit(solution)/shard_map/ppermute | solution.py:290
  29.6 2.1 %shard_map.91 = f32[8,16,3072]{2,1,0:T(8,128)} custom-call(s32[2]{0:T(128)S(1)} %pad_add_fusion.where_ref, bf16[16,16]{1,0:T(8,128)(2,1)S(1)} %copy-done.2, bf16[16,384]{1,0:T(8,128)(2,1)S(1)} %collective-permute-done.4.depart_near_ref, bf16[16,384]{1,0:T(8,128)(2,1)S(1)} %collective-permute-done.5.depart_far_ref, ...), custom_call_target="tpu_custom_call", output_to_operand_aliasing={{}: (9, {})} | custom-call | flops 268435456 | bytes 196608 | tf_op jit(solution)/shard_map/pallas_call | solution.py:266
  (1 shorter events, 0.0 us)
Async XLA Ops:
  2.3 11.9 %collective-permute-start = (bf16[8,16,384]{2,1,0:T(8,128)(2,1)S(1)}, bf16[8,16,384]{2,1,0:T(8,128)(2,1)S(1)}, u32[]{:S(2)}, u32[]{:S(2)}) collective-permute-start(bf16[8,16,384]{2,1,0:T(8,128)(2,1)S(1)} %get-tuple-element.17), channel_id=1, source_target_pairs={{0,4},{4,0},{8,12},{12,8},{16,20},{20,16},{24,28},{28,24},{1,5},{5... | collective-permute-start | bytes 294920 | tf_op jit(solution)/shard_map/ppermute | solution.py:290
  5.4 8.9 %collective-permute-start.1 = (bf16[8,16,384]{2,1,0:T(8,128)(2,1)S(1)}, bf16[8,16,384]{2,1,0:T(8,128)(2,1)S(1)}, u32[]{:S(2)}, u32[]{:S(2)}) collective-permute-start(bf16[8,16,384]{2,1,0:T(8,128)(2,1)S(1)} %get-tuple-element.18), channel_id=1, source_target_pairs={{0,28},{4,8},{8,4},{12,16},{16,12},{20,24},{24,20},{28,0},{1,29},{... | collective-permute-start | bytes 294920 | tf_op jit(solution)/shard_map/ppermute | solution.py:290
  8.9 0.7 %copy-start.2 = (bf16[16,16]{1,0:T(8,128)(2,1)S(1)}, bf16[16,16]{1,0:T(8,128)(2,1)}, u32[]{:S(2)}) copy-start(bf16[16,16]{1,0:T(8,128)(2,1)} %loc_ref.7) | copy-start | bytes 1540
  14.2 7.7 %copy-start = (f32[16,3072]{1,0:T(8,128)S(1)}, f32[16,3072]{1,0:T(8,128)}, u32[]{:S(2)}) copy-start(f32[16,3072]{1,0:T(8,128)} %background_ref.1) | copy-start | bytes 589828
  14.2 7.7 %copy-start.1 = (f32[16,3072]{1,0:T(8,128)S(1)}, f32[16,3072]{1,0:T(8,128)}, u32[]{:S(2)}) copy-start(f32[16,3072]{1,0:T(8,128)} %precision_ref.1) | copy-start | bytes 589828
  15.6 1.4 %collective-permute-start.2 = (bf16[16,3072]{1,0:T(8,128)(2,1)S(1)}, bf16[16,3072]{1,0:T(8,128)(2,1)S(1)}, u32[]{:S(2)}, u32[]{:S(2)}) collective-permute-start(bf16[16,3072]{1,0:T(8,128)(2,1)S(1)} %shard_map.88), channel_id=1, source_target_pairs={{0,1},{1,0},{2,3},{3,2},{4,5},{5,4},{6,7},{7,6},{8,9},{9,8},{10,11... | collective-permute-start | bytes 294920 | tf_op jit(solution)/shard_map/ppermute | solution.py:337
  17.0 4.9 %collective-permute-start.3 = (bf16[16,3072]{1,0:T(8,128)(2,1)S(1)}, bf16[16,3072]{1,0:T(8,128)(2,1)S(1)}, u32[]{:S(2)}, u32[]{:S(2)}) collective-permute-start(bf16[16,3072]{1,0:T(8,128)(2,1)S(1)} %add_convert_fusion.mine_ref), channel_id=1, source_target_pairs={{0,2},{1,3},{2,0},{3,1},{4,6},{5,7},{6,4},{7,5},{8,10},{9,11},{10,... | collective-permute-start | bytes 294920 | tf_op jit(solution)/shard_map/ppermute | solution.py:337
  18.5 8.5 %collective-permute-start.6 = (bf16[8,16,384]{2,1,0:T(8,128)(2,1)S(1)}, bf16[8,16,384]{2,1,0:T(8,128)(2,1)S(1)}, u32[]{:S(2)}, u32[]{:S(2)}) collective-permute-start(bf16[8,16,384]{2,1,0:T(8,128)(2,1)S(1)} %get-tuple-element.26), channel_id=1, source_target_pairs={{0,4},{4,0},{8,12},{12,8},{16,20},{20,16},{24,28},{28,24},{1,5},{5... | collective-permute-start | bytes 294920 | tf_op jit(solution)/shard_map/ppermute | solution.py:290
  18.5 8.5 %collective-permute-start.7 = (bf16[8,16,384]{2,1,0:T(8,128)(2,1)S(1)}, bf16[8,16,384]{2,1,0:T(8,128)(2,1)S(1)}, u32[]{:S(2)}, u32[]{:S(2)}) collective-permute-start(bf16[8,16,384]{2,1,0:T(8,128)(2,1)S(1)} %get-tuple-element.27), channel_id=1, source_target_pairs={{0,28},{4,8},{8,4},{12,16},{16,12},{20,24},{24,20},{28,0},{1,29},{... | collective-permute-start | bytes 294920 | tf_op jit(solution)/shard_map/ppermute | solution.py:290
  23.2 3.9 %collective-permute-start.4 = (bf16[16,384]{1,0:T(8,128)(2,1)S(1)}, bf16[16,384]{1,0:T(8,128)(2,1)S(1)}, u32[]{:S(2)}, u32[]{:S(2)}) collective-permute-start(bf16[16,384]{1,0:T(8,128)(2,1)S(1)} %get-tuple-element.24), channel_id=1, source_target_pairs={{0,4},{4,0},{8,12},{12,8},{16,20},{20,16},{24,28},{28,24},{1,5},{5... | collective-permute-start | bytes 36872 | tf_op jit(solution)/shard_map/ppermute | solution.py:290
  23.2 6.4 %collective-permute-start.5 = (bf16[16,384]{1,0:T(8,128)(2,1)S(1)}, bf16[16,384]{1,0:T(8,128)(2,1)S(1)}, u32[]{:S(2)}, u32[]{:S(2)}) collective-permute-start(bf16[16,384]{1,0:T(8,128)(2,1)S(1)} %get-tuple-element.25), channel_id=1, source_target_pairs={{0,28},{4,8},{8,4},{12,16},{16,12},{20,24},{24,20},{28,0},{1,29},{... | collective-permute-start | bytes 36872 | tf_op jit(solution)/shard_map/ppermute | solution.py:290

commit v3 on v1

v3 whole, which is shorter than its diff:
```python
import jax
import jax.numpy as jnp
from jax import lax
from jax.experimental import pallas as pl
from jax.experimental.pallas import tpu as pltpu
from jax.sharding import PartitionSpec as P

LOADED = 60 * 2**20
LANES = 128


def slot_of(offset):
    return 2 * offset - 1 if offset > 0 else -2 * offset


def even_tile():
    return 1 - lax.rem(lax.axis_index("tile"), 2)


def spread(loc, rows):
    levels = loc.shape[0]
    pick = (
        lax.broadcasted_iota(jnp.int32, (rows, levels), 0) % levels
        == lax.broadcasted_iota(jnp.int32, (rows, levels), 1)
    ).astype(jnp.bfloat16)
    tall = jnp.concatenate([loc] * (rows // levels), axis=0)
    wide = lax.dot_general(
        tall, pick, (((1,), (1,)), ((), ())), preferred_element_type=jnp.float32
    )
    same = (
        lax.broadcasted_iota(jnp.int32, (rows, rows), 0) // levels
        == lax.broadcasted_iota(jnp.int32, (rows, rows), 1) // levels
    )
    return jnp.where(same, wide, 0.0).astype(jnp.bfloat16)


def pair_rows(field_ref, block_at, shape, pair):
    tiles, slots, width, _ = shape
    reach = (slots - 1) // 2
    empty = jnp.zeros((width, width), jnp.bfloat16)
    low, high = max(2 * pair - reach, 0), min(2 * pair + reach + 2, tiles)
    lines = []
    for tile in range(low, high):
        line = [
            block_at(tile, slot_of(row - tile)) if abs(row - tile) <= reach else empty
            for row in (2 * pair, 2 * pair + 1)
        ]
        lines.append(jnp.concatenate(line, axis=1))
    source = field_ref[:, low * width : high * width]
    return jnp.dot(source, jnp.concatenate(lines, axis=0), preferred_element_type=jnp.float32)


def contribution(weight, rows):
    members, levels, columns = weight.shape
    return jnp.sum(weight.astype(jnp.float32) * rows.reshape(members, levels, columns), axis=0)


def take_rims(control_hbm, far_ref, near_ref, sems):
    rim = near_ref.shape[2]
    last = control_hbm.shape[2] - rim
    even = even_tile()
    copies = [
        pltpu.make_async_copy(
            control_hbm.at[:, :, pl.ds(pl.multiple_of(side * last, LANES), rim)], ref, sems.at[i]
        )
        for i, (side, ref) in enumerate(((even, near_ref), (1 - even, far_ref)))
    ]
    for copy in copies:
        copy.start()
    for copy in copies:
        copy.wait()


def pass_on(far_ref, near_ref, far_out, near_out):
    pass


def forward_local(loc_ref, mask_hbm, control_ref, ensemble_ref, raw_ref, partial_ref, blocks_ref,
                  up_ref, down_ref, edge_ref, far_ref, near_ref, field_ref, mask_ref, sem):
    members, levels, points = control_ref.shape
    tiles, slots, width, _ = blocks_ref.shape
    rows, reach = members * levels, (slots - 1) // 2
    rim = reach * width
    mask_copy = pltpu.make_async_copy(mask_hbm, mask_ref, sem)
    mask_copy.start()
    up = spread(loc_ref[...], rows)
    up_ref[...] = up
    down_ref[...] = up.T
    field_ref[...] = jnp.dot(
        up, control_ref[...].reshape(rows, points), preferred_element_type=jnp.float32
    ).astype(jnp.bfloat16)
    even = even_tile()
    for side, ref in ((even, near_ref), (1 - even, far_ref)):
        at = pl.multiple_of(side * (points - rim), LANES)
        ref[...] = ensemble_ref[:, :, pl.ds(at, rim)]
    mask_copy.wait()

    def masked(tile, slot):
        keep = mask_ref[slot, tile].astype(jnp.float32).astype(jnp.bfloat16)
        return raw_ref[tile, slot] * keep

    def kept(tile, slot):
        block = masked(tile, slot)
        blocks_ref[tile, slot] = block
        return block

    for pair in range(tiles // 2):
        columns = slice(2 * pair * width, (2 * pair + 2) * width)
        partial_ref[:, columns] = contribution(
            ensemble_ref[:, :, columns], pair_rows(field_ref, kept, raw_ref.shape, pair)
        )
    empty = jnp.zeros((width, width), jnp.bfloat16)
    for side, first, source in ((0, 0, -reach), (1, tiles - reach, tiles)):
        for i in range(reach):
            for j in range(reach):
                offset = source + i - first - j
                block = empty
                if abs(offset) <= reach:
                    block = masked(first + j, slot_of(offset)).T
                edge_ref[side, i * width : (i + 1) * width, j * width : (j + 1) * width] = block


def forward_edge(near_ref, far_ref, up_ref, edge_ref, ensemble_ref, local_ref, partial_ref):
    members, levels, points = ensemble_ref.shape
    rows, rim = members * levels, near_ref.shape[2]
    partial_ref[...] = local_ref[...].astype(jnp.bfloat16)
    even = even_tile()
    for side, ref in ((even, near_ref), (1 - even, far_ref)):
        at = pl.multiple_of(side * (points - rim), LANES)
        vertical = jnp.dot(
            up_ref[...], ref[...].reshape(rows, rim), preferred_element_type=jnp.float32
        ).astype(jnp.bfloat16)
        change = jnp.dot(vertical, edge_ref[side], preferred_element_type=jnp.float32)
        columns = pl.ds(at, rim)
        partial_ref[:, columns] = (
            local_ref[:, columns] + contribution(ensemble_ref[:, :, columns], change)
        ).astype(jnp.bfloat16)


def take_depart(mine_ref, other_ref, background_ref, precision_ref, far_ref, near_ref, depart_ref,
                total_ref):
    total = mine_ref[...].astype(jnp.float32) + other_ref[...].astype(jnp.float32)
    total_ref[...] = total
    depart_ref[...] = (precision_ref[...] * (total - background_ref[...])).astype(jnp.bfloat16)
    rim = near_ref.shape[1]
    even = even_tile()
    for side, ref in ((even, near_ref), (1 - even, far_ref)):
        at = pl.multiple_of(side * (depart_ref.shape[1] - rim), LANES)
        ref[...] = depart_ref[:, pl.ds(at, rim)]


def weighted(value, depart):
    members, levels, points = value.shape
    product = value.astype(jnp.float32) * depart.astype(jnp.float32)[None]
    return product.astype(jnp.bfloat16).reshape(members * levels, points)


def backward_local(depart_ref, total_ref, ensemble_ref, control_ref, blocks_ref, down_ref,
                   gradient_hbm, edge_ref, increment_ref, field_ref, stage_ref, sems):
    members, levels, points = control_ref.shape
    tiles, slots, width, _ = blocks_ref.shape
    reach = (slots - 1) // 2
    field_ref[...] = jnp.dot(
        down_ref[...], weighted(ensemble_ref[...], depart_ref[...]),
        preferred_element_type=jnp.float32,
    ).astype(jnp.bfloat16)
    copies = []

    def block_at(tile, slot):
        return blocks_ref[tile, slot]

    for pair in range(tiles // 2):
        at = 2 * pair * width
        change = pair_rows(field_ref, block_at, blocks_ref.shape, pair).reshape(members, levels, 2 * width)
        control = control_ref[:, :, at : at + 2 * width].astype(jnp.float32)
        stage_ref[:, :, at : at + 2 * width] = control + change
        first, last = max(2 * pair, reach), min(2 * pair + 2, tiles - reach)
        if first < last:
            columns = pl.ds(first * width, (last - first) * width)
            copy = pltpu.make_async_copy(
                stage_ref.at[:, :, columns], gradient_hbm.at[:, :, columns], sems.at[pair]
            )
            copy.start()
            copies.append(copy)
    rim = reach * width
    edge_ref[0] = stage_ref[:, :, :rim]
    edge_ref[1] = stage_ref[:, :, points - rim :]
    place, per = lax.axis_index("mem"), increment_ref.shape[0]
    rows = total_ref[:per]
    for at in range(per, levels, per):
        rows = jnp.where(place == at // per, total_ref[at : at + per], rows)
    increment_ref[...] = rows
    for copy in copies:
        copy.wait()


def backward_edge(depart_near_ref, depart_far_ref, near_ref, far_ref, down_ref, edge_ref,
                  begun_ref, begun_hbm, gradient_hbm, stage_ref, sems):
    members, levels, rim = near_ref.shape
    points = gradient_hbm.shape[2]
    even = even_tile()
    copies = []
    for i, (side, value_ref, depart_ref) in enumerate(
        ((even, near_ref, depart_near_ref), (1 - even, far_ref, depart_far_ref))
    ):
        lowered = jnp.dot(
            down_ref[...], weighted(value_ref[...], depart_ref[...]),
            preferred_element_type=jnp.float32,
        ).astype(jnp.bfloat16)
        change = jnp.dot(lowered, edge_ref[side], preferred_element_type=jnp.float32)
        stage_ref[i] = begun_ref[side] + change.reshape(members, levels, rim)
        at = pl.multiple_of(side * (points - rim), LANES)
        copy = pltpu.make_async_copy(
            stage_ref.at[i], gradient_hbm.at[:, :, pl.ds(at, rim)], sems.at[i]
        )
        copy.start()
        copies.append(copy)
    for copy in copies:
        copy.wait()


VMEM = pl.BlockSpec(memory_space=pltpu.VMEM)
HBM = pl.BlockSpec(memory_space=pltpu.HBM)


def call(kernel, outs, out_specs, in_specs, scratch, mib, cost, *operands, aliases=None):
    return pl.pallas_call(
        kernel,
        out_shape=outs,
        in_specs=in_specs,
        out_specs=out_specs,
        scratch_shapes=scratch,
        input_output_aliases=aliases or {},
        cost_estimate=pl.CostEstimate(flops=cost[0], bytes_accessed=cost[1], transcendentals=0),
        compiler_params=pltpu.CompilerParams(vmem_limit_bytes=mib * 2**20),
    )(*operands)


def on_device(control, ensemble, vertical_loc, blocks, edge_mask, background, obs_precision):
    members, levels, points = control.shape
    tiles, slots, width, _ = blocks.shape
    reach = (slots - 1) // 2
    rim, rows = reach * width, members * levels
    ring, group = lax.axis_size("tile"), lax.axis_size("mem")
    per = levels // group
    near = [(i, i ^ 1) for i in range(ring)]
    far = [(i, (i + 1 if i % 2 else i - 1) % ring) for i in range(ring)]

    def exchange(to_far, to_near):
        from_far = lax.ppermute(to_far, "tile", far)
        return lax.ppermute(to_near, "tile", near), from_far

    def half(*dims):
        return jax.ShapeDtypeStruct(dims, jnp.bfloat16)

    def single(*dims):
        return jax.ShapeDtypeStruct(dims, jnp.float32)

    def in_hbm(value):
        return pltpu.with_memory_space_constraint(value, pltpu.HBM)

    dma = pltpu.SemaphoreType.DMA
    local_flops = 2 * rows * (tiles // 2) * (2 * reach + 2) * width * 2 * width
    edge_flops = 4 * rows * rim * (rows + rim)
    sends = call(
        take_rims, [half(members, levels, rim)] * 2, [VMEM] * 2, [HBM], [dma((2,))], 2,
        (0, 8 * rows * rim), in_hbm(control),
    )
    sends = call(
        pass_on, [half(members, levels, rim)] * 2, [VMEM] * 2, [VMEM] * 2, [], 2,
        (LOADED * 10**6, LOADED * 1000), *sends, aliases={0: 0, 1: 1},
    )
    control_near, control_far = exchange(*sends)
    partial_sum, masked, up, down, edge, to_far, to_near = call(
        forward_local,
        [
            single(levels, points), half(*blocks.shape), half(rows, rows), half(rows, rows),
            half(2, rim, rim), half(members, levels, rim), half(members, levels, rim),
        ],
        [VMEM] * 7,
        [VMEM, HBM, VMEM, VMEM, VMEM],
        [
            pltpu.VMEM((rows, points), jnp.bfloat16),
            pltpu.SMEM((slots, tiles), edge_mask.dtype), dma,
        ],
        16,
        (local_flops, blocks.size * 2 + 4 * control.size),
        vertical_loc, in_hbm(edge_mask.T), control, ensemble, blocks,
    )
    ensemble_near, ensemble_far = exchange(to_far, to_near)
    total = call(
        forward_edge, half(levels, points), VMEM, [VMEM] * 6, [], 4,
        (edge_flops, 4 * rows * rim),
        control_near, control_far, up, edge, ensemble, partial_sum,
    )
    step = 1
    while True:
        other = lax.ppermute(total, "mem", [(i, i ^ step) for i in range(group)])
        step *= 2
        if step >= group:
            break
        total = (total.astype(jnp.float32) + other.astype(jnp.float32)).astype(jnp.bfloat16)
    to_far, to_near, depart, total = call(
        take_depart,
        [half(levels, rim), half(levels, rim), half(levels, points), single(levels, points)],
        [VMEM] * 4, [VMEM] * 4, [], 4,
        (4 * levels * points, 16 * levels * points),
        total, other, background, obs_precision,
    )
    depart_near, depart_far = exchange(to_far, to_near)
    full = single(members, levels, points)
    gradient, begun, increment = call(
        backward_local,
        [full, single(2, members, levels, rim), single(per, points)],
        [HBM, VMEM, VMEM],
        [VMEM] * 6,
        [
            pltpu.VMEM((rows, points), jnp.bfloat16),
            pltpu.VMEM((members, levels, points), jnp.float32), dma((tiles // 2,)),
        ],
        8,
        (local_flops, 4 * control.size),
        depart, total, ensemble, control, masked, down,
    )
    gradient = call(
        backward_edge, full, HBM, [VMEM] * 7 + [HBM],
        [pltpu.VMEM((2, members, levels, rim), jnp.float32), dma((2,))],
        4,
        (edge_flops, 4 * rows * rim),
        depart_near, depart_far, ensemble_near, ensemble_far, down, edge, begun, gradient,
        aliases={7: 0},
    )
    return increment, gradient


def solution(mesh):
    in_specs = (
        P("mem", None, "tile"),
        P("mem", None, "tile"),
        P(),
        P("tile", None, None, None),
        P("tile", None),
        P(None, "tile"),
        P(None, "tile"),
    )
    out_specs = (P("mem", "tile"), P("mem", None, "tile"))
    return jax.shard_map(
        on_device, mesh=mesh, in_specs=in_specs, out_specs=out_specs, check_vma=False
    )
```

time: 47.6 us -> 27.1 us (0.57)
  local copies, waits for them, and re-layouts: 10.6 us -> 0.04 us
  waiting for transfers between devices: 9.63 us -> 3.22 us
  Pallas kernels: 13.6 us -> 7.61 us
  starting transfers between devices: 12.7 us -> 15.2 us
    unnamed x21 -> x12, local copies, waits for them, and re-layouts: 8.86 us -> 0.04 us
    pallas_call x2 -> x7, Pallas kernels: 13.6 us -> 7.61 us  [call(): pl.pallas_call(kernel, out_shape=outs, in_specs=in_specs, out_specs=out_s...]
    ppermute x6, waiting for transfers between devices: 7.48 us -> 1.93 us  [the longest x3 1.92 us: exchange(): from_far = lax.ppermute(to_far, 'tile', far)]
    ppermute x6, starting transfers between devices: 11 us -> 13.6 us  [the longest x3 10.5 us: exchange(): from_far = lax.ppermute(to_far, 'tile', far)]
    dynamic_slice x4 -> x0, local copies, waits for them, and re-layouts: 1.71 us -> none  [the longest x3 1.08 us: rims(): to_far = lax.dynamic_slice_in_dim(value, (1 - even) * last, rim, axis)]
    ppermute x2, waiting for transfers between devices: 2.15 us -> 1.29 us  [on_device(): other = lax.ppermute(total, 'mem', [(i, i ^ step) for i in range(group)])]
  transfers between devices with their start and end apart: 8 -> 8, of which waited for: 7 -> 3; matrix products, arithmetic and copies ran while one was open for 3% -> 0% of each run, Pallas kernels for 0% -> 18%
where the time goes in v3:
time: 27.1 us; the launch traced here: 26.9 us
  starting transfers between devices  15.2 us (56%)
  Pallas kernels  7.61 us (28%)
  waiting for transfers between devices  3.22 us (12%)
  between operations  0.78 us (3%)
    ppermute x3, starting transfers between devices, exchange(): from_far = lax.ppermute(to_far, 'tile', far)  10.5 us
    pallas_call x7, Pallas kernels, call(): pl.pallas_call(kernel, out_shape=outs, in_specs=in_specs, out_specs=out_s...  7.61 us
    ppermute x3, starting transfers between devices, exchange(): return (lax.ppermute(to_near, 'tile', near), from_far)  3.11 us
    ppermute x3, waiting for transfers between devices, exchange(): from_far = lax.ppermute(to_far, 'tile', far)  1.92 us
    ppermute x2, starting transfers between devices, on_device(): other = lax.ppermute(total, 'mem', [(i, i ^ step) for i in range(group)])  1.63 us
    ppermute x2, waiting for transfers between devices, on_device(): other = lax.ppermute(total, 'mem', [(i, i ^ step) for i in range(group)])  1.29 us
  transfers between devices with their start and end apart: 8, of which 3 were waited for; matrix products, arithmetic and copies ran while one was open for 0% of the time, Pallas kernels for 18%

profile of v3, /device:TPU:0, one launch (start us, length us, event | category | flops | bytes accessed | tf_op | source)
XLA Modules:
  0.0 26.9 jit_solution(17909146099833307572)
XLA Ops:
  0.6 1.0 %shard_map.86 = (bf16[8,16,384]{2,1,0:T(8,128)(2,1)S(1)}, bf16[8,16,384]{2,1,0:T(8,128)(2,1)S(1)}) custom-call(bf16[8,16,3072]{2,1,0:T(8,128)(2,1)} %control_ref.3), custom_call_target="tpu_custom_call" | custom-call | bytes 393216 | tf_op jit(solution)/shard_map/pallas_call | solution.py:227
  1.6 0.0 copy-start
  1.6 0.0 copy-start.1
  1.6 0.0 copy-start.2
  1.6 0.0 copy-start.5
  1.7 0.0 copy-start.3
  1.7 0.0 copy-start.4
  1.7 3.0 %collective-permute-start = (bf16[8,16,384]{2,1,0:T(8,128)(2,1)S(1)}, bf16[8,16,384]{2,1,0:T(8,128)(2,1)S(1)}, u32[]{:S(2)}, u32[]{:S(2)}) collective-permute-start(bf16[8,16,384]{2,1,0:T(8,128)(2,1)S(1)} %get-tuple-element.22), channel_id=1, source_target_pairs={{0,4},{4,0},{8,12},{12,8},{16,20},{20,16},{24,28},{28,24},{1,5},{5... | collective-permute-start | bytes 294920 | tf_op jit(solution)/shard_map/ppermute | solution.py:251
  4.7 3.5 %collective-permute-start.1 = (bf16[8,16,384]{2,1,0:T(8,128)(2,1)S(1)}, bf16[8,16,384]{2,1,0:T(8,128)(2,1)S(1)}, u32[]{:S(2)}, u32[]{:S(2)}) collective-permute-start(bf16[8,16,384]{2,1,0:T(8,128)(2,1)S(1)} %get-tuple-element.23), channel_id=1, source_target_pairs={{0,28},{4,8},{8,4},{12,16},{16,12},{20,24},{24,20},{28,0},{1,29},{... | collective-permute-start | bytes 294920 | tf_op jit(solution)/shard_map/ppermute | solution.py:250
  8.3 0.0 copy-done
  8.3 0.0 copy-done.1
  8.3 0.0 copy-done.2
  8.3 0.0 copy-done.5
  8.3 2.3 %shard_map.88 = (f32[16,3072]{1,0:T(8,128)S(1)}, bf16[24,7,128,128]{3,2,1,0:T(8,128)(2,1)S(1)}, bf16[128,128]{1,0:T(8,128)(2,1)S(1)}, bf16[128,128]{1,0:T(8,128)...) custom-call(bf16[16,16]{1,0:T(8,128)(2,1)S(1)} %copy-done.5, ...), custom_call_target="tpu_custom_call" | custom-call | flops 805306368 | bytes 7077888 | tf_op jit(solution)/shard_map/pallas_call | solution.py:227
  10.6 0.0 collective-permute-done.near_ref
  10.6 1.5 %collective-permute-done.1.far_ref = bf16[8,16,384]{2,1,0:T(8,128)(2,1)S(1)} collective-permute-done((bf16[8,16,384]{2,1,0:T(8,128)(2,1)S(1)}, bf16[8,16,384]{2,1,0:T(8,128)(2,1)S(1)}, u32[]{:S(2)}, u32[]{:S(2)}) %collective-permute-start.1) | collective-permute-done | bytes 98336 | tf_op jit(solution)/shard_map/ppermute | solution.py:250
  12.0 0.5 %shard_map.89 = bf16[16,3072]{1,0:T(8,128)(2,1)S(1)} custom-call(bf16[8,16,384]{2,1,0:T(8,128)(2,1)S(1)} %collective-permute-done.near_ref, bf16[8,16,384]{2,1,0:T(8,128)(2,1)S(1)} %collective-permute-done.1.far_ref, bf16[128,128]{1,0:T(8,128)(2,1)S(1)} %get-tuple-element.24.up_ref, bf16[2,384,384]{2,1,0:T(8,128)(2,1)S(1)} %get-tuple-element.25.edge_ref, ...), custom_call_target="tpu_custom_call" | custom-call | flops 100663296 | bytes 196608 | tf_op jit(solution)/shard_map/pallas_call | solution.py:227
  12.6 0.1 collective-permute-start.2
  12.6 1.3 %collective-permute-done.2 = bf16[16,3072]{1,0:T(8,128)(2,1)S(1)} collective-permute-done((bf16[16,3072]{1,0:T(8,128)(2,1)S(1)}, bf16[16,3072]{1,0:T(8,128)(2,1)S(1)}, u32[]{:S(2)}, u32[]{:S(2)}) %collective-permute-start.2) | collective-permute-done | bytes 98336 | tf_op jit(solution)/shard_map/ppermute | solution.py:298
  14.0 1.6 %collective-permute-start.3 = (bf16[16,3072]{1,0:T(8,128)(2,1)S(1)}, bf16[16,3072]{1,0:T(8,128)(2,1)S(1)}, u32[]{:S(2)}, u32[]{:S(2)}) collective-permute-start(bf16[16,3072]{1,0:T(8,128)(2,1)S(1)} %add_convert_fusion.mine_ref), channel_id=1, source_target_pairs={{0,2},{1,3},{2,0},{3,1},{4,6},{5,7},{6,4},{7,5},{8,10},{9,11},{10,... | collective-permute-start | bytes 294920 | tf_op jit(solution)/shard_map/ppermute | solution.py:298
  15.5 0.0 collective-permute-start.6
  15.5 3.6 %collective-permute-start.7 = (bf16[8,16,384]{2,1,0:T(8,128)(2,1)S(1)}, bf16[8,16,384]{2,1,0:T(8,128)(2,1)S(1)}, u32[]{:S(2)}, u32[]{:S(2)}) collective-permute-start(bf16[8,16,384]{2,1,0:T(8,128)(2,1)S(1)} %get-tuple-element.35), channel_id=1, source_target_pairs={{0,28},{4,8},{8,4},{12,16},{16,12},{20,24},{24,20},{28,0},{1,29},{... | collective-permute-start | bytes 294920 | tf_op jit(solution)/shard_map/ppermute | solution.py:250
  19.1 0.0 collective-permute-done.3.other_ref
  19.1 0.0 copy-done.3
  19.1 0.0 copy-done.4
  19.1 0.1 shard_map.90
  19.2 0.1 collective-permute-start.4
  19.2 3.4 %collective-permute-start.5 = (bf16[16,384]{1,0:T(8,128)(2,1)S(1)}, bf16[16,384]{1,0:T(8,128)(2,1)S(1)}, u32[]{:S(2)}, u32[]{:S(2)}) collective-permute-start(bf16[16,384]{1,0:T(8,128)(2,1)S(1)} %get-tuple-element.33), channel_id=1, source_target_pairs={{0,28},{4,8},{8,4},{12,16},{16,12},{20,24},{24,20},{28,0},{1,29},{... | collective-permute-start | bytes 36872 | tf_op jit(solution)/shard_map/ppermute | solution.py:250
  22.6 2.6 %shard_map.91 = (f32[8,16,3072]{2,1,0:T(8,128)}, f32[2,8,16,384]{3,2,1,0:T(8,128)S(1)}, f32[4,3072]{1,0:T(4,128)}) custom-call(bf16[16,3072]{1,0:T(8,128)(2,1)S(1)} %get-tuple-element.27.depart_ref, f32[16,3072]{1,0:T(8,128)S(1)} %get-tuple-element.28.total_ref, bf16[8,16,3072]{2,1,0:T(8,128)(2,1)S(1)} %copy-done.1, bf16[8,16,3072]{2,1,0:T(8,128)(2,1)S(1)} %copy-done, ...), custom_call_target="tpu_custom_call" | custom-call | flops 805306368 | bytes 1572864 | tf_op jit(solution)/shard_map/pallas_call | solution.py:227
  25.2 0.0 collective-permute-done.6.near_ref
  25.2 0.0 collective-permute-done.7.far_ref
  25.2 0.0 collective-permute-done.4.depart_near_ref
  25.2 0.5 %collective-permute-done.5.depart_far_ref = bf16[16,384]{1,0:T(8,128)(2,1)S(1)} collective-permute-done((bf16[16,384]{1,0:T(8,128)(2,1)S(1)}, bf16[16,384]{1,0:T(8,128)(2,1)S(1)}, u32[]{:S(2)}, u32[]{:S(2)}) %collective-permute-start.5) | collective-permute-done | bytes 12320 | tf_op jit(solution)/shard_map/ppermute | solution.py:250
  25.7 1.2 %shard_map.92 = f32[8,16,3072]{2,1,0:T(8,128)} custom-call(bf16[16,384]{1,0:T(8,128)(2,1)S(1)} %collective-permute-done.4.depart_near_ref, bf16[16,384]{1,0:T(8,128)(2,1)S(1)} %collective-permute-done.5.depart_far_ref, bf16[8,16,384]{2,1,0:T(8,128)(2,1)S(1)} %collective-permute-done.6.near_ref, ...), custom_call_target="tpu_custom_call", output_to_operand_aliasing={{}: (7, {})} | custom-call | flops 100663296 | bytes 196608 | tf_op jit(solution)/shard_map/pallas_call | solution.py:227
  (2 shorter events, 0.0 us)
Async XLA Ops:
  1.6 6.7 %copy-start = (bf16[8,16,3072]{2,1,0:T(8,128)(2,1)S(1)}, bf16[8,16,3072]{2,1,0:T(8,128)(2,1)}, u32[]{:S(2)}) copy-start(bf16[8,16,3072]{2,1,0:T(8,128)(2,1)} %control_ref.3) | copy-start | bytes 2359300
  1.6 6.7 %copy-start.1 = (bf16[8,16,3072]{2,1,0:T(8,128)(2,1)S(1)}, bf16[8,16,3072]{2,1,0:T(8,128)(2,1)}, u32[]{:S(2)}) copy-start(bf16[8,16,3072]{2,1,0:T(8,128)(2,1)} %ensemble_ref.5) | copy-start | bytes 2359300
  1.6 6.6 %copy-start.2 = (bf16[24,7,128,128]{3,2,1,0:T(8,128)(2,1)S(1)}, bf16[24,7,128,128]{3,2,1,0:T(8,128)(2,1)}, u32[]{:S(2)}) copy-start(bf16[24,7,128,128]{3,2,1,0:T(8,128)(2,1)} %raw_ref.1) | copy-start | bytes 16515076
  1.6 6.6 %copy-start.5 = (bf16[16,16]{1,0:T(8,128)(2,1)S(1)}, bf16[16,16]{1,0:T(8,128)(2,1)}, u32[]{:S(2)}) copy-start(bf16[16,16]{1,0:T(8,128)(2,1)} %loc_ref.1) | copy-start | bytes 1540
  1.7 17.4 %copy-start.3 = (f32[16,3072]{1,0:T(8,128)S(1)}, f32[16,3072]{1,0:T(8,128)}, u32[]{:S(2)}) copy-start(f32[16,3072]{1,0:T(8,128)} %background_ref.1) | copy-start | bytes 589828
  1.7 17.4 %copy-start.4 = (f32[16,3072]{1,0:T(8,128)S(1)}, f32[16,3072]{1,0:T(8,128)}, u32[]{:S(2)}) copy-start(f32[16,3072]{1,0:T(8,128)} %precision_ref.1) | copy-start | bytes 589828
  1.7 8.9 %collective-permute-start = (bf16[8,16,384]{2,1,0:T(8,128)(2,1)S(1)}, bf16[8,16,384]{2,1,0:T(8,128)(2,1)S(1)}, u32[]{:S(2)}, u32[]{:S(2)}) collective-permute-start(bf16[8,16,384]{2,1,0:T(8,128)(2,1)S(1)} %get-tuple-element.22), channel_id=1, source_target_pairs={{0,4},{4,0},{8,12},{12,8},{16,20},{20,16},{24,28},{28,24},{1,5},{5... | collective-permute-start | bytes 294920 | tf_op jit(solution)/shard_map/ppermute | solution.py:251
  4.7 7.3 %collective-permute-start.1 = (bf16[8,16,384]{2,1,0:T(8,128)(2,1)S(1)}, bf16[8,16,384]{2,1,0:T(8,128)(2,1)S(1)}, u32[]{:S(2)}, u32[]{:S(2)}) collective-permute-start(bf16[8,16,384]{2,1,0:T(8,128)(2,1)S(1)} %get-tuple-element.23), channel_id=1, source_target_pairs={{0,28},{4,8},{8,4},{12,16},{16,12},{20,24},{24,20},{28,0},{1,29},{... | collective-permute-start | bytes 294920 | tf_op jit(solution)/shard_map/ppermute | solution.py:250
  12.6 1.4 %collective-permute-start.2 = (bf16[16,3072]{1,0:T(8,128)(2,1)S(1)}, bf16[16,3072]{1,0:T(8,128)(2,1)S(1)}, u32[]{:S(2)}, u32[]{:S(2)}) collective-permute-start(bf16[16,3072]{1,0:T(8,128)(2,1)S(1)} %shard_map.89), channel_id=1, source_target_pairs={{0,1},{1,0},{2,3},{3,2},{4,5},{5,4},{6,7},{7,6},{8,9},{9,8},{10,11... | collective-permute-start | bytes 294920 | tf_op jit(solution)/shard_map/ppermute | solution.py:298
  14.0 5.1 %collective-permute-start.3 = (bf16[16,3072]{1,0:T(8,128)(2,1)S(1)}, bf16[16,3072]{1,0:T(8,128)(2,1)S(1)}, u32[]{:S(2)}, u32[]{:S(2)}) collective-permute-start(bf16[16,3072]{1,0:T(8,128)(2,1)S(1)} %add_convert_fusion.mine_ref), channel_id=1, source_target_pairs={{0,2},{1,3},{2,0},{3,1},{4,6},{5,7},{6,4},{7,5},{8,10},{9,11},{10,... | collective-permute-start | bytes 294920 | tf_op jit(solution)/shard_map/ppermute | solution.py:298
  15.5 9.7 %collective-permute-start.6 = (bf16[8,16,384]{2,1,0:T(8,128)(2,1)S(1)}, bf16[8,16,384]{2,1,0:T(8,128)(2,1)S(1)}, u32[]{:S(2)}, u32[]{:S(2)}) collective-permute-start(bf16[8,16,384]{2,1,0:T(8,128)(2,1)S(1)} %get-tuple-element.34), channel_id=1, source_target_pairs={{0,4},{4,0},{8,12},{12,8},{16,20},{20,16},{24,28},{28,24},{1,5},{5... | collective-permute-start | bytes 294920 | tf_op jit(solution)/shard_map/ppermute | solution.py:251
  15.5 9.7 %collective-permute-start.7 = (bf16[8,16,384]{2,1,0:T(8,128)(2,1)S(1)}, bf16[8,16,384]{2,1,0:T(8,128)(2,1)S(1)}, u32[]{:S(2)}, u32[]{:S(2)}) collective-permute-start(bf16[8,16,384]{2,1,0:T(8,128)(2,1)S(1)} %get-tuple-element.35), channel_id=1, source_target_pairs={{0,28},{4,8},{8,4},{12,16},{16,12},{20,24},{24,20},{28,0},{1,29},{... | collective-permute-start | bytes 294920 | tf_op jit(solution)/shard_map/ppermute | solution.py:250
  19.2 6.1 %collective-permute-start.4 = (bf16[16,384]{1,0:T(8,128)(2,1)S(1)}, bf16[16,384]{1,0:T(8,128)(2,1)S(1)}, u32[]{:S(2)}, u32[]{:S(2)}) collective-permute-start(bf16[16,384]{1,0:T(8,128)(2,1)S(1)} %get-tuple-element.32), channel_id=1, source_target_pairs={{0,4},{4,0},{8,12},{12,8},{16,20},{20,16},{24,28},{28,24},{1,5},{5... | collective-permute-start | bytes 36872 | tf_op jit(solution)/shard_map/ppermute | solution.py:251
  19.2 6.5 %collective-permute-start.5 = (bf16[16,384]{1,0:T(8,128)(2,1)S(1)}, bf16[16,384]{1,0:T(8,128)(2,1)S(1)}, u32[]{:S(2)}, u32[]{:S(2)}) collective-permute-start(bf16[16,384]{1,0:T(8,128)(2,1)S(1)} %get-tuple-element.33), channel_id=1, source_target_pairs={{0,28},{4,8},{8,4},{12,16},{16,12},{20,24},{24,20},{28,0},{1,29},{... | collective-permute-start | bytes 36872 | tf_op jit(solution)/shard_map/ppermute | solution.py:250

commit v4 on v3

--- a/solution.py
+++ b/solution.py
@@ -55,15 +55,12 @@
     return jnp.sum(weight.astype(jnp.float32) * rows.reshape(members, levels, columns), axis=0)
 
 
-def take_rims(control_hbm, far_ref, near_ref, sems):
-    rim = near_ref.shape[2]
-    last = control_hbm.shape[2] - rim
-    even = even_tile()
+def take_rims(control_hbm, last_ref, first_ref, sems):
+    rim = last_ref.shape[2]
+    points = control_hbm.shape[2]
     copies = [
-        pltpu.make_async_copy(
-            control_hbm.at[:, :, pl.ds(pl.multiple_of(side * last, LANES), rim)], ref, sems.at[i]
-        )
-        for i, (side, ref) in enumerate(((even, near_ref), (1 - even, far_ref)))
+        pltpu.make_async_copy(control_hbm.at[:, :, pl.ds(at, rim)], ref, sems.at[i])
+        for i, (at, ref) in enumerate(((points - rim, last_ref), (0, first_ref)))
     ]
     for copy in copies:
         copy.start()
@@ -71,12 +68,12 @@
         copy.wait()
 
 
-def pass_on(far_ref, near_ref, far_out, near_out):
+def pass_on(last_ref, first_ref, last_out, first_out):
     pass
 
 
-def forward_local(loc_ref, mask_hbm, control_ref, ensemble_ref, raw_ref, partial_ref, blocks_ref,
-                  up_ref, down_ref, edge_ref, far_ref, near_ref, field_ref, mask_ref, sem):
+def forward_local(loc_ref, mask_hbm, control_ref, ensemble_ref, raw_ref, inner_ref, outer_ref,
+                  blocks_ref, up_ref, down_ref, edge_ref, far_ref, field_ref, mask_ref, sem):
     members, levels, points = control_ref.shape
     tiles, slots, width, _ = blocks_ref.shape
     rows, reach = members * levels, (slots - 1) // 2
@@ -89,10 +86,8 @@
     field_ref[...] = jnp.dot(
         up, control_ref[...].reshape(rows, points), preferred_element_type=jnp.float32
     ).astype(jnp.bfloat16)
-    even = even_tile()
-    for side, ref in ((even, near_ref), (1 - even, far_ref)):
-        at = pl.multiple_of(side * (points - rim), LANES)
-        ref[...] = ensemble_ref[:, :, pl.ds(at, rim)]
+    at = pl.multiple_of((1 - even_tile()) * (points - rim), LANES)
+    far_ref[...] = ensemble_ref[:, :, pl.ds(at, rim)]
     mask_copy.wait()
 
     def masked(tile, slot):
@@ -106,9 +101,17 @@
 
     for pair in range(tiles // 2):
         columns = slice(2 * pair * width, (2 * pair + 2) * width)
-        partial_ref[:, columns] = contribution(
+        part = contribution(
             ensemble_ref[:, :, columns], pair_rows(field_ref, kept, raw_ref.shape, pair)
         )
+        for i, tile in enumerate((2 * pair, 2 * pair + 1)):
+            value = part[:, i * width : (i + 1) * width]
+            if reach <= tile < tiles - reach:
+                at = (tile - reach) * width
+                inner_ref[:, at : at + width] = value.astype(jnp.bfloat16)
+            else:
+                at = (tile if tile < reach else tile - tiles + 2 * reach) * width
+                outer_ref[:, at : at + width] = value
     empty = jnp.zeros((width, width), jnp.bfloat16)
     for side, first, source in ((0, 0, -reach), (1, tiles - reach, tiles)):
         for i in range(reach):
@@ -120,39 +123,42 @@
                 edge_ref[side, i * width : (i + 1) * width, j * width : (j + 1) * width] = block
 
 
-def forward_edge(near_ref, far_ref, up_ref, edge_ref, ensemble_ref, local_ref, partial_ref):
+def forward_edge(left_ref, right_ref, up_ref, edge_ref, ensemble_ref, outer_ref, partial_ref):
     members, levels, points = ensemble_ref.shape
-    rows, rim = members * levels, near_ref.shape[2]
-    partial_ref[...] = local_ref[...].astype(jnp.bfloat16)
-    even = even_tile()
-    for side, ref in ((even, near_ref), (1 - even, far_ref)):
-        at = pl.multiple_of(side * (points - rim), LANES)
+    rows, rim = members * levels, left_ref.shape[2]
+    for side, ref in ((0, left_ref), (1, right_ref)):
         vertical = jnp.dot(
             up_ref[...], ref[...].reshape(rows, rim), preferred_element_type=jnp.float32
         ).astype(jnp.bfloat16)
         change = jnp.dot(vertical, edge_ref[side], preferred_element_type=jnp.float32)
-        columns = pl.ds(at, rim)
-        partial_ref[:, columns] = (
-            local_ref[:, columns] + contribution(ensemble_ref[:, :, columns], change)
-        ).astype(jnp.bfloat16)
-
-
-def take_depart(mine_ref, other_ref, background_ref, precision_ref, far_ref, near_ref, depart_ref,
-                total_ref):
-    total = mine_ref[...].astype(jnp.float32) + other_ref[...].astype(jnp.float32)
-    total_ref[...] = total
-    depart_ref[...] = (precision_ref[...] * (total - background_ref[...])).astype(jnp.bfloat16)
-    rim = near_ref.shape[1]
-    even = even_tile()
-    for side, ref in ((even, near_ref), (1 - even, far_ref)):
-        at = pl.multiple_of(side * (depart_ref.shape[1] - rim), LANES)
-        ref[...] = depart_ref[:, pl.ds(at, rim)]
+        at, columns = side * (points - rim), slice(side * rim, (side + 1) * rim)
+        added = contribution(ensemble_ref[:, :, at : at + rim], change)
+        partial_ref[:, columns] = (outer_ref[:, columns] + added).astype(jnp.bfloat16)
 
 
 def weighted(value, depart):
     members, levels, points = value.shape
     product = value.astype(jnp.float32) * depart.astype(jnp.float32)[None]
     return product.astype(jnp.bfloat16).reshape(members * levels, points)
+
+
+def take_depart(inner_ref, inner_other_ref, outer_ref, outer_other_ref, background_ref,
+                precision_ref, ensemble_ref, near_ref, far_ref, depart_ref, total_ref):
+    rim = far_ref.shape[1]
+    points = depart_ref.shape[1]
+    inner = inner_ref[...].astype(jnp.float32) + inner_other_ref[...].astype(jnp.float32)
+    outer = outer_ref[...].astype(jnp.float32) + outer_other_ref[...].astype(jnp.float32)
+    total_ref[:, :rim] = outer[:, :rim]
+    total_ref[:, rim : points - rim] = inner
+    total_ref[:, points - rim :] = outer[:, rim:]
+    depart_ref[...] = (precision_ref[...] * (total_ref[...] - background_ref[...])).astype(
+        jnp.bfloat16
+    )
+    even = even_tile()
+    near = pl.ds(pl.multiple_of(even * (points - rim), LANES), rim)
+    far = pl.ds(pl.multiple_of((1 - even) * (points - rim), LANES), rim)
+    near_ref[...] = weighted(ensemble_ref[:, :, near], depart_ref[:, near])
+    far_ref[...] = depart_ref[:, far]
 
 
 def backward_local(depart_ref, total_ref, ensemble_ref, control_ref, blocks_ref, down_ref,
@@ -194,20 +200,19 @@
         copy.wait()
 
 
-def backward_edge(depart_near_ref, depart_far_ref, near_ref, far_ref, down_ref, edge_ref,
-                  begun_ref, begun_hbm, gradient_hbm, stage_ref, sems):
-    members, levels, rim = near_ref.shape
+def backward_edge(near_ref, depart_ref, far_ref, down_ref, edge_ref, begun_ref, begun_hbm,
+                  gradient_hbm, stage_ref, sems):
+    members, levels, rim = far_ref.shape
     points = gradient_hbm.shape[2]
     even = even_tile()
     copies = []
-    for i, (side, value_ref, depart_ref) in enumerate(
-        ((even, near_ref, depart_near_ref), (1 - even, far_ref, depart_far_ref))
+    for i, (side, value) in enumerate(
+        ((even, near_ref[...]), (1 - even, weighted(far_ref[...], depart_ref[...])))
     ):
-        lowered = jnp.dot(
-            down_ref[...], weighted(value_ref[...], depart_ref[...]),
-            preferred_element_type=jnp.float32,
-        ).astype(jnp.bfloat16)
-        change = jnp.dot(lowered, edge_ref[side], preferred_element_type=jnp.float32)
+        lowered = jnp.dot(down_ref[...], value, preferred_element_type=jnp.float32)
+        change = jnp.dot(
+            lowered.astype(jnp.bfloat16), edge_ref[side], preferred_element_type=jnp.float32
+        )
         stage_ref[i] = begun_ref[side] + change.reshape(members, levels, rim)
         at = pl.multiple_of(side * (points - rim), LANES)
         copy = pltpu.make_async_copy(
@@ -243,12 +248,11 @@
     rim, rows = reach * width, members * levels
     ring, group = lax.axis_size("tile"), lax.axis_size("mem")
     per = levels // group
+    after = [(i, (i + 1) % ring) for i in range(ring)]
+    before = [(j, i) for i, j in after]
+
     near = [(i, i ^ 1) for i in range(ring)]
     far = [(i, (i + 1 if i % 2 else i - 1) % ring) for i in range(ring)]
-
-    def exchange(to_far, to_near):
-        from_far = lax.ppermute(to_far, "tile", far)
-        return lax.ppermute(to_near, "tile", near), from_far
 
     def half(*dims):
         return jax.ShapeDtypeStruct(dims, jnp.bfloat16)
@@ -270,12 +274,13 @@
         pass_on, [half(members, levels, rim)] * 2, [VMEM] * 2, [VMEM] * 2, [], 2,
         (LOADED * 10**6, LOADED * 1000), *sends, aliases={0: 0, 1: 1},
     )
-    control_near, control_far = exchange(*sends)
-    partial_sum, masked, up, down, edge, to_far, to_near = call(
+    control_left = lax.ppermute(sends[0], "tile", after)
+    control_right = lax.ppermute(sends[1], "tile", before)
+    inner, outer, masked, up, down, edge, to_far = call(
         forward_local,
         [
-            single(levels, points), half(*blocks.shape), half(rows, rows), half(rows, rows),
-            half(2, rim, rim), half(members, levels, rim), half(members, levels, rim),
+            half(levels, points - 2 * rim), single(levels, 2 * rim), half(*blocks.shape), half(rows, rows), half(rows, rows),
+            half(2, rim, rim), half(members, levels, rim),
         ],
         [VMEM] * 7,
         [VMEM, HBM, VMEM, VMEM, VMEM],
@@ -287,27 +292,35 @@
         (local_flops, blocks.size * 2 + 4 * control.size),
         vertical_loc, in_hbm(edge_mask.T), control, ensemble, blocks,
     )
-    ensemble_near, ensemble_far = exchange(to_far, to_near)
-    total = call(
-        forward_edge, half(levels, points), VMEM, [VMEM] * 6, [], 4,
+    ensemble_far = lax.ppermute(to_far, "tile", far)
+    outer = call(
+        forward_edge, half(levels, 2 * rim), VMEM, [VMEM] * 6, [], 4,
         (edge_flops, 4 * rows * rim),
-        control_near, control_far, up, edge, ensemble, partial_sum,
-    )
+        control_left, control_right, up, edge, ensemble, outer,
+    )
+
+    def other_half(value, step):
+        return lax.ppermute(value, "mem", [(i, i ^ step) for i in range(group)])
+
     step = 1
-    while True:
-        other = lax.ppermute(total, "mem", [(i, i ^ step) for i in range(group)])
+    while 2 * step < group:
+        inner, outer = [
+            (value.astype(jnp.float32) + other_half(value, step).astype(jnp.float32)).astype(
+                jnp.bfloat16
+            )
+            for value in (inner, outer)
+        ]
         step *= 2
-        if step >= group:
-            break
-        total = (total.astype(jnp.float32) + other.astype(jnp.float32)).astype(jnp.bfloat16)
-    to_far, to_near, depart, total = call(
+    to_near, to_far, depart, total = call(
         take_depart,
-        [half(levels, rim), half(levels, rim), half(levels, points), single(levels, points)],
-        [VMEM] * 4, [VMEM] * 4, [], 4,
+        [half(rows, rim), half(levels, rim), half(levels, points), single(levels, points)],
+        [VMEM] * 4, [VMEM] * 7, [], 4,
         (4 * levels * points, 16 * levels * points),
-        total, other, background, obs_precision,
-    )
-    depart_near, depart_far = exchange(to_far, to_near)
+        inner, other_half(inner, step), outer, other_half(outer, step), background, obs_precision,
+        ensemble,
+    )
+    weighted_near = lax.ppermute(to_near, "tile", near)
+    depart_far = lax.ppermute(to_far, "tile", far)
     full = single(members, levels, points)
     gradient, begun, increment = call(
         backward_local,
@@ -323,12 +336,12 @@
         depart, total, ensemble, control, masked, down,
     )
     gradient = call(
-        backward_edge, full, HBM, [VMEM] * 7 + [HBM],
+        backward_edge, full, HBM, [VMEM] * 6 + [HBM],
         [pltpu.VMEM((2, members, levels, rim), jnp.float32), dma((2,))],
         4,
         (edge_flops, 4 * rows * rim),
-        depart_near, depart_far, ensemble_near, ensemble_far, down, edge, begun, gradient,
-        aliases={7: 0},
+        weighted_near, depart_far, ensemble_far, down, edge, begun, gradient,
+        aliases={6: 0},
     )
     return increment, gradient
 

time: 27.1 us -> 26.6 us (0.982)
  waiting for transfers between devices: 3.22 us -> 1.68 us
  starting transfers between devices: 15.2 us -> 16.1 us
    ppermute x8 -> x9, waiting for transfers between devices: 3.22 us -> 1.68 us  [the longest x1 0.78 us: on_device(): control_right = lax.ppermute(sends[1], 'tile', before)]
    ppermute x8 -> x9, starting transfers between devices: 15.2 us -> 16.1 us  [the longest x1 3.79 us: on_device(): ensemble_far = lax.ppermute(to_far, 'tile', far)]
  transfers between devices with their start and end apart: 8 -> 9, of which waited for: 3 -> 3; matrix products, arithmetic and copies ran while one was open for 0% -> 0% of each run, Pallas kernels for 18% -> 21%
where the time goes in v4:
time: 26.6 us; the launch traced here: 26.5 us
  starting transfers between devices  16.1 us (61%)
  Pallas kernels  7.79 us (29%)
  waiting for transfers between devices  1.68 us (6%)
  between operations  0.79 us (3%)
    pallas_call x7, Pallas kernels, call(): pl.pallas_call(kernel, out_shape=outs, in_specs=in_specs, out_specs=out_s...  7.79 us
    ppermute x1, starting transfers between devices, on_device(): ensemble_far = lax.ppermute(to_far, 'tile', far)  3.79 us
    ppermute x1, starting transfers between devices, on_device(): depart_far = lax.ppermute(to_far, 'tile', far)  3.3 us
    ppermute x1, starting transfers between devices, on_device(): control_right = lax.ppermute(sends[1], 'tile', before)  3.1 us
    ppermute x1, starting transfers between devices, on_device(): control_left = lax.ppermute(sends[0], 'tile', after)  3.02 us
    ppermute x4, starting transfers between devices, other_half(): return lax.ppermute(value, 'mem', [(i, i ^ step) for i in range(group)])  2.84 us
    ppermute x1, waiting for transfers between devices, on_device(): control_right = lax.ppermute(sends[1], 'tile', before)  0.78 us
    ppermute x1, waiting for transfers between devices, on_device(): depart_far = lax.ppermute(to_far, 'tile', far)  0.58 us
  transfers between devices with their start and end apart: 9, of which 3 were waited for; matrix products, arithmetic and copies ran while one was open for 0% of the time, Pallas kernels for 21%

profile of v4, /device:TPU:0, one launch (start us, length us, event | category | flops | bytes accessed | tf_op | source)
XLA Modules:
  0.0 26.5 jit_solution(8319663961009703015)
XLA Ops:
  0.6 1.0 %shard_map.87 = (bf16[8,16,384]{2,1,0:T(8,128)(2,1)S(1)}, bf16[8,16,384]{2,1,0:T(8,128)(2,1)S(1)}) custom-call(bf16[8,16,3072]{2,1,0:T(8,128)(2,1)} %control_ref.3), custom_call_target="tpu_custom_call" | custom-call | bytes 393216 | tf_op jit(solution)/shard_map/pallas_call | solution.py:232
  1.6 0.0 copy-start
  1.6 0.0 copy-start.1
  1.6 0.0 copy-start.2
  1.6 0.0 copy-start.5
  1.7 0.0 copy-start.3
  1.7 0.0 copy-start.4
  1.7 3.0 %collective-permute-start.2 = (bf16[8,16,384]{2,1,0:T(8,128)(2,1)S(1)}, bf16[8,16,384]{2,1,0:T(8,128)(2,1)S(1)}, u32[]{:S(2)}, u32[]{:S(2)}) collective-permute-start(bf16[8,16,384]{2,1,0:T(8,128)(2,1)S(1)} %get-tuple-element.23), channel_id=1, source_target_pairs={{0,4},{4,8},{8,12},{12,16},{16,20},{20,24},{24,28},{28,0},{1,5},{5... | collective-permute-start | bytes 294920 | tf_op jit(solution)/shard_map/ppermute | solution.py:277
  4.7 3.1 %collective-permute-start.3 = (bf16[8,16,384]{2,1,0:T(8,128)(2,1)S(1)}, bf16[8,16,384]{2,1,0:T(8,128)(2,1)S(1)}, u32[]{:S(2)}, u32[]{:S(2)}) collective-permute-start(bf16[8,16,384]{2,1,0:T(8,128)(2,1)S(1)} %get-tuple-element.24), channel_id=1, source_target_pairs={{4,0},{8,4},{12,8},{16,12},{20,16},{24,20},{28,24},{0,28},{5,1},{9... | collective-permute-start | bytes 294920 | tf_op jit(solution)/shard_map/ppermute | solution.py:278
  7.8 0.0 copy-done
  7.8 0.0 copy-done.1
  7.8 0.0 copy-done.2
  7.8 0.0 copy-done.5
  7.8 2.4 %shard_map.86 = (bf16[16,2304]{1,0:T(8,128)(2,1)S(1)}, f32[16,768]{1,0:T(8,128)S(1)}, bf16[24,7,128,128]{3,2,1,0:T(8,128)(2,1)S(1)}, bf16[128,128]{1,0:T(8,128)(...) custom-call(bf16[16,16]{1,0:T(8,128)(2,1)S(1)} %copy-done.5, ...), custom_call_target="tpu_custom_call" | custom-call | flops 805306368 | bytes 7077888 | tf_op jit(solution)/shard_map/pallas_call | solution.py:232
  10.3 0.1 collective-permute-start
  10.3 0.3 %collective-permute-done.2.left_ref = bf16[8,16,384]{2,1,0:T(8,128)(2,1)S(1)} collective-permute-done((bf16[8,16,384]{2,1,0:T(8,128)(2,1)S(1)}, bf16[8,16,384]{2,1,0:T(8,128)(2,1)S(1)}, u32[]{:S(2)}, u32[]{:S(2)}) %collective-permute-start.2) | collective-permute-done | bytes 98336 | tf_op jit(solution)/shard_map/ppermute | solution.py:277
  10.6 0.8 %collective-permute-done.3.right_ref = bf16[8,16,384]{2,1,0:T(8,128)(2,1)S(1)} collective-permute-done((bf16[8,16,384]{2,1,0:T(8,128)(2,1)S(1)}, bf16[8,16,384]{2,1,0:T(8,128)(2,1)S(1)}, u32[]{:S(2)}, u32[]{:S(2)}) %collective-permute-start.3) | collective-permute-done | bytes 98336 | tf_op jit(solution)/shard_map/ppermute | solution.py:278
  11.4 0.5 %shard_map.89 = bf16[16,768]{1,0:T(8,128)(2,1)S(1)} custom-call(bf16[8,16,384]{2,1,0:T(8,128)(2,1)S(1)} %collective-permute-done.2.left_ref, bf16[8,16,384]{2,1,0:T(8,128)(2,1)S(1)} %collective-permute-done.3.right_ref, bf16[128,128]{1,0:T(8,128)(2,1)S(1)} %get-tuple-element.25.up_ref, bf16[2,384,384]{2,1,0:T(8,128)(2,1)S(1)} %get-tuple-element.26.edge_ref, ...), custom_call_target="tpu_custom_call" | custom-call | flops 100663296 | bytes 196608 | tf_op jit(solution)/shard_map/pallas_call | solution.py:232
  12.0 0.1 collective-permute-start.4
  12.0 0.0 collective-permute-done
  12.1 1.6 %collective-permute-start.1 = (bf16[16,2304]{1,0:T(8,128)(2,1)S(1)}, bf16[16,2304]{1,0:T(8,128)(2,1)S(1)}, u32[]{:S(2)}, u32[]{:S(2)}) collective-permute-start(bf16[16,2304]{1,0:T(8,128)(2,1)S(1)} %add_convert_fusion.inner_ref), channel_id=1, source_target_pairs={{0,2},{1,3},{2,0},{3,1},{4,6},{5,7},{6,4},{7,5},{8,10},{9,11},{10,... | collective-permute-start | bytes 221192 | tf_op jit(solution)/shard_map/ppermute | solution.py:303
  13.6 0.0 collective-permute-done.4
  13.6 1.1 %collective-permute-start.5 = (bf16[16,768]{1,0:T(8,128)(2,1)S(1)}, bf16[16,768]{1,0:T(8,128)(2,1)S(1)}, u32[]{:S(2)}, u32[]{:S(2)}) collective-permute-start(bf16[16,768]{1,0:T(8,128)(2,1)S(1)} %add_convert_fusion.1.outer_ref), channel_id=1, source_target_pairs={{0,2},{1,3},{2,0},{3,1},{4,6},{5,7},{6,4},{7,5},{8,10},{9,11},{10,... | collective-permute-start | bytes 73736 | tf_op jit(solution)/shard_map/ppermute | solution.py:303
  14.8 3.8 %collective-permute-start.8 = (bf16[8,16,384]{2,1,0:T(8,128)(2,1)S(1)}, bf16[8,16,384]{2,1,0:T(8,128)(2,1)S(1)}, u32[]{:S(2)}, u32[]{:S(2)}) collective-permute-start(bf16[8,16,384]{2,1,0:T(8,128)(2,1)S(1)} %get-tuple-element.35), channel_id=1, source_target_pairs={{0,28},{4,8},{8,4},{12,16},{16,12},{20,24},{24,20},{28,0},{1,29},{... | collective-permute-start | bytes 294920 | tf_op jit(solution)/shard_map/ppermute | solution.py:295
  18.6 0.0 collective-permute-done.5.outer_other_ref
  18.6 0.0 collective-permute-done.1.inner_other_ref
  18.6 0.0 copy-done.3
  18.6 0.0 copy-done.4
  18.6 0.1 shard_map.90
  18.7 0.1 collective-permute-start.6
  18.8 3.3 %collective-permute-start.7 = (bf16[16,384]{1,0:T(8,128)(2,1)S(1)}, bf16[16,384]{1,0:T(8,128)(2,1)S(1)}, u32[]{:S(2)}, u32[]{:S(2)}) collective-permute-start(bf16[16,384]{1,0:T(8,128)(2,1)S(1)} %get-tuple-element.34), channel_id=1, source_target_pairs={{0,28},{4,8},{8,4},{12,16},{16,12},{20,24},{24,20},{28,0},{1,29},{... | collective-permute-start | bytes 36872 | tf_op jit(solution)/shard_map/ppermute | solution.py:323
  22.1 2.6 %shard_map.91 = (f32[8,16,3072]{2,1,0:T(8,128)}, f32[2,8,16,384]{3,2,1,0:T(8,128)S(1)}, f32[4,3072]{1,0:T(4,128)}) custom-call(bf16[16,3072]{1,0:T(8,128)(2,1)S(1)} %get-tuple-element.28.depart_ref, f32[16,3072]{1,0:T(8,128)S(1)} %get-tuple-element.29.total_ref, bf16[8,16,3072]{2,1,0:T(8,128)(2,1)S(1)} %copy-done, bf16[8,16,3072]{2,1,0:T(8,128)(2,1)S(1)} %copy-done.1, ...), custom_call_target="tpu_custom_call" | custom-call | flops 805306368 | bytes 1572864 | tf_op jit(solution)/shard_map/pallas_call | solution.py:232
  24.7 0.0 collective-permute-done.8.far_ref
  24.7 0.6 %collective-permute-done.7.depart_ref = bf16[16,384]{1,0:T(8,128)(2,1)S(1)} collective-permute-done((bf16[16,384]{1,0:T(8,128)(2,1)S(1)}, bf16[16,384]{1,0:T(8,128)(2,1)S(1)}, u32[]{:S(2)}, u32[]{:S(2)}) %collective-permute-start.7) | collective-permute-done | bytes 12320 | tf_op jit(solution)/shard_map/ppermute | solution.py:323
  25.2 0.0 collective-permute-done.6.near_ref
  25.2 1.2 %shard_map.92 = f32[8,16,3072]{2,1,0:T(8,128)} custom-call(bf16[128,384]{1,0:T(8,128)(2,1)S(1)} %collective-permute-done.6.near_ref, bf16[16,384]{1,0:T(8,128)(2,1)S(1)} %collective-permute-done.7.depart_ref, bf16[8,16,384]{2,1,0:T(8,128)(2,1)S(1)} %collective-permute-done.8.far_ref, ...), custom_call_target="tpu_custom_call", output_to_operand_aliasing={{}: (6, {})} | custom-call | flops 100663296 | bytes 196608 | tf_op jit(solution)/shard_map/pallas_call | solution.py:232
  (3 shorter events, 0.0 us)
Async XLA Ops:
  1.6 6.2 %copy-start = (bf16[8,16,3072]{2,1,0:T(8,128)(2,1)S(1)}, bf16[8,16,3072]{2,1,0:T(8,128)(2,1)}, u32[]{:S(2)}) copy-start(bf16[8,16,3072]{2,1,0:T(8,128)(2,1)} %ensemble_ref.7) | copy-start | bytes 2359300
  1.6 6.2 %copy-start.1 = (bf16[8,16,3072]{2,1,0:T(8,128)(2,1)S(1)}, bf16[8,16,3072]{2,1,0:T(8,128)(2,1)}, u32[]{:S(2)}) copy-start(bf16[8,16,3072]{2,1,0:T(8,128)(2,1)} %control_ref.3) | copy-start | bytes 2359300
  1.6 6.2 %copy-start.2 = (bf16[24,7,128,128]{3,2,1,0:T(8,128)(2,1)S(1)}, bf16[24,7,128,128]{3,2,1,0:T(8,128)(2,1)}, u32[]{:S(2)}) copy-start(bf16[24,7,128,128]{3,2,1,0:T(8,128)(2,1)} %raw_ref.1) | copy-start | bytes 16515076
  1.6 6.2 %copy-start.5 = (bf16[16,16]{1,0:T(8,128)(2,1)S(1)}, bf16[16,16]{1,0:T(8,128)(2,1)}, u32[]{:S(2)}) copy-start(bf16[16,16]{1,0:T(8,128)(2,1)} %loc_ref.1) | copy-start | bytes 1540
  1.7 16.9 %copy-start.3 = (f32[16,3072]{1,0:T(8,128)S(1)}, f32[16,3072]{1,0:T(8,128)}, u32[]{:S(2)}) copy-start(f32[16,3072]{1,0:T(8,128)} %background_ref.1) | copy-start | bytes 589828
  1.7 16.9 %copy-start.4 = (f32[16,3072]{1,0:T(8,128)S(1)}, f32[16,3072]{1,0:T(8,128)}, u32[]{:S(2)}) copy-start(f32[16,3072]{1,0:T(8,128)} %precision_ref.1) | copy-start | bytes 589828
  1.7 9.0 %collective-permute-start.2 = (bf16[8,16,384]{2,1,0:T(8,128)(2,1)S(1)}, bf16[8,16,384]{2,1,0:T(8,128)(2,1)S(1)}, u32[]{:S(2)}, u32[]{:S(2)}) collective-permute-start(bf16[8,16,384]{2,1,0:T(8,128)(2,1)S(1)} %get-tuple-element.23), channel_id=1, source_target_pairs={{0,4},{4,8},{8,12},{12,16},{16,20},{20,24},{24,28},{28,0},{1,5},{5... | collective-permute-start | bytes 294920 | tf_op jit(solution)/shard_map/ppermute | solution.py:277
  4.7 6.7 %collective-permute-start.3 = (bf16[8,16,384]{2,1,0:T(8,128)(2,1)S(1)}, bf16[8,16,384]{2,1,0:T(8,128)(2,1)S(1)}, u32[]{:S(2)}, u32[]{:S(2)}) collective-permute-start(bf16[8,16,384]{2,1,0:T(8,128)(2,1)S(1)} %get-tuple-element.24), channel_id=1, source_target_pairs={{4,0},{8,4},{12,8},{16,12},{20,16},{24,20},{28,24},{0,28},{5,1},{9... | collective-permute-start | bytes 294920 | tf_op jit(solution)/shard_map/ppermute | solution.py:278
  10.3 1.8 %collective-permute-start = (bf16[16,2304]{1,0:T(8,128)(2,1)S(1)}, bf16[16,2304]{1,0:T(8,128)(2,1)S(1)}, u32[]{:S(2)}, u32[]{:S(2)}) collective-permute-start(bf16[16,2304]{1,0:T(8,128)(2,1)S(1)} %get-tuple-element.20), channel_id=1, source_target_pairs={{0,1},{1,0},{2,3},{3,2},{4,5},{5,4},{6,7},{7,6},{8,9},{9,8},{10,11... | collective-permute-start | bytes 221192 | tf_op jit(solution)/shard_map/ppermute | solution.py:303
  12.0 1.7 %collective-permute-start.4 = (bf16[16,768]{1,0:T(8,128)(2,1)S(1)}, bf16[16,768]{1,0:T(8,128)(2,1)S(1)}, u32[]{:S(2)}, u32[]{:S(2)}) collective-permute-start(bf16[16,768]{1,0:T(8,128)(2,1)S(1)} %shard_map.89), channel_id=1, source_target_pairs={{0,1},{1,0},{2,3},{3,2},{4,5},{5,4},{6,7},{7,6},{8,9},{9,8},{10,11... | collective-permute-start | bytes 73736 | tf_op jit(solution)/shard_map/ppermute | solution.py:303
  12.1 6.5 %collective-permute-start.1 = (bf16[16,2304]{1,0:T(8,128)(2,1)S(1)}, bf16[16,2304]{1,0:T(8,128)(2,1)S(1)}, u32[]{:S(2)}, u32[]{:S(2)}) collective-permute-start(bf16[16,2304]{1,0:T(8,128)(2,1)S(1)} %add_convert_fusion.inner_ref), channel_id=1, source_target_pairs={{0,2},{1,3},{2,0},{3,1},{4,6},{5,7},{6,4},{7,5},{8,10},{9,11},{10,... | collective-permute-start | bytes 221192 | tf_op jit(solution)/shard_map/ppermute | solution.py:303
  13.6 4.9 %collective-permute-start.5 = (bf16[16,768]{1,0:T(8,128)(2,1)S(1)}, bf16[16,768]{1,0:T(8,128)(2,1)S(1)}, u32[]{:S(2)}, u32[]{:S(2)}) collective-permute-start(bf16[16,768]{1,0:T(8,128)(2,1)S(1)} %add_convert_fusion.1.outer_ref), channel_id=1, source_target_pairs={{0,2},{1,3},{2,0},{3,1},{4,6},{5,7},{6,4},{7,5},{8,10},{9,11},{10,... | collective-permute-start | bytes 73736 | tf_op jit(solution)/shard_map/ppermute | solution.py:303
  14.8 9.9 %collective-permute-start.8 = (bf16[8,16,384]{2,1,0:T(8,128)(2,1)S(1)}, bf16[8,16,384]{2,1,0:T(8,128)(2,1)S(1)}, u32[]{:S(2)}, u32[]{:S(2)}) collective-permute-start(bf16[8,16,384]{2,1,0:T(8,128)(2,1)S(1)} %get-tuple-element.35), channel_id=1, source_target_pairs={{0,28},{4,8},{8,4},{12,16},{16,12},{20,24},{24,20},{28,0},{1,29},{... | collective-permute-start | bytes 294920 | tf_op jit(solution)/shard_map/ppermute | solution.py:295
  18.7 6.5 %collective-permute-start.6 = (bf16[128,384]{1,0:T(8,128)(2,1)S(1)}, bf16[128,384]{1,0:T(8,128)(2,1)S(1)}, u32[]{:S(2)}, u32[]{:S(2)}) collective-permute-start(bf16[128,384]{1,0:T(8,128)(2,1)S(1)} %get-tuple-element.33), channel_id=1, source_target_pairs={{0,4},{4,0},{8,12},{12,8},{16,20},{20,16},{24,28},{28,24},{1,5},{5... | collective-permute-start | bytes 294920 | tf_op jit(solution)/shard_map/ppermute | solution.py:322
  18.8 6.5 %collective-permute-start.7 = (bf16[16,384]{1,0:T(8,128)(2,1)S(1)}, bf16[16,384]{1,0:T(8,128)(2,1)S(1)}, u32[]{:S(2)}, u32[]{:S(2)}) collective-permute-start(bf16[16,384]{1,0:T(8,128)(2,1)S(1)} %get-tuple-element.34), channel_id=1, source_target_pairs={{0,28},{4,8},{8,4},{12,16},{16,12},{20,24},{24,20},{28,0},{1,29},{... | collective-permute-start | bytes 36872 | tf_op jit(solution)/shard_map/ppermute | solution.py:323

commit v5 on v4

--- a/solution.py
+++ b/solution.py
@@ -6,15 +6,10 @@
 from jax.sharding import PartitionSpec as P
 
 LOADED = 60 * 2**20
-LANES = 128
 
 
 def slot_of(offset):
     return 2 * offset - 1 if offset > 0 else -2 * offset
-
-
-def even_tile():
-    return 1 - lax.rem(lax.axis_index("tile"), 2)
 
 
 def spread(loc, rows):
@@ -73,7 +68,7 @@
 
 
 def forward_local(loc_ref, mask_hbm, control_ref, ensemble_ref, raw_ref, inner_ref, outer_ref,
-                  blocks_ref, up_ref, down_ref, edge_ref, far_ref, field_ref, mask_ref, sem):
+                  blocks_ref, up_ref, down_ref, edge_ref, last_ref, field_ref, mask_ref, sem):
     members, levels, points = control_ref.shape
     tiles, slots, width, _ = blocks_ref.shape
     rows, reach = members * levels, (slots - 1) // 2
@@ -86,8 +81,7 @@
     field_ref[...] = jnp.dot(
         up, control_ref[...].reshape(rows, points), preferred_element_type=jnp.float32
     ).astype(jnp.bfloat16)
-    at = pl.multiple_of((1 - even_tile()) * (points - rim), LANES)
-    far_ref[...] = ensemble_ref[:, :, pl.ds(at, rim)]
+    last_ref[...] = ensemble_ref[:, :, points - rim :]
     mask_copy.wait()
 
     def masked(tile, slot):
@@ -143,8 +137,8 @@
 
 
 def take_depart(inner_ref, inner_other_ref, outer_ref, outer_other_ref, background_ref,
-                precision_ref, ensemble_ref, near_ref, far_ref, depart_ref, total_ref):
-    rim = far_ref.shape[1]
+                precision_ref, ensemble_ref, last_ref, first_ref, depart_ref, total_ref):
+    rim = last_ref.shape[1]
     points = depart_ref.shape[1]
     inner = inner_ref[...].astype(jnp.float32) + inner_other_ref[...].astype(jnp.float32)
     outer = outer_ref[...].astype(jnp.float32) + outer_other_ref[...].astype(jnp.float32)
@@ -154,32 +148,38 @@
     depart_ref[...] = (precision_ref[...] * (total_ref[...] - background_ref[...])).astype(
         jnp.bfloat16
     )
-    even = even_tile()
-    near = pl.ds(pl.multiple_of(even * (points - rim), LANES), rim)
-    far = pl.ds(pl.multiple_of((1 - even) * (points - rim), LANES), rim)
-    near_ref[...] = weighted(ensemble_ref[:, :, near], depart_ref[:, near])
-    far_ref[...] = depart_ref[:, far]
+    last_ref[...] = depart_ref[:, points - rim :]
+    first_ref[...] = weighted(ensemble_ref[:, :, :rim], depart_ref[:, :rim])
 
 
 def backward_local(depart_ref, total_ref, ensemble_ref, control_ref, blocks_ref, down_ref,
-                   gradient_hbm, edge_ref, increment_ref, field_ref, stage_ref, sems):
+                   gradient_hbm, increment_hbm, edge_ref, field_ref, stage_ref, rows_ref, sems):
     members, levels, points = control_ref.shape
     tiles, slots, width, _ = blocks_ref.shape
     reach = (slots - 1) // 2
+    rim, pairs = reach * width, tiles // 2
+    place, per = lax.axis_index("mem"), rows_ref.shape[0]
+    rows = total_ref[:per]
+    for at in range(per, levels, per):
+        rows = jnp.where(place == at // per, total_ref[at : at + per], rows)
+    rows_ref[...] = rows
+    copies = [pltpu.make_async_copy(rows_ref, increment_hbm, sems.at[pairs])]
+    copies[0].start()
     field_ref[...] = jnp.dot(
         down_ref[...], weighted(ensemble_ref[...], depart_ref[...]),
         preferred_element_type=jnp.float32,
     ).astype(jnp.bfloat16)
-    copies = []
 
     def block_at(tile, slot):
         return blocks_ref[tile, slot]
 
-    for pair in range(tiles // 2):
+    for pair in sorted(range(pairs), key=lambda pair: -min(pair, pairs - 1 - pair)):
         at = 2 * pair * width
-        change = pair_rows(field_ref, block_at, blocks_ref.shape, pair).reshape(members, levels, 2 * width)
+        change = pair_rows(field_ref, block_at, blocks_ref.shape, pair)
         control = control_ref[:, :, at : at + 2 * width].astype(jnp.float32)
-        stage_ref[:, :, at : at + 2 * width] = control + change
+        stage_ref[:, :, at : at + 2 * width] = control + change.reshape(
+            members, levels, 2 * width
+        )
         first, last = max(2 * pair, reach), min(2 * pair + 2, tiles - reach)
         if first < last:
             columns = pl.ds(first * width, (last - first) * width)
@@ -188,35 +188,26 @@
             )
             copy.start()
             copies.append(copy)
-    rim = reach * width
     edge_ref[0] = stage_ref[:, :, :rim]
     edge_ref[1] = stage_ref[:, :, points - rim :]
-    place, per = lax.axis_index("mem"), increment_ref.shape[0]
-    rows = total_ref[:per]
-    for at in range(per, levels, per):
-        rows = jnp.where(place == at // per, total_ref[at : at + per], rows)
-    increment_ref[...] = rows
     for copy in copies:
         copy.wait()
 
 
-def backward_edge(near_ref, depart_ref, far_ref, down_ref, edge_ref, begun_ref, begun_hbm,
+def backward_edge(depart_ref, right_ref, left_ref, down_ref, edge_ref, begun_ref, begun_hbm,
                   gradient_hbm, stage_ref, sems):
-    members, levels, rim = far_ref.shape
-    points = gradient_hbm.shape[2]
-    even = even_tile()
+    members, levels, points = gradient_hbm.shape
+    rim = right_ref.shape[1]
     copies = []
-    for i, (side, value) in enumerate(
-        ((even, near_ref[...]), (1 - even, weighted(far_ref[...], depart_ref[...])))
-    ):
+    for side, value in ((0, weighted(left_ref[...], depart_ref[...])), (1, right_ref[...])):
         lowered = jnp.dot(down_ref[...], value, preferred_element_type=jnp.float32)
         change = jnp.dot(
             lowered.astype(jnp.bfloat16), edge_ref[side], preferred_element_type=jnp.float32
         )
-        stage_ref[i] = begun_ref[side] + change.reshape(members, levels, rim)
-        at = pl.multiple_of(side * (points - rim), LANES)
+        stage_ref[side] = begun_ref[side] + change.reshape(members, levels, rim)
+        columns = pl.ds(side * (points - rim), rim)
         copy = pltpu.make_async_copy(
-            stage_ref.at[i], gradient_hbm.at[:, :, pl.ds(at, rim)], sems.at[i]
+            stage_ref.at[side], gradient_hbm.at[:, :, columns], sems.at[side]
         )
         copy.start()
         copies.append(copy)
@@ -251,9 +242,6 @@
     after = [(i, (i + 1) % ring) for i in range(ring)]
     before = [(j, i) for i, j in after]
 
-    near = [(i, i ^ 1) for i in range(ring)]
-    far = [(i, (i + 1 if i % 2 else i - 1) % ring) for i in range(ring)]
-
     def half(*dims):
         return jax.ShapeDtypeStruct(dims, jnp.bfloat16)
 
@@ -276,7 +264,7 @@
     )
     control_left = lax.ppermute(sends[0], "tile", after)
     control_right = lax.ppermute(sends[1], "tile", before)
-    inner, outer, masked, up, down, edge, to_far = call(
+    inner, outer, masked, up, down, edge, last = call(
         forward_local,
         [
             half(levels, points - 2 * rim), single(levels, 2 * rim), half(*blocks.shape), half(rows, rows), half(rows, rows),
@@ -292,7 +280,7 @@
         (local_flops, blocks.size * 2 + 4 * control.size),
         vertical_loc, in_hbm(edge_mask.T), control, ensemble, blocks,
     )
-    ensemble_far = lax.ppermute(to_far, "tile", far)
+    ensemble_left = lax.ppermute(last, "tile", after)
     outer = call(
         forward_edge, half(levels, 2 * rim), VMEM, [VMEM] * 6, [], 4,
         (edge_flops, 4 * rows * rim),
@@ -311,28 +299,29 @@
             for value in (inner, outer)
         ]
         step *= 2
-    to_near, to_far, depart, total = call(
+    last, first, depart, total = call(
         take_depart,
-        [half(rows, rim), half(levels, rim), half(levels, points), single(levels, points)],
+        [half(levels, rim), half(rows, rim), half(levels, points), single(levels, points)],
         [VMEM] * 4, [VMEM] * 7, [], 4,
         (4 * levels * points, 16 * levels * points),
         inner, other_half(inner, step), outer, other_half(outer, step), background, obs_precision,
         ensemble,
     )
-    weighted_near = lax.ppermute(to_near, "tile", near)
-    depart_far = lax.ppermute(to_far, "tile", far)
+    depart_left = lax.ppermute(last, "tile", after)
+    weighted_right = lax.ppermute(first, "tile", before)
     full = single(members, levels, points)
-    gradient, begun, increment = call(
+    gradient, increment, begun = call(
         backward_local,
-        [full, single(2, members, levels, rim), single(per, points)],
-        [HBM, VMEM, VMEM],
+        [full, single(per, points), single(2, members, levels, rim)],
+        [HBM, HBM, VMEM],
         [VMEM] * 6,
         [
             pltpu.VMEM((rows, points), jnp.bfloat16),
-            pltpu.VMEM((members, levels, points), jnp.float32), dma((tiles // 2,)),
+            pltpu.VMEM((members, levels, points), jnp.float32),
+            pltpu.VMEM((per, points), jnp.float32), dma((tiles // 2 + 1,)),
         ],
         8,
-        (local_flops, 4 * control.size),
+        (16 * local_flops, 4 * control.size),
         depart, total, ensemble, control, masked, down,
     )
     gradient = call(
@@ -340,7 +329,7 @@
         [pltpu.VMEM((2, members, levels, rim), jnp.float32), dma((2,))],
         4,
         (edge_flops, 4 * rows * rim),
-        weighted_near, depart_far, ensemble_far, down, edge, begun, gradient,
+        depart_left, weighted_right, ensemble_left, down, edge, begun, gradient,
         aliases={6: 0},
     )
     return increment, gradient

time: 26.6 us -> 26 us (0.977)
  waiting for transfers between devices: 1.68 us -> 4.15 us
  starting transfers between devices: 16.1 us -> 14 us
  Pallas kernels: 7.79 us -> 6.8 us
    ppermute x4, waiting for transfers between devices: 0.01 us -> 2.45 us  [other_half(): return lax.ppermute(value, 'mem', [(i, i ^ step) for i in range(group)])]
    ppermute x3, starting transfers between devices: 7.16 us -> 5.09 us  [the longest x1 4.41 us: on_device(): weighted_right = lax.ppermute(first, 'tile', before)]
    pallas_call x7, Pallas kernels: 7.79 us -> 6.8 us  [call(): pl.pallas_call(kernel, out_shape=outs, in_specs=in_specs, out_specs=out_s...]
    ppermute x1, waiting for transfers between devices: 0.31 us -> 0.66 us  [on_device(): control_left = lax.ppermute(sends[0], 'tile', after)]
    ppermute x3, waiting for transfers between devices: 0.58 us -> 0.26 us  [the longest x1 0.26 us: on_device(): weighted_right = lax.ppermute(first, 'tile', before)]
  transfers between devices with their start and end apart: 9 -> 9, of which waited for: 3 -> 4; matrix products, arithmetic and copies ran while one was open for 0% -> 0% of each run, Pallas kernels for 21% -> 18%
where the time goes in v5:
time: 26 us; the launch traced here: 25.9 us
  starting transfers between devices  14 us (54%)
  Pallas kernels  6.8 us (26%)
  waiting for transfers between devices  4.15 us (16%)
  between operations  0.78 us (3%)
    pallas_call x7, Pallas kernels, call(): pl.pallas_call(kernel, out_shape=outs, in_specs=in_specs, out_specs=out_s...  6.8 us
    ppermute x1, starting transfers between devices, on_device(): weighted_right = lax.ppermute(first, 'tile', before)  4.41 us
    ppermute x1, starting transfers between devices, on_device(): control_right = lax.ppermute(sends[1], 'tile', before)  3.1 us
    ppermute x1, starting transfers between devices, on_device(): control_left = lax.ppermute(sends[0], 'tile', after)  3.02 us
    ppermute x4, starting transfers between devices, other_half(): return lax.ppermute(value, 'mem', [(i, i ^ step) for i in range(group)])  2.84 us
    ppermute x4, waiting for transfers between devices, other_half(): return lax.ppermute(value, 'mem', [(i, i ^ step) for i in range(group)])  2.45 us
    ppermute x1, waiting for transfers between devices, on_device(): control_right = lax.ppermute(sends[1], 'tile', before)  0.78 us
    ppermute x1, waiting for transfers between devices, on_device(): control_left = lax.ppermute(sends[0], 'tile', after)  0.66 us
  transfers between devices with their start and end apart: 9, of which 4 were waited for; matrix products, arithmetic and copies ran while one was open for 0% of the time, Pallas kernels for 18%

profile of v5, /device:TPU:0, one launch (start us, length us, event | category | flops | bytes accessed | tf_op | source)
XLA Modules:
  0.0 25.9 jit_solution(14247368134403959161)
XLA Ops:
  0.6 1.0 %shard_map.87 = (bf16[8,16,384]{2,1,0:T(8,128)(2,1)S(1)}, bf16[8,16,384]{2,1,0:T(8,128)(2,1)S(1)}) custom-call(bf16[8,16,3072]{2,1,0:T(8,128)(2,1)} %control_ref.3), custom_call_target="tpu_custom_call" | custom-call | bytes 393216 | tf_op jit(solution)/shard_map/pallas_call | solution.py:223
  1.6 0.0 copy-start
  1.6 0.0 copy-start.1
  1.6 0.0 copy-start.2
  1.6 0.0 copy-start.5
  1.7 0.0 copy-start.3
  1.7 0.0 copy-start.4
  1.7 3.0 %collective-permute-start.2 = (bf16[8,16,384]{2,1,0:T(8,128)(2,1)S(1)}, bf16[8,16,384]{2,1,0:T(8,128)(2,1)S(1)}, u32[]{:S(2)}, u32[]{:S(2)}) collective-permute-start(bf16[8,16,384]{2,1,0:T(8,128)(2,1)S(1)} %get-tuple-element.23), channel_id=1, source_target_pairs={{0,4},{4,8},{8,12},{12,16},{16,20},{20,24},{24,28},{28,0},{1,5},{5... | collective-permute-start | bytes 294920 | tf_op jit(solution)/shard_map/ppermute | solution.py:265
  4.7 3.1 %collective-permute-start.3 = (bf16[8,16,384]{2,1,0:T(8,128)(2,1)S(1)}, bf16[8,16,384]{2,1,0:T(8,128)(2,1)S(1)}, u32[]{:S(2)}, u32[]{:S(2)}) collective-permute-start(bf16[8,16,384]{2,1,0:T(8,128)(2,1)S(1)} %get-tuple-element.24), channel_id=1, source_target_pairs={{4,0},{8,4},{12,8},{16,12},{20,16},{24,20},{28,24},{0,28},{5,1},{9... | collective-permute-start | bytes 294920 | tf_op jit(solution)/shard_map/ppermute | solution.py:266
  7.8 0.0 copy-done
  7.8 0.0 copy-done.1
  7.8 0.0 copy-done.2
  7.8 0.0 copy-done.5
  7.8 2.1 %shard_map.86 = (bf16[16,2304]{1,0:T(8,128)(2,1)S(1)}, f32[16,768]{1,0:T(8,128)S(1)}, bf16[24,7,128,128]{3,2,1,0:T(8,128)(2,1)S(1)}, bf16[128,128]{1,0:T(8,128)(...) custom-call(bf16[16,16]{1,0:T(8,128)(2,1)S(1)} %copy-done.5, ...), custom_call_target="tpu_custom_call" | custom-call | flops 805306368 | bytes 7077888 | tf_op jit(solution)/shard_map/pallas_call | solution.py:223
  9.9 0.1 collective-permute-start
  10.0 0.7 %collective-permute-done.2.left_ref = bf16[8,16,384]{2,1,0:T(8,128)(2,1)S(1)} collective-permute-done((bf16[8,16,384]{2,1,0:T(8,128)(2,1)S(1)}, bf16[8,16,384]{2,1,0:T(8,128)(2,1)S(1)}, u32[]{:S(2)}, u32[]{:S(2)}) %collective-permute-start.2) | collective-permute-done | bytes 98336 | tf_op jit(solution)/shard_map/ppermute | solution.py:265
  10.6 0.8 %collective-permute-done.3.right_ref = bf16[8,16,384]{2,1,0:T(8,128)(2,1)S(1)} collective-permute-done((bf16[8,16,384]{2,1,0:T(8,128)(2,1)S(1)}, bf16[8,16,384]{2,1,0:T(8,128)(2,1)S(1)}, u32[]{:S(2)}, u32[]{:S(2)}) %collective-permute-start.3) | collective-permute-done | bytes 98336 | tf_op jit(solution)/shard_map/ppermute | solution.py:266
  11.4 0.5 %shard_map.89 = bf16[16,768]{1,0:T(8,128)(2,1)S(1)} custom-call(bf16[8,16,384]{2,1,0:T(8,128)(2,1)S(1)} %collective-permute-done.2.left_ref, bf16[8,16,384]{2,1,0:T(8,128)(2,1)S(1)} %collective-permute-done.3.right_ref, bf16[128,128]{1,0:T(8,128)(2,1)S(1)} %get-tuple-element.25.up_ref, bf16[2,384,384]{2,1,0:T(8,128)(2,1)S(1)} %get-tuple-element.26.edge_ref, ...), custom_call_target="tpu_custom_call" | custom-call | flops 100663296 | bytes 196608 | tf_op jit(solution)/shard_map/pallas_call | solution.py:223
  12.0 0.1 collective-permute-start.4
  12.0 0.0 collective-permute-done
  12.1 1.6 %collective-permute-start.1 = (bf16[16,2304]{1,0:T(8,128)(2,1)S(1)}, bf16[16,2304]{1,0:T(8,128)(2,1)S(1)}, u32[]{:S(2)}, u32[]{:S(2)}) collective-permute-start(bf16[16,2304]{1,0:T(8,128)(2,1)S(1)} %add_convert_fusion.inner_ref), channel_id=1, source_target_pairs={{0,2},{1,3},{2,0},{3,1},{4,6},{5,7},{6,4},{7,5},{8,10},{9,11},{10,... | collective-permute-start | bytes 221192 | tf_op jit(solution)/shard_map/ppermute | solution.py:291
  13.6 0.0 collective-permute-done.4
  13.6 1.1 %collective-permute-start.5 = (bf16[16,768]{1,0:T(8,128)(2,1)S(1)}, bf16[16,768]{1,0:T(8,128)(2,1)S(1)}, u32[]{:S(2)}, u32[]{:S(2)}) collective-permute-start(bf16[16,768]{1,0:T(8,128)(2,1)S(1)} %add_convert_fusion.1.outer_ref), channel_id=1, source_target_pairs={{0,2},{1,3},{2,0},{3,1},{4,6},{5,7},{6,4},{7,5},{8,10},{9,11},{10,... | collective-permute-start | bytes 73736 | tf_op jit(solution)/shard_map/ppermute | solution.py:291
  14.8 0.3 %collective-permute-start.8 = (bf16[8,16,384]{2,1,0:T(8,128)(2,1)S(1)}, bf16[8,16,384]{2,1,0:T(8,128)(2,1)S(1)}, u32[]{:S(2)}, u32[]{:S(2)}) collective-permute-start(bf16[8,16,384]{2,1,0:T(8,128)(2,1)S(1)} %get-tuple-element.35), channel_id=1, source_target_pairs={{0,4},{4,8},{8,12},{12,16},{16,20},{20,24},{24,28},{28,0},{1,5},{5... | collective-permute-start | bytes 294920 | tf_op jit(solution)/shard_map/ppermute | solution.py:283
  15.1 2.4 %collective-permute-done.5.outer_other_ref = bf16[16,768]{1,0:T(8,128)(2,1)S(1)} collective-permute-done((bf16[16,768]{1,0:T(8,128)(2,1)S(1)}, bf16[16,768]{1,0:T(8,128)(2,1)S(1)}, u32[]{:S(2)}, u32[]{:S(2)}) %collective-permute-start.5) | collective-permute-done | bytes 24608 | tf_op jit(solution)/shard_map/ppermute | solution.py:291
  17.5 0.0 collective-permute-done.1.inner_other_ref
  17.5 0.0 copy-done.3
  17.5 0.0 copy-done.4
  17.5 0.1 shard_map.90
  17.6 0.4 %collective-permute-start.6 = (bf16[16,384]{1,0:T(8,128)(2,1)S(1)}, bf16[16,384]{1,0:T(8,128)(2,1)S(1)}, u32[]{:S(2)}, u32[]{:S(2)}) collective-permute-start(bf16[16,384]{1,0:T(8,128)(2,1)S(1)} %get-tuple-element.33), channel_id=1, source_target_pairs={{0,4},{4,8},{8,12},{12,16},{16,20},{20,24},{24,28},{28,0},{1,5},{5... | collective-permute-start | bytes 36872 | tf_op jit(solution)/shard_map/ppermute | solution.py:310
  18.0 4.4 %collective-permute-start.7 = (bf16[128,384]{1,0:T(8,128)(2,1)S(1)}, bf16[128,384]{1,0:T(8,128)(2,1)S(1)}, u32[]{:S(2)}, u32[]{:S(2)}) collective-permute-start(bf16[128,384]{1,0:T(8,128)(2,1)S(1)} %get-tuple-element.34), channel_id=1, source_target_pairs={{4,0},{8,4},{12,8},{16,12},{20,16},{24,20},{28,24},{0,28},{5,1},{9... | collective-permute-start | bytes 294920 | tf_op jit(solution)/shard_map/ppermute | solution.py:311
  22.4 1.9 %shard_map.91 = (f32[8,16,3072]{2,1,0:T(8,128)}, f32[4,3072]{1,0:T(4,128)}, f32[2,8,16,384]{3,2,1,0:T(8,128)S(1)}) custom-call(bf16[16,3072]{1,0:T(8,128)(2,1)S(1)} %get-tuple-element.28.depart_ref, f32[16,3072]{1,0:T(8,128)S(1)} %get-tuple-element.29.total_ref, bf16[8,16,3072]{2,1,0:T(8,128)(2,1)S(1)} %copy-done, bf16[8,16,3072]{2,1,0:T(8,128)(2,1)S(1)} %copy-done.2, ...), custom_call_target="tpu_custom_call" | custom-call | flops 12884901888 | bytes 1572864 | tf_op jit(solution)/shard_map/pallas_call | solution.py:223
  24.4 0.0 collective-permute-done.8.left_ref
  24.4 0.0 collective-permute-done.6.depart_ref
  24.4 0.3 collective-permute-done.7.right_ref
  24.6 1.2 %shard_map.92 = f32[8,16,3072]{2,1,0:T(8,128)} custom-call(bf16[16,384]{1,0:T(8,128)(2,1)S(1)} %collective-permute-done.6.depart_ref, bf16[128,384]{1,0:T(8,128)(2,1)S(1)} %collective-permute-done.7.right_ref, bf16[8,16,384]{2,1,0:T(8,128)(2,1)S(1)} %collective-permute-done.8.left_ref, ...), custom_call_target="tpu_custom_call", output_to_operand_aliasing={{}: (6, {})} | custom-call | flops 100663296 | bytes 196608 | tf_op jit(solution)/shard_map/pallas_call | solution.py:223
  (3 shorter events, 0.0 us)
Async XLA Ops:
  1.6 6.2 %copy-start = (bf16[8,16,3072]{2,1,0:T(8,128)(2,1)S(1)}, bf16[8,16,3072]{2,1,0:T(8,128)(2,1)}, u32[]{:S(2)}) copy-start(bf16[8,16,3072]{2,1,0:T(8,128)(2,1)} %ensemble_ref.7) | copy-start | bytes 2359300
  1.6 6.2 %copy-start.1 = (bf16[24,7,128,128]{3,2,1,0:T(8,128)(2,1)S(1)}, bf16[24,7,128,128]{3,2,1,0:T(8,128)(2,1)}, u32[]{:S(2)}) copy-start(bf16[24,7,128,128]{3,2,1,0:T(8,128)(2,1)} %raw_ref.1) | copy-start | bytes 16515076
  1.6 6.2 %copy-start.2 = (bf16[8,16,3072]{2,1,0:T(8,128)(2,1)S(1)}, bf16[8,16,3072]{2,1,0:T(8,128)(2,1)}, u32[]{:S(2)}) copy-start(bf16[8,16,3072]{2,1,0:T(8,128)(2,1)} %control_ref.3) | copy-start | bytes 2359300
  1.6 6.2 %copy-start.5 = (bf16[16,16]{1,0:T(8,128)(2,1)S(1)}, bf16[16,16]{1,0:T(8,128)(2,1)}, u32[]{:S(2)}) copy-start(bf16[16,16]{1,0:T(8,128)(2,1)} %loc_ref.1) | copy-start | bytes 1540
  1.7 15.9 %copy-start.3 = (f32[16,3072]{1,0:T(8,128)S(1)}, f32[16,3072]{1,0:T(8,128)}, u32[]{:S(2)}) copy-start(f32[16,3072]{1,0:T(8,128)} %background_ref.1) | copy-start | bytes 589828
  1.7 15.9 %copy-start.4 = (f32[16,3072]{1,0:T(8,128)S(1)}, f32[16,3072]{1,0:T(8,128)}, u32[]{:S(2)}) copy-start(f32[16,3072]{1,0:T(8,128)} %precision_ref.1) | copy-start | bytes 589828
  1.7 9.0 %collective-permute-start.2 = (bf16[8,16,384]{2,1,0:T(8,128)(2,1)S(1)}, bf16[8,16,384]{2,1,0:T(8,128)(2,1)S(1)}, u32[]{:S(2)}, u32[]{:S(2)}) collective-permute-start(bf16[8,16,384]{2,1,0:T(8,128)(2,1)S(1)} %get-tuple-element.23), channel_id=1, source_target_pairs={{0,4},{4,8},{8,12},{12,16},{16,20},{20,24},{24,28},{28,0},{1,5},{5... | collective-permute-start | bytes 294920 | tf_op jit(solution)/shard_map/ppermute | solution.py:265
  4.7 6.7 %collective-permute-start.3 = (bf16[8,16,384]{2,1,0:T(8,128)(2,1)S(1)}, bf16[8,16,384]{2,1,0:T(8,128)(2,1)S(1)}, u32[]{:S(2)}, u32[]{:S(2)}) collective-permute-start(bf16[8,16,384]{2,1,0:T(8,128)(2,1)S(1)} %get-tuple-element.24), channel_id=1, source_target_pairs={{4,0},{8,4},{12,8},{16,12},{20,16},{24,20},{28,24},{0,28},{5,1},{9... | collective-permute-start | bytes 294920 | tf_op jit(solution)/shard_map/ppermute | solution.py:266
  9.9 2.1 %collective-permute-start = (bf16[16,2304]{1,0:T(8,128)(2,1)S(1)}, bf16[16,2304]{1,0:T(8,128)(2,1)S(1)}, u32[]{:S(2)}, u32[]{:S(2)}) collective-permute-start(bf16[16,2304]{1,0:T(8,128)(2,1)S(1)} %get-tuple-element.20), channel_id=1, source_target_pairs={{0,1},{1,0},{2,3},{3,2},{4,5},{5,4},{6,7},{7,6},{8,9},{9,8},{10,11... | collective-permute-start | bytes 221192 | tf_op jit(solution)/shard_map/ppermute | solution.py:291
  12.0 1.7 %collective-permute-start.4 = (bf16[16,768]{1,0:T(8,128)(2,1)S(1)}, bf16[16,768]{1,0:T(8,128)(2,1)S(1)}, u32[]{:S(2)}, u32[]{:S(2)}) collective-permute-start(bf16[16,768]{1,0:T(8,128)(2,1)S(1)} %shard_map.89), channel_id=1, source_target_pairs={{0,1},{1,0},{2,3},{3,2},{4,5},{5,4},{6,7},{7,6},{8,9},{9,8},{10,11... | collective-permute-start | bytes 73736 | tf_op jit(solution)/shard_map/ppermute | solution.py:291
  12.1 5.5 %collective-permute-start.1 = (bf16[16,2304]{1,0:T(8,128)(2,1)S(1)}, bf16[16,2304]{1,0:T(8,128)(2,1)S(1)}, u32[]{:S(2)}, u32[]{:S(2)}) collective-permute-start(bf16[16,2304]{1,0:T(8,128)(2,1)S(1)} %add_convert_fusion.inner_ref), channel_id=1, source_target_pairs={{0,2},{1,3},{2,0},{3,1},{4,6},{5,7},{6,4},{7,5},{8,10},{9,11},{10,... | collective-permute-start | bytes 221192 | tf_op jit(solution)/shard_map/ppermute | solution.py:291
  13.6 3.9 %collective-permute-start.5 = (bf16[16,768]{1,0:T(8,128)(2,1)S(1)}, bf16[16,768]{1,0:T(8,128)(2,1)S(1)}, u32[]{:S(2)}, u32[]{:S(2)}) collective-permute-start(bf16[16,768]{1,0:T(8,128)(2,1)S(1)} %add_convert_fusion.1.outer_ref), channel_id=1, source_target_pairs={{0,2},{1,3},{2,0},{3,1},{4,6},{5,7},{6,4},{7,5},{8,10},{9,11},{10,... | collective-permute-start | bytes 73736 | tf_op jit(solution)/shard_map/ppermute | solution.py:291
  14.8 9.6 %collective-permute-start.8 = (bf16[8,16,384]{2,1,0:T(8,128)(2,1)S(1)}, bf16[8,16,384]{2,1,0:T(8,128)(2,1)S(1)}, u32[]{:S(2)}, u32[]{:S(2)}) collective-permute-start(bf16[8,16,384]{2,1,0:T(8,128)(2,1)S(1)} %get-tuple-element.35), channel_id=1, source_target_pairs={{0,4},{4,8},{8,12},{12,16},{16,20},{20,24},{24,28},{28,0},{1,5},{5... | collective-permute-start | bytes 294920 | tf_op jit(solution)/shard_map/ppermute | solution.py:283
  17.6 6.7 %collective-permute-start.6 = (bf16[16,384]{1,0:T(8,128)(2,1)S(1)}, bf16[16,384]{1,0:T(8,128)(2,1)S(1)}, u32[]{:S(2)}, u32[]{:S(2)}) collective-permute-start(bf16[16,384]{1,0:T(8,128)(2,1)S(1)} %get-tuple-element.33), channel_id=1, source_target_pairs={{0,4},{4,8},{8,12},{12,16},{16,20},{20,24},{24,28},{28,0},{1,5},{5... | collective-permute-start | bytes 36872 | tf_op jit(solution)/shard_map/ppermute | solution.py:310
  18.0 6.6 %collective-permute-start.7 = (bf16[128,384]{1,0:T(8,128)(2,1)S(1)}, bf16[128,384]{1,0:T(8,128)(2,1)S(1)}, u32[]{:S(2)}, u32[]{:S(2)}) collective-permute-start(bf16[128,384]{1,0:T(8,128)(2,1)S(1)} %get-tuple-element.34), channel_id=1, source_target_pairs={{4,0},{8,4},{12,8},{16,12},{20,16},{24,20},{28,24},{0,28},{5,1},{9... | collective-permute-start | bytes 294920 | tf_op jit(solution)/shard_map/ppermute | solution.py:311

commit v6 on v5

--- a/solution.py
+++ b/solution.py
@@ -136,28 +136,43 @@
     return product.astype(jnp.bfloat16).reshape(members * levels, points)
 
 
-def take_depart(inner_ref, inner_other_ref, outer_ref, outer_other_ref, background_ref,
-                precision_ref, ensemble_ref, last_ref, first_ref, depart_ref, total_ref):
-    rim = last_ref.shape[1]
-    points = depart_ref.shape[1]
-    inner = inner_ref[...].astype(jnp.float32) + inner_other_ref[...].astype(jnp.float32)
-    outer = outer_ref[...].astype(jnp.float32) + outer_other_ref[...].astype(jnp.float32)
-    total_ref[:, :rim] = outer[:, :rim]
-    total_ref[:, rim : points - rim] = inner
-    total_ref[:, points - rim :] = outer[:, rim:]
-    depart_ref[...] = (precision_ref[...] * (total_ref[...] - background_ref[...])).astype(
-        jnp.bfloat16
-    )
-    last_ref[...] = depart_ref[:, points - rim :]
-    first_ref[...] = weighted(ensemble_ref[:, :, :rim], depart_ref[:, :rim])
-
-
-def backward_local(depart_ref, total_ref, ensemble_ref, control_ref, blocks_ref, down_ref,
-                   gradient_hbm, increment_hbm, edge_ref, field_ref, stage_ref, rows_ref, sems):
+def fold_inner(mine_ref, other_ref, last_ref, sum_ref, last_out):
+    total = mine_ref[...].astype(jnp.float32) + other_ref[...].astype(jnp.float32)
+    sum_ref[...] = total.astype(jnp.bfloat16)
+
+
+def depart_at(total, background_ref, precision_ref, columns):
+    departed = precision_ref[:, columns] * (total - background_ref[:, columns])
+    return departed.astype(jnp.bfloat16)
+
+
+def take_outer(mine_ref, other_ref, background_ref, precision_ref, ensemble_ref, last_ref,
+               first_ref, total_ref, depart_ref):
+    rim, points = last_ref.shape[1], background_ref.shape[1]
+    total = mine_ref[...].astype(jnp.float32) + other_ref[...].astype(jnp.float32)
+    total_ref[...] = total
+    first = depart_at(total[:, :rim], background_ref, precision_ref, slice(0, rim))
+    last = depart_at(total[:, rim:], background_ref, precision_ref, slice(points - rim, points))
+    depart_ref[:, :rim] = first
+    depart_ref[:, rim:] = last
+    last_ref[...] = last
+    first_ref[...] = weighted(ensemble_ref[:, :, :rim], first)
+
+
+def backward_local(outer_total_ref, outer_depart_ref, background_ref, precision_ref, inner_ref,
+                   inner_other_ref, ensemble_ref, control_ref, blocks_ref, down_ref,
+                   gradient_hbm, increment_hbm, edge_ref, field_ref, stage_ref, total_ref,
+                   rows_ref, sems):
     members, levels, points = control_ref.shape
     tiles, slots, width, _ = blocks_ref.shape
     reach = (slots - 1) // 2
     rim, pairs = reach * width, tiles // 2
+    inner = inner_ref[...].astype(jnp.float32) + inner_other_ref[...].astype(jnp.float32)
+    total_ref[:, :rim] = outer_total_ref[:, :rim]
+    total_ref[:, rim : points - rim] = inner
+    total_ref[:, points - rim :] = outer_total_ref[:, rim:]
+    depart = depart_at(inner, background_ref, precision_ref, slice(rim, points - rim))
+    depart = jnp.concatenate([outer_depart_ref[:, :rim], depart, outer_depart_ref[:, rim:]], axis=1)
     place, per = lax.axis_index("mem"), rows_ref.shape[0]
     rows = total_ref[:per]
     for at in range(per, levels, per):
@@ -166,8 +181,7 @@
     copies = [pltpu.make_async_copy(rows_ref, increment_hbm, sems.at[pairs])]
     copies[0].start()
     field_ref[...] = jnp.dot(
-        down_ref[...], weighted(ensemble_ref[...], depart_ref[...]),
-        preferred_element_type=jnp.float32,
+        down_ref[...], weighted(ensemble_ref[...], depart), preferred_element_type=jnp.float32
     ).astype(jnp.bfloat16)
 
     def block_at(tile, slot):
@@ -280,7 +294,6 @@
         (local_flops, blocks.size * 2 + 4 * control.size),
         vertical_loc, in_hbm(edge_mask.T), control, ensemble, blocks,
     )
-    ensemble_left = lax.ppermute(last, "tile", after)
     outer = call(
         forward_edge, half(levels, 2 * rim), VMEM, [VMEM] * 6, [], 4,
         (edge_flops, 4 * rows * rim),
@@ -292,20 +305,21 @@
 
     step = 1
     while 2 * step < group:
-        inner, outer = [
-            (value.astype(jnp.float32) + other_half(value, step).astype(jnp.float32)).astype(
-                jnp.bfloat16
-            )
-            for value in (inner, outer)
-        ]
+        outer_other, inner_other = other_half(outer, step), other_half(inner, step)
+        outer = (outer.astype(jnp.float32) + outer_other.astype(jnp.float32)).astype(jnp.bfloat16)
+        inner, last = call(
+            fold_inner, [half(*inner.shape), half(*last.shape)], [VMEM] * 2, [VMEM] * 3, [], 2,
+            (levels * points, 6 * levels * points), inner, inner_other, last, aliases={2: 1},
+        )
         step *= 2
-    last, first, depart, total = call(
-        take_depart,
-        [half(levels, rim), half(rows, rim), half(levels, points), single(levels, points)],
-        [VMEM] * 4, [VMEM] * 7, [], 4,
-        (4 * levels * points, 16 * levels * points),
-        inner, other_half(inner, step), outer, other_half(outer, step), background, obs_precision,
-        ensemble,
+    ensemble_left = lax.ppermute(last, "tile", after)
+    outer_other, inner_other = other_half(outer, step), other_half(inner, step)
+    last, first, outer, outer_depart = call(
+        take_outer,
+        [half(levels, rim), half(rows, rim), single(levels, 2 * rim), half(levels, 2 * rim)],
+        [VMEM] * 4, [VMEM] * 5, [], 4,
+        (1 * local_flops, 32 * levels * rim),
+        outer, outer_other, background, obs_precision, ensemble,
     )
     depart_left = lax.ppermute(last, "tile", after)
     weighted_right = lax.ppermute(first, "tile", before)
@@ -314,15 +328,17 @@
         backward_local,
         [full, single(per, points), single(2, members, levels, rim)],
         [HBM, HBM, VMEM],
-        [VMEM] * 6,
+        [VMEM] * 10,
         [
             pltpu.VMEM((rows, points), jnp.bfloat16),
             pltpu.VMEM((members, levels, points), jnp.float32),
+            pltpu.VMEM((levels, points), jnp.float32),
             pltpu.VMEM((per, points), jnp.float32), dma((tiles // 2 + 1,)),
         ],
         8,
-        (16 * local_flops, 4 * control.size),
-        depart, total, ensemble, control, masked, down,
+        (4 * local_flops, 4 * control.size),
+        outer, outer_depart, background, obs_precision, inner, inner_other, ensemble, control,
+        masked, down,
     )
     gradient = call(
         backward_edge, full, HBM, [VMEM] * 6 + [HBM],

time: 26 us -> 25.6 us (0.985)
  waiting for transfers between devices: 4.15 us -> 3.86 us
    ppermute x4, waiting for transfers between devices: 2.45 us -> 2.08 us  [other_half(): return lax.ppermute(value, 'mem', [(i, i ^ step) for i in range(group)])]
    ppermute x1, starting transfers between devices: 4.41 us -> 4.08 us  [on_device(): weighted_right = lax.ppermute(first, 'tile', before)]
    ppermute x1, starting transfers between devices: 0.37 us -> 0.69 us  [on_device(): depart_left = lax.ppermute(last, 'tile', after)]
    pallas_call x7 -> x8, Pallas kernels: 6.8 us -> 6.77 us  [call(): pl.pallas_call(kernel, out_shape=outs, in_specs=in_specs, out_specs=out_s...]
  transfers between devices with their start and end apart: 9 -> 9, of which waited for: 4 -> 5; matrix products, arithmetic and copies ran while one was open for 0% -> 0% of each run, Pallas kernels for 18% -> 16%
where the time goes in v6:
time: 25.6 us; the launch traced here: 25.4 us
  starting transfers between devices  13.9 us (54%)
  Pallas kernels  6.77 us (26%)
  waiting for transfers between devices  3.86 us (15%)
  between operations  0.76 us (3%)
    pallas_call x8, Pallas kernels, call(): pl.pallas_call(kernel, out_shape=outs, in_specs=in_specs, out_specs=out_s...  6.77 us
    ppermute x1, starting transfers between devices, on_device(): weighted_right = lax.ppermute(first, 'tile', before)  4.08 us
    ppermute x1, starting transfers between devices, on_device(): control_right = lax.ppermute(sends[1], 'tile', before)  3.1 us
    ppermute x1, starting transfers between devices, on_device(): control_left = lax.ppermute(sends[0], 'tile', after)  3.02 us
    ppermute x4, starting transfers between devices, other_half(): return lax.ppermute(value, 'mem', [(i, i ^ step) for i in range(group)])  2.72 us
    ppermute x4, waiting for transfers between devices, other_half(): return lax.ppermute(value, 'mem', [(i, i ^ step) for i in range(group)])  2.08 us
    ppermute x1, waiting for transfers between devices, on_device(): control_right = lax.ppermute(sends[1], 'tile', before)  0.78 us
    ppermute x1, waiting for transfers between devices, on_device(): control_left = lax.ppermute(sends[0], 'tile', after)  0.74 us
  transfers between devices with their start and end apart: 9, of which 5 were waited for; matrix products, arithmetic and copies ran while one was open for 0% of the time, Pallas kernels for 16%

profile of v6, /device:TPU:0, one launch (start us, length us, event | category | flops | bytes accessed | tf_op | source)
XLA Modules:
  0.0 25.4 jit_solution(7704906549202131049)
XLA Ops:
  0.6 1.0 %shard_map.86 = (bf16[8,16,384]{2,1,0:T(8,128)(2,1)S(1)}, bf16[8,16,384]{2,1,0:T(8,128)(2,1)S(1)}) custom-call(bf16[8,16,3072]{2,1,0:T(8,128)(2,1)} %control_ref.3), custom_call_target="tpu_custom_call" | custom-call | bytes 393216 | tf_op jit(solution)/shard_map/pallas_call | solution.py:237
  1.6 0.0 copy-start
  1.6 0.0 copy-start.1
  1.6 0.0 copy-start.2
  1.6 0.0 copy-start.3
  1.7 0.0 copy-start.4
  1.7 0.0 copy-start.5
  1.7 3.0 %collective-permute-start = (bf16[8,16,384]{2,1,0:T(8,128)(2,1)S(1)}, bf16[8,16,384]{2,1,0:T(8,128)(2,1)S(1)}, u32[]{:S(2)}, u32[]{:S(2)}) collective-permute-start(bf16[8,16,384]{2,1,0:T(8,128)(2,1)S(1)} %get-tuple-element.24), channel_id=1, source_target_pairs={{0,4},{4,8},{8,12},{12,16},{16,20},{20,24},{24,28},{28,0},{1,5},{5... | collective-permute-start | bytes 294920 | tf_op jit(solution)/shard_map/ppermute | solution.py:279
  4.7 3.1 %collective-permute-start.1 = (bf16[8,16,384]{2,1,0:T(8,128)(2,1)S(1)}, bf16[8,16,384]{2,1,0:T(8,128)(2,1)S(1)}, u32[]{:S(2)}, u32[]{:S(2)}) collective-permute-start(bf16[8,16,384]{2,1,0:T(8,128)(2,1)S(1)} %get-tuple-element.25), channel_id=1, source_target_pairs={{4,0},{8,4},{12,8},{16,12},{20,16},{24,20},{28,24},{0,28},{5,1},{9... | collective-permute-start | bytes 294920 | tf_op jit(solution)/shard_map/ppermute | solution.py:280
  7.8 0.0 copy-done
  7.8 0.0 copy-done.1
  7.8 0.0 copy-done.2
  7.8 0.0 copy-done.3
  7.8 2.1 %shard_map.88 = (bf16[16,2304]{1,0:T(8,128)(2,1)S(1)}, f32[16,768]{1,0:T(8,128)S(1)}, bf16[24,7,128,128]{3,2,1,0:T(8,128)(2,1)S(1)}, bf16[128,128]{1,0:T(8,128)(...) custom-call(bf16[16,16]{1,0:T(8,128)(2,1)S(1)} %copy-done.3, ...), custom_call_target="tpu_custom_call" | custom-call | flops 805306368 | bytes 7077888 | tf_op jit(solution)/shard_map/pallas_call | solution.py:237
  9.9 0.7 %collective-permute-done.left_ref = bf16[8,16,384]{2,1,0:T(8,128)(2,1)S(1)} collective-permute-done((bf16[8,16,384]{2,1,0:T(8,128)(2,1)S(1)}, bf16[8,16,384]{2,1,0:T(8,128)(2,1)S(1)}, u32[]{:S(2)}, u32[]{:S(2)}) %collective-permute-start) | collective-permute-done | bytes 98336 | tf_op jit(solution)/shard_map/ppermute | solution.py:279
  10.6 0.8 %collective-permute-done.1.right_ref = bf16[8,16,384]{2,1,0:T(8,128)(2,1)S(1)} collective-permute-done((bf16[8,16,384]{2,1,0:T(8,128)(2,1)S(1)}, bf16[8,16,384]{2,1,0:T(8,128)(2,1)S(1)}, u32[]{:S(2)}, u32[]{:S(2)}) %collective-permute-start.1) | collective-permute-done | bytes 98336 | tf_op jit(solution)/shard_map/ppermute | solution.py:280
  11.4 0.5 %shard_map.89 = bf16[16,768]{1,0:T(8,128)(2,1)S(1)} custom-call(bf16[8,16,384]{2,1,0:T(8,128)(2,1)S(1)} %collective-permute-done.left_ref, bf16[8,16,384]{2,1,0:T(8,128)(2,1)S(1)} %collective-permute-done.1.right_ref, bf16[128,128]{1,0:T(8,128)(2,1)S(1)} %get-tuple-element.26.up_ref, bf16[2,384,384]{2,1,0:T(8,128)(2,1)S(1)} %get-tuple-element.27.edge_ref, ...), custom_call_target="tpu_custom_call" | custom-call | flops 100663296 | bytes 196608 | tf_op jit(solution)/shard_map/pallas_call | solution.py:237
  12.0 0.1 collective-permute-start.2
  12.0 0.5 %collective-permute-start.4 = (bf16[16,2304]{1,0:T(8,128)(2,1)S(1)}, bf16[16,2304]{1,0:T(8,128)(2,1)S(1)}, u32[]{:S(2)}, u32[]{:S(2)}) collective-permute-start(bf16[16,2304]{1,0:T(8,128)(2,1)S(1)} %get-tuple-element.31.mine_ref), channel_id=1, source_target_pairs={{0,1},{1,0},{2,3},{3,2},{4,5},{5,4},{6,7},{7,6},{8,9},{9,8},{10,11... | collective-permute-start | bytes 221192 | tf_op jit(solution)/shard_map/ppermute | solution.py:304
  12.5 0.7 %collective-permute-done.2 = bf16[16,768]{1,0:T(8,128)(2,1)S(1)} collective-permute-done((bf16[16,768]{1,0:T(8,128)(2,1)S(1)}, bf16[16,768]{1,0:T(8,128)(2,1)S(1)}, u32[]{:S(2)}, u32[]{:S(2)}) %collective-permute-start.2) | collective-permute-done | bytes 24608 | tf_op jit(solution)/shard_map/ppermute | solution.py:304
  13.2 1.6 %collective-permute-start.3 = (bf16[16,768]{1,0:T(8,128)(2,1)S(1)}, bf16[16,768]{1,0:T(8,128)(2,1)S(1)}, u32[]{:S(2)}, u32[]{:S(2)}) collective-permute-start(bf16[16,768]{1,0:T(8,128)(2,1)S(1)} %add_convert_fusion.mine_ref), channel_id=1, source_target_pairs={{0,2},{1,3},{2,0},{3,1},{4,6},{5,7},{6,4},{7,5},{8,10},{9,11},{10,... | collective-permute-start | bytes 73736 | tf_op jit(solution)/shard_map/ppermute | solution.py:304
  14.8 0.0 collective-permute-done.4.other_ref
  14.8 0.6 %collective-permute-start.5 = (bf16[16,2304]{1,0:T(8,128)(2,1)S(1)}, bf16[16,2304]{1,0:T(8,128)(2,1)S(1)}, u32[]{:S(2)}, u32[]{:S(2)}) collective-permute-start(bf16[16,2304]{1,0:T(8,128)(2,1)S(1)} %get-tuple-element.33.inner_ref), channel_id=1, source_target_pairs={{0,2},{1,3},{2,0},{3,1},{4,6},{5,7},{6,4},{7,5},{8,10},{9,11},{10,... | collective-permute-start | bytes 221192 | tf_op jit(solution)/shard_map/ppermute | solution.py:304
  15.4 0.3 %collective-permute-start.8 = (bf16[8,16,384]{2,1,0:T(8,128)(2,1)S(1)}, bf16[8,16,384]{2,1,0:T(8,128)(2,1)S(1)}, u32[]{:S(2)}, u32[]{:S(2)}) collective-permute-start(bf16[8,16,384]{2,1,0:T(8,128)(2,1)S(1)} %get-tuple-element.39), channel_id=1, source_target_pairs={{0,4},{4,8},{8,12},{12,16},{16,20},{20,24},{24,28},{28,0},{1,5},{5... | collective-permute-start | bytes 294920 | tf_op jit(solution)/shard_map/ppermute | solution.py:315
  15.7 1.4 %collective-permute-done.3.other_ref = bf16[16,768]{1,0:T(8,128)(2,1)S(1)} collective-permute-done((bf16[16,768]{1,0:T(8,128)(2,1)S(1)}, bf16[16,768]{1,0:T(8,128)(2,1)S(1)}, u32[]{:S(2)}, u32[]{:S(2)}) %collective-permute-start.3) | collective-permute-done | bytes 24608 | tf_op jit(solution)/shard_map/ppermute | solution.py:304
  17.1 0.0 copy-done.4
  17.1 0.0 copy-done.5
  17.2 0.7 %collective-permute-start.6 = (bf16[16,384]{1,0:T(8,128)(2,1)S(1)}, bf16[16,384]{1,0:T(8,128)(2,1)S(1)}, u32[]{:S(2)}, u32[]{:S(2)}) collective-permute-start(bf16[16,384]{1,0:T(8,128)(2,1)S(1)} %get-tuple-element.37), channel_id=1, source_target_pairs={{0,4},{4,8},{8,12},{12,16},{16,20},{20,24},{24,28},{28,0},{1,5},{5... | collective-permute-start | bytes 36872 | tf_op jit(solution)/shard_map/ppermute | solution.py:324
  17.9 4.1 %collective-permute-start.7 = (bf16[128,384]{1,0:T(8,128)(2,1)S(1)}, bf16[128,384]{1,0:T(8,128)(2,1)S(1)}, u32[]{:S(2)}, u32[]{:S(2)}) collective-permute-start(bf16[128,384]{1,0:T(8,128)(2,1)S(1)} %get-tuple-element.38), channel_id=1, source_target_pairs={{4,0},{8,4},{12,8},{16,12},{20,16},{24,20},{28,24},{0,28},{5,1},{9... | collective-permute-start | bytes 294920 | tf_op jit(solution)/shard_map/ppermute | solution.py:325
  21.9 0.0 collective-permute-done.5.inner_other_ref
  21.9 1.9 %shard_map.92 = (f32[8,16,3072]{2,1,0:T(8,128)}, f32[4,3072]{1,0:T(4,128)}, f32[2,8,16,384]{3,2,1,0:T(8,128)S(1)}) custom-call(f32[16,768]{1,0:T(8,128)S(1)} %get-tuple-element.29.outer_total_ref, bf16[16,768]{1,0:T(8,128)(2,1)S(1)} %get-tuple-element.30.outer_depart_ref, f32[16,3072]{1,0:T(8,128)S(1)} %copy-done.4, f32[16,3072]{1,0:T(8,128)S(1)} %copy-done.5, ...), custom_call_target="tpu_custom_call" | custom-call | flops 3221225472 | bytes 1572864 | tf_op jit(solution)/shard_map/pallas_call | solution.py:237
  23.9 0.0 collective-permute-done.6.depart_ref
  23.9 0.0 collective-permute-done.8.left_ref
  23.9 0.3 collective-permute-done.7.right_ref
  24.2 1.2 %shard_map.93 = f32[8,16,3072]{2,1,0:T(8,128)} custom-call(bf16[16,384]{1,0:T(8,128)(2,1)S(1)} %collective-permute-done.6.depart_ref, bf16[128,384]{1,0:T(8,128)(2,1)S(1)} %collective-permute-done.7.right_ref, bf16[8,16,384]{2,1,0:T(8,128)(2,1)S(1)} %collective-permute-done.8.left_ref, ...), custom_call_target="tpu_custom_call", output_to_operand_aliasing={{}: (6, {})} | custom-call | flops 100663296 | bytes 196608 | tf_op jit(solution)/shard_map/pallas_call | solution.py:237
  (4 shorter events, 0.1 us)
Async XLA Ops:
  1.6 6.2 %copy-start = (bf16[24,7,128,128]{3,2,1,0:T(8,128)(2,1)S(1)}, bf16[24,7,128,128]{3,2,1,0:T(8,128)(2,1)}, u32[]{:S(2)}) copy-start(bf16[24,7,128,128]{3,2,1,0:T(8,128)(2,1)} %raw_ref.1) | copy-start | bytes 16515076
  1.6 6.2 %copy-start.1 = (bf16[8,16,3072]{2,1,0:T(8,128)(2,1)S(1)}, bf16[8,16,3072]{2,1,0:T(8,128)(2,1)}, u32[]{:S(2)}) copy-start(bf16[8,16,3072]{2,1,0:T(8,128)(2,1)} %control_ref.3) | copy-start | bytes 2359300
  1.6 6.2 %copy-start.2 = (bf16[8,16,3072]{2,1,0:T(8,128)(2,1)S(1)}, bf16[8,16,3072]{2,1,0:T(8,128)(2,1)}, u32[]{:S(2)}) copy-start(bf16[8,16,3072]{2,1,0:T(8,128)(2,1)} %ensemble_ref.7) | copy-start | bytes 2359300
  1.6 6.2 %copy-start.3 = (bf16[16,16]{1,0:T(8,128)(2,1)S(1)}, bf16[16,16]{1,0:T(8,128)(2,1)}, u32[]{:S(2)}) copy-start(bf16[16,16]{1,0:T(8,128)(2,1)} %loc_ref.1) | copy-start | bytes 1540
  1.7 15.5 %copy-start.4 = (f32[16,3072]{1,0:T(8,128)S(1)}, f32[16,3072]{1,0:T(8,128)}, u32[]{:S(2)}) copy-start(f32[16,3072]{1,0:T(8,128)} %background_ref.3) | copy-start | bytes 589828
  1.7 15.5 %copy-start.5 = (f32[16,3072]{1,0:T(8,128)S(1)}, f32[16,3072]{1,0:T(8,128)}, u32[]{:S(2)}) copy-start(f32[16,3072]{1,0:T(8,128)} %precision_ref.3) | copy-start | bytes 589828
  1.7 9.0 %collective-permute-start = (bf16[8,16,384]{2,1,0:T(8,128)(2,1)S(1)}, bf16[8,16,384]{2,1,0:T(8,128)(2,1)S(1)}, u32[]{:S(2)}, u32[]{:S(2)}) collective-permute-start(bf16[8,16,384]{2,1,0:T(8,128)(2,1)S(1)} %get-tuple-element.24), channel_id=1, source_target_pairs={{0,4},{4,8},{8,12},{12,16},{16,20},{20,24},{24,28},{28,0},{1,5},{5... | collective-permute-start | bytes 294920 | tf_op jit(solution)/shard_map/ppermute | solution.py:279
  4.7 6.7 %collective-permute-start.1 = (bf16[8,16,384]{2,1,0:T(8,128)(2,1)S(1)}, bf16[8,16,384]{2,1,0:T(8,128)(2,1)S(1)}, u32[]{:S(2)}, u32[]{:S(2)}) collective-permute-start(bf16[8,16,384]{2,1,0:T(8,128)(2,1)S(1)} %get-tuple-element.25), channel_id=1, source_target_pairs={{4,0},{8,4},{12,8},{16,12},{20,16},{24,20},{28,24},{0,28},{5,1},{9... | collective-permute-start | bytes 294920 | tf_op jit(solution)/shard_map/ppermute | solution.py:280
  12.0 1.3 %collective-permute-start.2 = (bf16[16,768]{1,0:T(8,128)(2,1)S(1)}, bf16[16,768]{1,0:T(8,128)(2,1)S(1)}, u32[]{:S(2)}, u32[]{:S(2)}) collective-permute-start(bf16[16,768]{1,0:T(8,128)(2,1)S(1)} %shard_map.89), channel_id=1, source_target_pairs={{0,1},{1,0},{2,3},{3,2},{4,5},{5,4},{6,7},{7,6},{8,9},{9,8},{10,11... | collective-permute-start | bytes 73736 | tf_op jit(solution)/shard_map/ppermute | solution.py:304
  12.0 2.8 %collective-permute-start.4 = (bf16[16,2304]{1,0:T(8,128)(2,1)S(1)}, bf16[16,2304]{1,0:T(8,128)(2,1)S(1)}, u32[]{:S(2)}, u32[]{:S(2)}) collective-permute-start(bf16[16,2304]{1,0:T(8,128)(2,1)S(1)} %get-tuple-element.31.mine_ref), channel_id=1, source_target_pairs={{0,1},{1,0},{2,3},{3,2},{4,5},{5,4},{6,7},{7,6},{8,9},{9,8},{10,11... | collective-permute-start | bytes 221192 | tf_op jit(solution)/shard_map/ppermute | solution.py:304
  13.2 3.9 %collective-permute-start.3 = (bf16[16,768]{1,0:T(8,128)(2,1)S(1)}, bf16[16,768]{1,0:T(8,128)(2,1)S(1)}, u32[]{:S(2)}, u32[]{:S(2)}) collective-permute-start(bf16[16,768]{1,0:T(8,128)(2,1)S(1)} %add_convert_fusion.mine_ref), channel_id=1, source_target_pairs={{0,2},{1,3},{2,0},{3,1},{4,6},{5,7},{6,4},{7,5},{8,10},{9,11},{10,... | collective-permute-start | bytes 73736 | tf_op jit(solution)/shard_map/ppermute | solution.py:304
  14.8 7.1 %collective-permute-start.5 = (bf16[16,2304]{1,0:T(8,128)(2,1)S(1)}, bf16[16,2304]{1,0:T(8,128)(2,1)S(1)}, u32[]{:S(2)}, u32[]{:S(2)}) collective-permute-start(bf16[16,2304]{1,0:T(8,128)(2,1)S(1)} %get-tuple-element.33.inner_ref), channel_id=1, source_target_pairs={{0,2},{1,3},{2,0},{3,1},{4,6},{5,7},{6,4},{7,5},{8,10},{9,11},{10,... | collective-permute-start | bytes 221192 | tf_op jit(solution)/shard_map/ppermute | solution.py:304
  15.4 8.5 %collective-permute-start.8 = (bf16[8,16,384]{2,1,0:T(8,128)(2,1)S(1)}, bf16[8,16,384]{2,1,0:T(8,128)(2,1)S(1)}, u32[]{:S(2)}, u32[]{:S(2)}) collective-permute-start(bf16[8,16,384]{2,1,0:T(8,128)(2,1)S(1)} %get-tuple-element.39), channel_id=1, source_target_pairs={{0,4},{4,8},{8,12},{12,16},{16,20},{20,24},{24,28},{28,0},{1,5},{5... | collective-permute-start | bytes 294920 | tf_op jit(solution)/shard_map/ppermute | solution.py:315
  17.2 6.7 %collective-permute-start.6 = (bf16[16,384]{1,0:T(8,128)(2,1)S(1)}, bf16[16,384]{1,0:T(8,128)(2,1)S(1)}, u32[]{:S(2)}, u32[]{:S(2)}) collective-permute-start(bf16[16,384]{1,0:T(8,128)(2,1)S(1)} %get-tuple-element.37), channel_id=1, source_target_pairs={{0,4},{4,8},{8,12},{12,16},{16,20},{20,24},{24,28},{28,0},{1,5},{5... | collective-permute-start | bytes 36872 | tf_op jit(solution)/shard_map/ppermute | solution.py:324
  17.9 6.3 %collective-permute-start.7 = (bf16[128,384]{1,0:T(8,128)(2,1)S(1)}, bf16[128,384]{1,0:T(8,128)(2,1)S(1)}, u32[]{:S(2)}, u32[]{:S(2)}) collective-permute-start(bf16[128,384]{1,0:T(8,128)(2,1)S(1)} %get-tuple-element.38), channel_id=1, source_target_pairs={{4,0},{8,4},{12,8},{16,12},{20,16},{24,20},{28,24},{0,28},{5,1},{9... | collective-permute-start | bytes 294920 | tf_op jit(solution)/shard_map/ppermute | solution.py:325

commit v7 on v6

--- a/solution.py
+++ b/solution.py
@@ -68,7 +68,7 @@
 
 
 def forward_local(loc_ref, mask_hbm, control_ref, ensemble_ref, raw_ref, inner_ref, outer_ref,
-                  blocks_ref, up_ref, down_ref, edge_ref, last_ref, field_ref, mask_ref, sem):
+                  blocks_ref, up_ref, down_ref, edge_ref, field_ref, mask_ref, sem):
     members, levels, points = control_ref.shape
     tiles, slots, width, _ = blocks_ref.shape
     rows, reach = members * levels, (slots - 1) // 2
@@ -81,7 +81,6 @@
     field_ref[...] = jnp.dot(
         up, control_ref[...].reshape(rows, points), preferred_element_type=jnp.float32
     ).astype(jnp.bfloat16)
-    last_ref[...] = ensemble_ref[:, :, points - rim :]
     mask_copy.wait()
 
     def masked(tile, slot):
@@ -136,26 +135,21 @@
     return product.astype(jnp.bfloat16).reshape(members * levels, points)
 
 
-def fold_inner(mine_ref, other_ref, last_ref, sum_ref, last_out):
-    total = mine_ref[...].astype(jnp.float32) + other_ref[...].astype(jnp.float32)
-    sum_ref[...] = total.astype(jnp.bfloat16)
-
-
 def depart_at(total, background_ref, precision_ref, columns):
     departed = precision_ref[:, columns] * (total - background_ref[:, columns])
     return departed.astype(jnp.bfloat16)
 
 
-def take_outer(mine_ref, other_ref, background_ref, precision_ref, ensemble_ref, last_ref,
-               first_ref, total_ref, depart_ref):
+def take_outer(background_ref, precision_ref, ensemble_ref, *refs):
+    *part_refs, last_ref, first_ref, total_ref, depart_ref = refs
     rim, points = last_ref.shape[1], background_ref.shape[1]
-    total = mine_ref[...].astype(jnp.float32) + other_ref[...].astype(jnp.float32)
+    total = sum(ref[...].astype(jnp.float32) for ref in part_refs)
     total_ref[...] = total
     first = depart_at(total[:, :rim], background_ref, precision_ref, slice(0, rim))
     last = depart_at(total[:, rim:], background_ref, precision_ref, slice(points - rim, points))
     depart_ref[:, :rim] = first
     depart_ref[:, rim:] = last
-    last_ref[...] = last
+    last_ref[...] = weighted(ensemble_ref[:, :, points - rim :], last)
     first_ref[...] = weighted(ensemble_ref[:, :, :rim], first)
 
 
@@ -208,13 +202,13 @@
         copy.wait()
 
 
-def backward_edge(depart_ref, right_ref, left_ref, down_ref, edge_ref, begun_ref, begun_hbm,
-                  gradient_hbm, stage_ref, sems):
+def backward_edge(left_ref, right_ref, down_ref, edge_ref, begun_ref, begun_hbm, gradient_hbm,
+                  stage_ref, sems):
     members, levels, points = gradient_hbm.shape
     rim = right_ref.shape[1]
     copies = []
-    for side, value in ((0, weighted(left_ref[...], depart_ref[...])), (1, right_ref[...])):
-        lowered = jnp.dot(down_ref[...], value, preferred_element_type=jnp.float32)
+    for side, ref in ((0, left_ref), (1, right_ref)):
+        lowered = jnp.dot(down_ref[...], ref[...], preferred_element_type=jnp.float32)
         change = jnp.dot(
             lowered.astype(jnp.bfloat16), edge_ref[side], preferred_element_type=jnp.float32
         )
@@ -278,13 +272,13 @@
     )
     control_left = lax.ppermute(sends[0], "tile", after)
     control_right = lax.ppermute(sends[1], "tile", before)
-    inner, outer, masked, up, down, edge, last = call(
+    inner, outer, masked, up, down, edge = call(
         forward_local,
         [
             half(levels, points - 2 * rim), single(levels, 2 * rim), half(*blocks.shape), half(rows, rows), half(rows, rows),
-            half(2, rim, rim), half(members, levels, rim),
+            half(2, rim, rim),
         ],
-        [VMEM] * 7,
+        [VMEM] * 6,
         [VMEM, HBM, VMEM, VMEM, VMEM],
         [
             pltpu.VMEM((rows, points), jnp.bfloat16),
@@ -303,25 +297,28 @@
     def other_half(value, step):
         return lax.ppermute(value, "mem", [(i, i ^ step) for i in range(group)])
 
+    def sum_of(parts):
+        return sum(part.astype(jnp.float32) for part in parts).astype(jnp.bfloat16)
+
+    outers, done = [outer], 1
+    while done < group:
+        outer = sum_of(outers)
+        most = min(4, group // done)
+        outers = [outer] + [other_half(outer, done * i) for i in range(1, most)]
+        done *= most
     step = 1
     while 2 * step < group:
-        outer_other, inner_other = other_half(outer, step), other_half(inner, step)
-        outer = (outer.astype(jnp.float32) + outer_other.astype(jnp.float32)).astype(jnp.bfloat16)
-        inner, last = call(
-            fold_inner, [half(*inner.shape), half(*last.shape)], [VMEM] * 2, [VMEM] * 3, [], 2,
-            (levels * points, 6 * levels * points), inner, inner_other, last, aliases={2: 1},
-        )
+        inner = sum_of([inner, other_half(inner, step)])
         step *= 2
-    ensemble_left = lax.ppermute(last, "tile", after)
-    outer_other, inner_other = other_half(outer, step), other_half(inner, step)
+    inner_other = other_half(inner, step)
     last, first, outer, outer_depart = call(
         take_outer,
-        [half(levels, rim), half(rows, rim), single(levels, 2 * rim), half(levels, 2 * rim)],
-        [VMEM] * 4, [VMEM] * 5, [], 4,
+        [half(rows, rim), half(rows, rim), single(levels, 2 * rim), half(levels, 2 * rim)],
+        [VMEM] * 4, [VMEM] * (3 + len(outers)), [], 4,
         (1 * local_flops, 32 * levels * rim),
-        outer, outer_other, background, obs_precision, ensemble,
-    )
-    depart_left = lax.ppermute(last, "tile", after)
+        background, obs_precision, ensemble, *outers,
+    )
+    weighted_left = lax.ppermute(last, "tile", after)
     weighted_right = lax.ppermute(first, "tile", before)
     full = single(members, levels, points)
     gradient, increment, begun = call(
@@ -341,12 +338,12 @@
         masked, down,
     )
     gradient = call(
-        backward_edge, full, HBM, [VMEM] * 6 + [HBM],
+        backward_edge, full, HBM, [VMEM] * 5 + [HBM],
         [pltpu.VMEM((2, members, levels, rim), jnp.float32), dma((2,))],
         4,
         (edge_flops, 4 * rows * rim),
-        depart_left, weighted_right, ensemble_left, down, edge, begun, gradient,
-        aliases={6: 0},
+        weighted_left, weighted_right, down, edge, begun, gradient,
+        aliases={5: 0},
     )
     return increment, gradient
 

time: 25.6 us -> 25.6 us (level)
  starting transfers between devices: 13.9 us -> 14.5 us
  waiting for transfers between devices: 3.86 us -> 3.38 us
    ppermute x4 -> x5, waiting for transfers between devices: 2.08 us -> 0.65 us  [other_half(): return lax.ppermute(value, 'mem', [(i, i ^ step) for i in range(group)])]
    ppermute x2 -> x1, waiting for transfers between devices: 0.01 us -> 1.04 us  [on_device(): weighted_left = lax.ppermute(last, 'tile', after)]
    ppermute x4 -> x5, starting transfers between devices: 2.72 us -> 3.55 us  [other_half(): return lax.ppermute(value, 'mem', [(i, i ^ step) for i in range(group)])]
    ppermute x2 -> x1, starting transfers between devices: 1.01 us -> 0.2 us  [on_device(): weighted_left = lax.ppermute(last, 'tile', after)]
    ppermute x1, starting transfers between devices: 4.08 us -> 4.58 us  [on_device(): weighted_right = lax.ppermute(first, 'tile', before)]
    pallas_call x8 -> x7, Pallas kernels: 6.77 us -> 6.77 us  [call(): pl.pallas_call(kernel, out_shape=outs, in_specs=in_specs, out_specs=out_s...]
  transfers between devices with their start and end apart: 9 -> 9, of which waited for: 5 -> 5; matrix products, arithmetic and copies ran while one was open for 0% -> 0% of each run, Pallas kernels for 16% -> 18%
where the time goes in v7:
time: 25.6 us; the launch traced here: 25.4 us
  starting transfers between devices  14.5 us (57%)
  Pallas kernels  6.77 us (26%)
  waiting for transfers between devices  3.38 us (13%)
  between operations  0.75 us (3%)
    pallas_call x7, Pallas kernels, call(): pl.pallas_call(kernel, out_shape=outs, in_specs=in_specs, out_specs=out_s...  6.77 us
    ppermute x1, starting transfers between devices, on_device(): weighted_right = lax.ppermute(first, 'tile', before)  4.58 us
    ppermute x5, starting transfers between devices, other_half(): return lax.ppermute(value, 'mem', [(i, i ^ step) for i in range(group)])  3.55 us
    ppermute x1, starting transfers between devices, on_device(): control_right = lax.ppermute(sends[1], 'tile', before)  3.1 us
    ppermute x1, starting transfers between devices, on_device(): control_left = lax.ppermute(sends[0], 'tile', after)  3.02 us
    ppermute x1, waiting for transfers between devices, on_device(): weighted_left = lax.ppermute(last, 'tile', after)  1.04 us
    ppermute x1, waiting for transfers between devices, on_device(): control_right = lax.ppermute(sends[1], 'tile', before)  0.78 us
    ppermute x1, waiting for transfers between devices, on_device(): control_left = lax.ppermute(sends[0], 'tile', after)  0.66 us
  transfers between devices with their start and end apart: 9, of which 5 were waited for; matrix products, arithmetic and copies ran while one was open for 0% of the time, Pallas kernels for 18%

profile of v7, /device:TPU:0, one launch (start us, length us, event | category | flops | bytes accessed | tf_op | source)
XLA Modules:
  0.0 25.4 jit_solution(15875286155174175351)
XLA Ops:
  0.6 1.0 %shard_map.86 = (bf16[8,16,384]{2,1,0:T(8,128)(2,1)S(1)}, bf16[8,16,384]{2,1,0:T(8,128)(2,1)S(1)}) custom-call(bf16[8,16,3072]{2,1,0:T(8,128)(2,1)} %control_ref.3), custom_call_target="tpu_custom_call" | custom-call | bytes 393216 | tf_op jit(solution)/shard_map/pallas_call | solution.py:231
  1.6 0.0 copy-start
  1.6 0.0 copy-start.1
  1.6 0.0 copy-start.2
  1.6 0.0 copy-start.3
  1.7 0.0 copy-start.4
  1.7 0.0 copy-start.5
  1.7 3.0 %collective-permute-start = (bf16[8,16,384]{2,1,0:T(8,128)(2,1)S(1)}, bf16[8,16,384]{2,1,0:T(8,128)(2,1)S(1)}, u32[]{:S(2)}, u32[]{:S(2)}) collective-permute-start(bf16[8,16,384]{2,1,0:T(8,128)(2,1)S(1)} %get-tuple-element.21), channel_id=1, source_target_pairs={{0,4},{4,8},{8,12},{12,16},{16,20},{20,24},{24,28},{28,0},{1,5},{5... | collective-permute-start | bytes 294920 | tf_op jit(solution)/shard_map/ppermute | solution.py:273
  4.7 3.1 %collective-permute-start.1 = (bf16[8,16,384]{2,1,0:T(8,128)(2,1)S(1)}, bf16[8,16,384]{2,1,0:T(8,128)(2,1)S(1)}, u32[]{:S(2)}, u32[]{:S(2)}) collective-permute-start(bf16[8,16,384]{2,1,0:T(8,128)(2,1)S(1)} %get-tuple-element.22), channel_id=1, source_target_pairs={{4,0},{8,4},{12,8},{16,12},{20,16},{24,20},{28,24},{0,28},{5,1},{9... | collective-permute-start | bytes 294920 | tf_op jit(solution)/shard_map/ppermute | solution.py:274
  7.8 0.0 copy-done
  7.8 0.0 copy-done.1
  7.8 0.0 copy-done.2
  7.8 0.0 copy-done.3
  7.8 2.1 %shard_map.88 = (bf16[16,2304]{1,0:T(8,128)(2,1)S(1)}, f32[16,768]{1,0:T(8,128)S(1)}, bf16[24,7,128,128]{3,2,1,0:T(8,128)(2,1)S(1)}, bf16[128,128]{1,0:T(8,128)(...) custom-call(bf16[16,16]{1,0:T(8,128)(2,1)S(1)} %copy-done.3, s32[7,24]{1,0:T(8,128)} %bitcast.1, ...), custom_call_target="tpu_custom_call" | custom-call | flops 805306368 | bytes 7077888 | tf_op jit(solution)/shard_map/pallas_call | solution.py:231
  9.9 0.1 collective-permute-start.5
  10.0 0.7 %collective-permute-done.left_ref = bf16[8,16,384]{2,1,0:T(8,128)(2,1)S(1)} collective-permute-done((bf16[8,16,384]{2,1,0:T(8,128)(2,1)S(1)}, bf16[8,16,384]{2,1,0:T(8,128)(2,1)S(1)}, u32[]{:S(2)}, u32[]{:S(2)}) %collective-permute-start) | collective-permute-done | bytes 98336 | tf_op jit(solution)/shard_map/ppermute | solution.py:273
  10.6 0.8 %collective-permute-done.1.right_ref = bf16[8,16,384]{2,1,0:T(8,128)(2,1)S(1)} collective-permute-done((bf16[8,16,384]{2,1,0:T(8,128)(2,1)S(1)}, bf16[8,16,384]{2,1,0:T(8,128)(2,1)S(1)}, u32[]{:S(2)}, u32[]{:S(2)}) %collective-permute-start.1) | collective-permute-done | bytes 98336 | tf_op jit(solution)/shard_map/ppermute | solution.py:274
  11.4 0.5 %shard_map.89.refs_0_ = bf16[16,768]{1,0:T(8,128)(2,1)S(1)} custom-call(bf16[8,16,384]{2,1,0:T(8,128)(2,1)S(1)} %collective-permute-done.left_ref, bf16[8,16,384]{2,1,0:T(8,128)(2,1)S(1)} %collective-permute-done.1.right_ref, bf16[128,128]{1,0:T(8,128)(2,1)S(1)} %get-tuple-element.23.up_ref, bf16[2,384,384]{2,1,0:T(8,128)(2,1)S(1)} %get-tuple-element.24.edge_ref, ...), custom_call_target="tpu_custom_call" | custom-call | flops 100663296 | bytes 196608 | tf_op jit(solution)/shard_map/pallas_call | solution.py:231
  12.0 0.3 %collective-permute-start.4 = (bf16[16,768]{1,0:T(8,128)(2,1)S(1)}, bf16[16,768]{1,0:T(8,128)(2,1)S(1)}, u32[]{:S(2)}, u32[]{:S(2)}) collective-permute-start(bf16[16,768]{1,0:T(8,128)(2,1)S(1)} %shard_map.89.refs_0_), channel_id=1, source_target_pairs={{0,3},{1,2},{2,1},{3,0},{4,7},{5,6},{6,5},{7,4},{8,11},{9,10},{10,... | collective-permute-start | bytes 73736 | tf_op jit(solution)/shard_map/ppermute | solution.py:298
  12.3 1.3 %collective-permute-start.3 = (bf16[16,768]{1,0:T(8,128)(2,1)S(1)}, bf16[16,768]{1,0:T(8,128)(2,1)S(1)}, u32[]{:S(2)}, u32[]{:S(2)}) collective-permute-start(bf16[16,768]{1,0:T(8,128)(2,1)S(1)} %shard_map.89.refs_0_), channel_id=1, source_target_pairs={{0,2},{1,3},{2,0},{3,1},{4,6},{5,7},{6,4},{7,5},{8,10},{9,11},{10,... | collective-permute-start | bytes 73736 | tf_op jit(solution)/shard_map/ppermute | solution.py:298
  13.6 0.3 %collective-permute-start.2 = (bf16[16,768]{1,0:T(8,128)(2,1)S(1)}, bf16[16,768]{1,0:T(8,128)(2,1)S(1)}, u32[]{:S(2)}, u32[]{:S(2)}) collective-permute-start(bf16[16,768]{1,0:T(8,128)(2,1)S(1)} %shard_map.89.refs_0_), channel_id=1, source_target_pairs={{0,1},{1,0},{2,3},{3,2},{4,5},{5,4},{6,7},{7,6},{8,9},{9,8},{10,11... | collective-permute-start | bytes 73736 | tf_op jit(solution)/shard_map/ppermute | solution.py:298
  13.9 0.0 collective-permute-done.5
  13.9 1.6 %collective-permute-start.6 = (bf16[16,2304]{1,0:T(8,128)(2,1)S(1)}, bf16[16,2304]{1,0:T(8,128)(2,1)S(1)}, u32[]{:S(2)}, u32[]{:S(2)}) collective-permute-start(bf16[16,2304]{1,0:T(8,128)(2,1)S(1)} %add_convert_fusion.inner_ref), channel_id=1, source_target_pairs={{0,2},{1,3},{2,0},{3,1},{4,6},{5,7},{6,4},{7,5},{8,10},{9,11},{10,... | collective-permute-start | bytes 221192 | tf_op jit(solution)/shard_map/ppermute | solution.py:298
  15.5 0.0 collective-permute-done.4.refs_3_
  15.5 0.6 %collective-permute-done.3.refs_2_ = bf16[16,768]{1,0:T(8,128)(2,1)S(1)} collective-permute-done((bf16[16,768]{1,0:T(8,128)(2,1)S(1)}, bf16[16,768]{1,0:T(8,128)(2,1)S(1)}, u32[]{:S(2)}, u32[]{:S(2)}) %collective-permute-start.3) | collective-permute-done | bytes 24608 | tf_op jit(solution)/shard_map/ppermute | solution.py:298
  16.1 0.0 collective-permute-done.2.refs_1_
  16.1 0.0 copy-done.4
  16.1 0.0 copy-done.5
  16.1 0.1 shard_map.90
  16.2 0.2 collective-permute-start.7
  16.4 4.6 %collective-permute-start.8 = (bf16[128,384]{1,0:T(8,128)(2,1)S(1)}, bf16[128,384]{1,0:T(8,128)(2,1)S(1)}, u32[]{:S(2)}, u32[]{:S(2)}) collective-permute-start(bf16[128,384]{1,0:T(8,128)(2,1)S(1)} %get-tuple-element.33), channel_id=1, source_target_pairs={{4,0},{8,4},{12,8},{16,12},{20,16},{24,20},{28,24},{0,28},{5,1},{9... | collective-permute-start | bytes 294920 | tf_op jit(solution)/shard_map/ppermute | solution.py:322
  21.0 0.0 collective-permute-done.6.inner_other_ref
  21.0 1.9 %shard_map.91 = (f32[8,16,3072]{2,1,0:T(8,128)}, f32[4,3072]{1,0:T(4,128)}, f32[2,8,16,384]{3,2,1,0:T(8,128)S(1)}) custom-call(f32[16,768]{1,0:T(8,128)S(1)} %get-tuple-element.26.outer_total_ref, bf16[16,768]{1,0:T(8,128)(2,1)S(1)} %get-tuple-element.27.outer_depart_ref, f32[16,3072]{1,0:T(8,128)S(1)} %copy-done.4, f32[16,3072]{1,0:T(8,128)S(1)} %copy-done.5, ...), custom_call_target="tpu_custom_call" | custom-call | flops 3221225472 | bytes 1572864 | tf_op jit(solution)/shard_map/pallas_call | solution.py:231
  22.9 1.0 %collective-permute-done.7.left_ref = bf16[128,384]{1,0:T(8,128)(2,1)S(1)} collective-permute-done((bf16[128,384]{1,0:T(8,128)(2,1)S(1)}, bf16[128,384]{1,0:T(8,128)(2,1)S(1)}, u32[]{:S(2)}, u32[]{:S(2)}) %collective-permute-start.7) | collective-permute-done | bytes 98336 | tf_op jit(solution)/shard_map/ppermute | solution.py:321
  23.9 0.2 collective-permute-done.8.right_ref
  24.2 1.2 %shard_map.92 = f32[8,16,3072]{2,1,0:T(8,128)} custom-call(bf16[128,384]{1,0:T(8,128)(2,1)S(1)} %collective-permute-done.7.left_ref, bf16[128,384]{1,0:T(8,128)(2,1)S(1)} %collective-permute-done.8.right_ref, bf16[128,128]{1,0:T(8,128)(2,1)S(1)} %get-tuple-element.30.down_ref, ...), custom_call_target="tpu_custom_call", output_to_operand_aliasing={{}: (5, {})} | custom-call | flops 100663296 | bytes 196608 | tf_op jit(solution)/shard_map/pallas_call | solution.py:231
  (2 shorter events, 0.0 us)
Async XLA Ops:
  1.6 6.2 %copy-start = (bf16[24,7,128,128]{3,2,1,0:T(8,128)(2,1)S(1)}, bf16[24,7,128,128]{3,2,1,0:T(8,128)(2,1)}, u32[]{:S(2)}) copy-start(bf16[24,7,128,128]{3,2,1,0:T(8,128)(2,1)} %raw_ref.1) | copy-start | bytes 16515076
  1.6 6.2 %copy-start.1 = (bf16[8,16,3072]{2,1,0:T(8,128)(2,1)S(1)}, bf16[8,16,3072]{2,1,0:T(8,128)(2,1)}, u32[]{:S(2)}) copy-start(bf16[8,16,3072]{2,1,0:T(8,128)(2,1)} %ensemble_ref.7) | copy-start | bytes 2359300
  1.6 6.2 %copy-start.2 = (bf16[8,16,3072]{2,1,0:T(8,128)(2,1)S(1)}, bf16[8,16,3072]{2,1,0:T(8,128)(2,1)}, u32[]{:S(2)}) copy-start(bf16[8,16,3072]{2,1,0:T(8,128)(2,1)} %control_ref.3) | copy-start | bytes 2359300
  1.6 6.2 %copy-start.3 = (bf16[16,16]{1,0:T(8,128)(2,1)S(1)}, bf16[16,16]{1,0:T(8,128)(2,1)}, u32[]{:S(2)}) copy-start(bf16[16,16]{1,0:T(8,128)(2,1)} %loc_ref.1) | copy-start | bytes 1540
  1.7 14.5 %copy-start.4 = (f32[16,3072]{1,0:T(8,128)S(1)}, f32[16,3072]{1,0:T(8,128)}, u32[]{:S(2)}) copy-start(f32[16,3072]{1,0:T(8,128)} %background_ref.3) | copy-start | bytes 589828
  1.7 14.4 %copy-start.5 = (f32[16,3072]{1,0:T(8,128)S(1)}, f32[16,3072]{1,0:T(8,128)}, u32[]{:S(2)}) copy-start(f32[16,3072]{1,0:T(8,128)} %precision_ref.3) | copy-start | bytes 589828
  1.7 9.0 %collective-permute-start = (bf16[8,16,384]{2,1,0:T(8,128)(2,1)S(1)}, bf16[8,16,384]{2,1,0:T(8,128)(2,1)S(1)}, u32[]{:S(2)}, u32[]{:S(2)}) collective-permute-start(bf16[8,16,384]{2,1,0:T(8,128)(2,1)S(1)} %get-tuple-element.21), channel_id=1, source_target_pairs={{0,4},{4,8},{8,12},{12,16},{16,20},{20,24},{24,28},{28,0},{1,5},{5... | collective-permute-start | bytes 294920 | tf_op jit(solution)/shard_map/ppermute | solution.py:273
  4.7 6.7 %collective-permute-start.1 = (bf16[8,16,384]{2,1,0:T(8,128)(2,1)S(1)}, bf16[8,16,384]{2,1,0:T(8,128)(2,1)S(1)}, u32[]{:S(2)}, u32[]{:S(2)}) collective-permute-start(bf16[8,16,384]{2,1,0:T(8,128)(2,1)S(1)} %get-tuple-element.22), channel_id=1, source_target_pairs={{4,0},{8,4},{12,8},{16,12},{20,16},{24,20},{28,24},{0,28},{5,1},{9... | collective-permute-start | bytes 294920 | tf_op jit(solution)/shard_map/ppermute | solution.py:274
  9.9 4.0 %collective-permute-start.5 = (bf16[16,2304]{1,0:T(8,128)(2,1)S(1)}, bf16[16,2304]{1,0:T(8,128)(2,1)S(1)}, u32[]{:S(2)}, u32[]{:S(2)}) collective-permute-start(bf16[16,2304]{1,0:T(8,128)(2,1)S(1)} %get-tuple-element.28), channel_id=1, source_target_pairs={{0,1},{1,0},{2,3},{3,2},{4,5},{5,4},{6,7},{7,6},{8,9},{9,8},{10,11... | collective-permute-start | bytes 221192 | tf_op jit(solution)/shard_map/ppermute | solution.py:298
  12.0 3.5 %collective-permute-start.4 = (bf16[16,768]{1,0:T(8,128)(2,1)S(1)}, bf16[16,768]{1,0:T(8,128)(2,1)S(1)}, u32[]{:S(2)}, u32[]{:S(2)}) collective-permute-start(bf16[16,768]{1,0:T(8,128)(2,1)S(1)} %shard_map.89.refs_0_), channel_id=1, source_target_pairs={{0,3},{1,2},{2,1},{3,0},{4,7},{5,6},{6,5},{7,4},{8,11},{9,10},{10,... | collective-permute-start | bytes 73736 | tf_op jit(solution)/shard_map/ppermute | solution.py:298
  12.3 3.8 %collective-permute-start.3 = (bf16[16,768]{1,0:T(8,128)(2,1)S(1)}, bf16[16,768]{1,0:T(8,128)(2,1)S(1)}, u32[]{:S(2)}, u32[]{:S(2)}) collective-permute-start(bf16[16,768]{1,0:T(8,128)(2,1)S(1)} %shard_map.89.refs_0_), channel_id=1, source_target_pairs={{0,2},{1,3},{2,0},{3,1},{4,6},{5,7},{6,4},{7,5},{8,10},{9,11},{10,... | collective-permute-start | bytes 73736 | tf_op jit(solution)/shard_map/ppermute | solution.py:298
  13.6 2.5 %collective-permute-start.2 = (bf16[16,768]{1,0:T(8,128)(2,1)S(1)}, bf16[16,768]{1,0:T(8,128)(2,1)S(1)}, u32[]{:S(2)}, u32[]{:S(2)}) collective-permute-start(bf16[16,768]{1,0:T(8,128)(2,1)S(1)} %shard_map.89.refs_0_), channel_id=1, source_target_pairs={{0,1},{1,0},{2,3},{3,2},{4,5},{5,4},{6,7},{7,6},{8,9},{9,8},{10,11... | collective-permute-start | bytes 73736 | tf_op jit(solution)/shard_map/ppermute | solution.py:298
  13.9 7.1 %collective-permute-start.6 = (bf16[16,2304]{1,0:T(8,128)(2,1)S(1)}, bf16[16,2304]{1,0:T(8,128)(2,1)S(1)}, u32[]{:S(2)}, u32[]{:S(2)}) collective-permute-start(bf16[16,2304]{1,0:T(8,128)(2,1)S(1)} %add_convert_fusion.inner_ref), channel_id=1, source_target_pairs={{0,2},{1,3},{2,0},{3,1},{4,6},{5,7},{6,4},{7,5},{8,10},{9,11},{10,... | collective-permute-start | bytes 221192 | tf_op jit(solution)/shard_map/ppermute | solution.py:298
  16.2 7.8 %collective-permute-start.7 = (bf16[128,384]{1,0:T(8,128)(2,1)S(1)}, bf16[128,384]{1,0:T(8,128)(2,1)S(1)}, u32[]{:S(2)}, u32[]{:S(2)}) collective-permute-start(bf16[128,384]{1,0:T(8,128)(2,1)S(1)} %get-tuple-element.32), channel_id=1, source_target_pairs={{0,4},{4,8},{8,12},{12,16},{16,20},{20,24},{24,28},{28,0},{1,5},{5... | collective-permute-start | bytes 294920 | tf_op jit(solution)/shard_map/ppermute | solution.py:321
  16.4 7.8 %collective-permute-start.8 = (bf16[128,384]{1,0:T(8,128)(2,1)S(1)}, bf16[128,384]{1,0:T(8,128)(2,1)S(1)}, u32[]{:S(2)}, u32[]{:S(2)}) collective-permute-start(bf16[128,384]{1,0:T(8,128)(2,1)S(1)} %get-tuple-element.33), channel_id=1, source_target_pairs={{4,0},{8,4},{12,8},{16,12},{20,16},{24,20},{28,24},{0,28},{5,1},{9... | collective-permute-start | bytes 294920 | tf_op jit(solution)/shard_map/ppermute | solution.py:322

commit v8 on v6

--- a/solution.py
+++ b/solution.py
@@ -212,19 +212,26 @@
                   gradient_hbm, stage_ref, sems):
     members, levels, points = gradient_hbm.shape
     rim = right_ref.shape[1]
+    values = (weighted(left_ref[...], depart_ref[...]), right_ref[...])
+    lowered = [
+        jnp.dot(down_ref[...], value, preferred_element_type=jnp.float32).astype(jnp.bfloat16)
+        for value in values
+    ]
+    changes = [
+        jnp.dot(value, edge_ref[side], preferred_element_type=jnp.float32)
+        for side, value in enumerate(lowered)
+    ]
     copies = []
-    for side, value in ((0, weighted(left_ref[...], depart_ref[...])), (1, right_ref[...])):
-        lowered = jnp.dot(down_ref[...], value, preferred_element_type=jnp.float32)
-        change = jnp.dot(
-            lowered.astype(jnp.bfloat16), edge_ref[side], preferred_element_type=jnp.float32
-        )
+    for side, change in enumerate(changes):
         stage_ref[side] = begun_ref[side] + change.reshape(members, levels, rim)
         columns = pl.ds(side * (points - rim), rim)
-        copy = pltpu.make_async_copy(
-            stage_ref.at[side], gradient_hbm.at[:, :, columns], sems.at[side]
+        copies.append(
+            pltpu.make_async_copy(
+                stage_ref.at[side], gradient_hbm.at[:, :, columns], sems.at[side]
+            )
         )
+    for copy in copies:
         copy.start()
-        copies.append(copy)
     for copy in copies:
         copy.wait()
 

time: 25.6 us -> 25.5 us (level)
  no operation moved by 1% of the time
where the time goes in v8:
time: 25.5 us; the launch traced here: 25.3 us
  starting transfers between devices  13.9 us (55%)
  Pallas kernels  6.73 us (26%)
  waiting for transfers between devices  3.86 us (15%)
  between operations  0.76 us (3%)
    pallas_call x8, Pallas kernels, call(): pl.pallas_call(kernel, out_shape=outs, in_specs=in_specs, out_specs=out_s...  6.73 us
    ppermute x1, starting transfers between devices, on_device(): weighted_right = lax.ppermute(first, 'tile', before)  4.08 us
    ppermute x1, starting transfers between devices, on_device(): control_right = lax.ppermute(sends[1], 'tile', before)  3.1 us
    ppermute x1, starting transfers between devices, on_device(): control_left = lax.ppermute(sends[0], 'tile', after)  3.02 us
    ppermute x4, starting transfers between devices, other_half(): return lax.ppermute(value, 'mem', [(i, i ^ step) for i in range(group)])  2.72 us
    ppermute x4, waiting for transfers between devices, other_half(): return lax.ppermute(value, 'mem', [(i, i ^ step) for i in range(group)])  2.08 us
    ppermute x1, waiting for transfers between devices, on_device(): control_right = lax.ppermute(sends[1], 'tile', before)  0.78 us
    ppermute x1, waiting for transfers between devices, on_device(): control_left = lax.ppermute(sends[0], 'tile', after)  0.74 us
  transfers between devices with their start and end apart: 9, of which 5 were waited for; matrix products, arithmetic and copies ran while one was open for 0% of the time, Pallas kernels for 16%

profile of v8, /device:TPU:0, one launch (start us, length us, event | category | flops | bytes accessed | tf_op | source)
XLA Modules:
  0.0 25.3 jit_solution(10250810879484510488)
XLA Ops:
  0.6 1.0 %shard_map.86 = (bf16[8,16,384]{2,1,0:T(8,128)(2,1)S(1)}, bf16[8,16,384]{2,1,0:T(8,128)(2,1)S(1)}) custom-call(bf16[8,16,3072]{2,1,0:T(8,128)(2,1)} %control_ref.3), custom_call_target="tpu_custom_call" | custom-call | bytes 393216 | tf_op jit(solution)/shard_map/pallas_call | solution.py:244
  1.6 0.0 copy-start
  1.6 0.0 copy-start.1
  1.6 0.0 copy-start.2
  1.6 0.0 copy-start.3
  1.7 0.0 copy-start.4
  1.7 0.0 copy-start.5
  1.7 3.0 %collective-permute-start = (bf16[8,16,384]{2,1,0:T(8,128)(2,1)S(1)}, bf16[8,16,384]{2,1,0:T(8,128)(2,1)S(1)}, u32[]{:S(2)}, u32[]{:S(2)}) collective-permute-start(bf16[8,16,384]{2,1,0:T(8,128)(2,1)S(1)} %get-tuple-element.24), channel_id=1, source_target_pairs={{0,4},{4,8},{8,12},{12,16},{16,20},{20,24},{24,28},{28,0},{1,5},{5... | collective-permute-start | bytes 294920 | tf_op jit(solution)/shard_map/ppermute | solution.py:286
  4.7 3.1 %collective-permute-start.1 = (bf16[8,16,384]{2,1,0:T(8,128)(2,1)S(1)}, bf16[8,16,384]{2,1,0:T(8,128)(2,1)S(1)}, u32[]{:S(2)}, u32[]{:S(2)}) collective-permute-start(bf16[8,16,384]{2,1,0:T(8,128)(2,1)S(1)} %get-tuple-element.25), channel_id=1, source_target_pairs={{4,0},{8,4},{12,8},{16,12},{20,16},{24,20},{28,24},{0,28},{5,1},{9... | collective-permute-start | bytes 294920 | tf_op jit(solution)/shard_map/ppermute | solution.py:287
  7.8 0.0 copy-done
  7.8 0.0 copy-done.1
  7.8 0.0 copy-done.2
  7.8 0.0 copy-done.3
  7.8 2.1 %shard_map.88 = (bf16[16,2304]{1,0:T(8,128)(2,1)S(1)}, f32[16,768]{1,0:T(8,128)S(1)}, bf16[24,7,128,128]{3,2,1,0:T(8,128)(2,1)S(1)}, bf16[128,128]{1,0:T(8,128)(...) custom-call(bf16[16,16]{1,0:T(8,128)(2,1)S(1)} %copy-done.3, ...), custom_call_target="tpu_custom_call" | custom-call | flops 805306368 | bytes 7077888 | tf_op jit(solution)/shard_map/pallas_call | solution.py:244
  9.9 0.7 %collective-permute-done.left_ref = bf16[8,16,384]{2,1,0:T(8,128)(2,1)S(1)} collective-permute-done((bf16[8,16,384]{2,1,0:T(8,128)(2,1)S(1)}, bf16[8,16,384]{2,1,0:T(8,128)(2,1)S(1)}, u32[]{:S(2)}, u32[]{:S(2)}) %collective-permute-start) | collective-permute-done | bytes 98336 | tf_op jit(solution)/shard_map/ppermute | solution.py:286
  10.6 0.8 %collective-permute-done.1.right_ref = bf16[8,16,384]{2,1,0:T(8,128)(2,1)S(1)} collective-permute-done((bf16[8,16,384]{2,1,0:T(8,128)(2,1)S(1)}, bf16[8,16,384]{2,1,0:T(8,128)(2,1)S(1)}, u32[]{:S(2)}, u32[]{:S(2)}) %collective-permute-start.1) | collective-permute-done | bytes 98336 | tf_op jit(solution)/shard_map/ppermute | solution.py:287
  11.4 0.5 %shard_map.89 = bf16[16,768]{1,0:T(8,128)(2,1)S(1)} custom-call(bf16[8,16,384]{2,1,0:T(8,128)(2,1)S(1)} %collective-permute-done.left_ref, bf16[8,16,384]{2,1,0:T(8,128)(2,1)S(1)} %collective-permute-done.1.right_ref, bf16[128,128]{1,0:T(8,128)(2,1)S(1)} %get-tuple-element.26.up_ref, bf16[2,384,384]{2,1,0:T(8,128)(2,1)S(1)} %get-tuple-element.27.edge_ref, ...), custom_call_target="tpu_custom_call" | custom-call | flops 100663296 | bytes 196608 | tf_op jit(solution)/shard_map/pallas_call | solution.py:244
  12.0 0.1 collective-permute-start.2
  12.0 0.5 %collective-permute-start.4 = (bf16[16,2304]{1,0:T(8,128)(2,1)S(1)}, bf16[16,2304]{1,0:T(8,128)(2,1)S(1)}, u32[]{:S(2)}, u32[]{:S(2)}) collective-permute-start(bf16[16,2304]{1,0:T(8,128)(2,1)S(1)} %get-tuple-element.31.mine_ref), channel_id=1, source_target_pairs={{0,1},{1,0},{2,3},{3,2},{4,5},{5,4},{6,7},{7,6},{8,9},{9,8},{10,11... | collective-permute-start | bytes 221192 | tf_op jit(solution)/shard_map/ppermute | solution.py:311
  12.5 0.7 %collective-permute-done.2 = bf16[16,768]{1,0:T(8,128)(2,1)S(1)} collective-permute-done((bf16[16,768]{1,0:T(8,128)(2,1)S(1)}, bf16[16,768]{1,0:T(8,128)(2,1)S(1)}, u32[]{:S(2)}, u32[]{:S(2)}) %collective-permute-start.2) | collective-permute-done | bytes 24608 | tf_op jit(solution)/shard_map/ppermute | solution.py:311
  13.2 1.6 %collective-permute-start.3 = (bf16[16,768]{1,0:T(8,128)(2,1)S(1)}, bf16[16,768]{1,0:T(8,128)(2,1)S(1)}, u32[]{:S(2)}, u32[]{:S(2)}) collective-permute-start(bf16[16,768]{1,0:T(8,128)(2,1)S(1)} %add_convert_fusion.mine_ref), channel_id=1, source_target_pairs={{0,2},{1,3},{2,0},{3,1},{4,6},{5,7},{6,4},{7,5},{8,10},{9,11},{10,... | collective-permute-start | bytes 73736 | tf_op jit(solution)/shard_map/ppermute | solution.py:311
  14.8 0.0 collective-permute-done.4.other_ref
  14.8 0.6 %collective-permute-start.5 = (bf16[16,2304]{1,0:T(8,128)(2,1)S(1)}, bf16[16,2304]{1,0:T(8,128)(2,1)S(1)}, u32[]{:S(2)}, u32[]{:S(2)}) collective-permute-start(bf16[16,2304]{1,0:T(8,128)(2,1)S(1)} %get-tuple-element.33.inner_ref), channel_id=1, source_target_pairs={{0,2},{1,3},{2,0},{3,1},{4,6},{5,7},{6,4},{7,5},{8,10},{9,11},{10,... | collective-permute-start | bytes 221192 | tf_op jit(solution)/shard_map/ppermute | solution.py:311
  15.4 0.3 %collective-permute-start.8 = (bf16[8,16,384]{2,1,0:T(8,128)(2,1)S(1)}, bf16[8,16,384]{2,1,0:T(8,128)(2,1)S(1)}, u32[]{:S(2)}, u32[]{:S(2)}) collective-permute-start(bf16[8,16,384]{2,1,0:T(8,128)(2,1)S(1)} %get-tuple-element.39), channel_id=1, source_target_pairs={{0,4},{4,8},{8,12},{12,16},{16,20},{20,24},{24,28},{28,0},{1,5},{5... | collective-permute-start | bytes 294920 | tf_op jit(solution)/shard_map/ppermute | solution.py:322
  15.7 1.4 %collective-permute-done.3.other_ref = bf16[16,768]{1,0:T(8,128)(2,1)S(1)} collective-permute-done((bf16[16,768]{1,0:T(8,128)(2,1)S(1)}, bf16[16,768]{1,0:T(8,128)(2,1)S(1)}, u32[]{:S(2)}, u32[]{:S(2)}) %collective-permute-start.3) | collective-permute-done | bytes 24608 | tf_op jit(solution)/shard_map/ppermute | solution.py:311
  17.1 0.0 copy-done.4
  17.1 0.0 copy-done.5
  17.2 0.7 %collective-permute-start.6 = (bf16[16,384]{1,0:T(8,128)(2,1)S(1)}, bf16[16,384]{1,0:T(8,128)(2,1)S(1)}, u32[]{:S(2)}, u32[]{:S(2)}) collective-permute-start(bf16[16,384]{1,0:T(8,128)(2,1)S(1)} %get-tuple-element.37), channel_id=1, source_target_pairs={{0,4},{4,8},{8,12},{12,16},{16,20},{20,24},{24,28},{28,0},{1,5},{5... | collective-permute-start | bytes 36872 | tf_op jit(solution)/shard_map/ppermute | solution.py:331
  17.9 4.1 %collective-permute-start.7 = (bf16[128,384]{1,0:T(8,128)(2,1)S(1)}, bf16[128,384]{1,0:T(8,128)(2,1)S(1)}, u32[]{:S(2)}, u32[]{:S(2)}) collective-permute-start(bf16[128,384]{1,0:T(8,128)(2,1)S(1)} %get-tuple-element.38), channel_id=1, source_target_pairs={{4,0},{8,4},{12,8},{16,12},{20,16},{24,20},{28,24},{0,28},{5,1},{9... | collective-permute-start | bytes 294920 | tf_op jit(solution)/shard_map/ppermute | solution.py:332
  21.9 0.0 collective-permute-done.5.inner_other_ref
  21.9 1.9 %shard_map.92 = (f32[8,16,3072]{2,1,0:T(8,128)}, f32[4,3072]{1,0:T(4,128)}, f32[2,8,16,384]{3,2,1,0:T(8,128)S(1)}) custom-call(f32[16,768]{1,0:T(8,128)S(1)} %get-tuple-element.29.outer_total_ref, bf16[16,768]{1,0:T(8,128)(2,1)S(1)} %get-tuple-element.30.outer_depart_ref, f32[16,3072]{1,0:T(8,128)S(1)} %copy-done.4, f32[16,3072]{1,0:T(8,128)S(1)} %copy-done.5, ...), custom_call_target="tpu_custom_call" | custom-call | flops 3221225472 | bytes 1572864 | tf_op jit(solution)/shard_map/pallas_call | solution.py:244
  23.9 0.0 collective-permute-done.6.depart_ref
  23.9 0.0 collective-permute-done.8.left_ref
  23.9 0.3 collective-permute-done.7.right_ref
  24.2 1.2 %shard_map.93 = f32[8,16,3072]{2,1,0:T(8,128)} custom-call(bf16[16,384]{1,0:T(8,128)(2,1)S(1)} %collective-permute-done.6.depart_ref, bf16[128,384]{1,0:T(8,128)(2,1)S(1)} %collective-permute-done.7.right_ref, bf16[8,16,384]{2,1,0:T(8,128)(2,1)S(1)} %collective-permute-done.8.left_ref, ...), custom_call_target="tpu_custom_call", output_to_operand_aliasing={{}: (6, {})} | custom-call | flops 100663296 | bytes 196608 | tf_op jit(solution)/shard_map/pallas_call | solution.py:244
  (4 shorter events, 0.1 us)
Async XLA Ops:
  1.6 6.2 %copy-start = (bf16[24,7,128,128]{3,2,1,0:T(8,128)(2,1)S(1)}, bf16[24,7,128,128]{3,2,1,0:T(8,128)(2,1)}, u32[]{:S(2)}) copy-start(bf16[24,7,128,128]{3,2,1,0:T(8,128)(2,1)} %raw_ref.1) | copy-start | bytes 16515076
  1.6 6.2 %copy-start.1 = (bf16[8,16,3072]{2,1,0:T(8,128)(2,1)S(1)}, bf16[8,16,3072]{2,1,0:T(8,128)(2,1)}, u32[]{:S(2)}) copy-start(bf16[8,16,3072]{2,1,0:T(8,128)(2,1)} %control_ref.3) | copy-start | bytes 2359300
  1.6 6.2 %copy-start.2 = (bf16[8,16,3072]{2,1,0:T(8,128)(2,1)S(1)}, bf16[8,16,3072]{2,1,0:T(8,128)(2,1)}, u32[]{:S(2)}) copy-start(bf16[8,16,3072]{2,1,0:T(8,128)(2,1)} %ensemble_ref.7) | copy-start | bytes 2359300
  1.6 6.2 %copy-start.3 = (bf16[16,16]{1,0:T(8,128)(2,1)S(1)}, bf16[16,16]{1,0:T(8,128)(2,1)}, u32[]{:S(2)}) copy-start(bf16[16,16]{1,0:T(8,128)(2,1)} %loc_ref.1) | copy-start | bytes 1540
  1.7 15.5 %copy-start.4 = (f32[16,3072]{1,0:T(8,128)S(1)}, f32[16,3072]{1,0:T(8,128)}, u32[]{:S(2)}) copy-start(f32[16,3072]{1,0:T(8,128)} %background_ref.3) | copy-start | bytes 589828
  1.7 15.5 %copy-start.5 = (f32[16,3072]{1,0:T(8,128)S(1)}, f32[16,3072]{1,0:T(8,128)}, u32[]{:S(2)}) copy-start(f32[16,3072]{1,0:T(8,128)} %precision_ref.3) | copy-start | bytes 589828
  1.7 9.0 %collective-permute-start = (bf16[8,16,384]{2,1,0:T(8,128)(2,1)S(1)}, bf16[8,16,384]{2,1,0:T(8,128)(2,1)S(1)}, u32[]{:S(2)}, u32[]{:S(2)}) collective-permute-start(bf16[8,16,384]{2,1,0:T(8,128)(2,1)S(1)} %get-tuple-element.24), channel_id=1, source_target_pairs={{0,4},{4,8},{8,12},{12,16},{16,20},{20,24},{24,28},{28,0},{1,5},{5... | collective-permute-start | bytes 294920 | tf_op jit(solution)/shard_map/ppermute | solution.py:286
  4.7 6.7 %collective-permute-start.1 = (bf16[8,16,384]{2,1,0:T(8,128)(2,1)S(1)}, bf16[8,16,384]{2,1,0:T(8,128)(2,1)S(1)}, u32[]{:S(2)}, u32[]{:S(2)}) collective-permute-start(bf16[8,16,384]{2,1,0:T(8,128)(2,1)S(1)} %get-tuple-element.25), channel_id=1, source_target_pairs={{4,0},{8,4},{12,8},{16,12},{20,16},{24,20},{28,24},{0,28},{5,1},{9... | collective-permute-start | bytes 294920 | tf_op jit(solution)/shard_map/ppermute | solution.py:287
  12.0 1.3 %collective-permute-start.2 = (bf16[16,768]{1,0:T(8,128)(2,1)S(1)}, bf16[16,768]{1,0:T(8,128)(2,1)S(1)}, u32[]{:S(2)}, u32[]{:S(2)}) collective-permute-start(bf16[16,768]{1,0:T(8,128)(2,1)S(1)} %shard_map.89), channel_id=1, source_target_pairs={{0,1},{1,0},{2,3},{3,2},{4,5},{5,4},{6,7},{7,6},{8,9},{9,8},{10,11... | collective-permute-start | bytes 73736 | tf_op jit(solution)/shard_map/ppermute | solution.py:311
  12.0 2.8 %collective-permute-start.4 = (bf16[16,2304]{1,0:T(8,128)(2,1)S(1)}, bf16[16,2304]{1,0:T(8,128)(2,1)S(1)}, u32[]{:S(2)}, u32[]{:S(2)}) collective-permute-start(bf16[16,2304]{1,0:T(8,128)(2,1)S(1)} %get-tuple-element.31.mine_ref), channel_id=1, source_target_pairs={{0,1},{1,0},{2,3},{3,2},{4,5},{5,4},{6,7},{7,6},{8,9},{9,8},{10,11... | collective-permute-start | bytes 221192 | tf_op jit(solution)/shard_map/ppermute | solution.py:311
  13.2 3.9 %collective-permute-start.3 = (bf16[16,768]{1,0:T(8,128)(2,1)S(1)}, bf16[16,768]{1,0:T(8,128)(2,1)S(1)}, u32[]{:S(2)}, u32[]{:S(2)}) collective-permute-start(bf16[16,768]{1,0:T(8,128)(2,1)S(1)} %add_convert_fusion.mine_ref), channel_id=1, source_target_pairs={{0,2},{1,3},{2,0},{3,1},{4,6},{5,7},{6,4},{7,5},{8,10},{9,11},{10,... | collective-permute-start | bytes 73736 | tf_op jit(solution)/shard_map/ppermute | solution.py:311
  14.8 7.1 %collective-permute-start.5 = (bf16[16,2304]{1,0:T(8,128)(2,1)S(1)}, bf16[16,2304]{1,0:T(8,128)(2,1)S(1)}, u32[]{:S(2)}, u32[]{:S(2)}) collective-permute-start(bf16[16,2304]{1,0:T(8,128)(2,1)S(1)} %get-tuple-element.33.inner_ref), channel_id=1, source_target_pairs={{0,2},{1,3},{2,0},{3,1},{4,6},{5,7},{6,4},{7,5},{8,10},{9,11},{10,... | collective-permute-start | bytes 221192 | tf_op jit(solution)/shard_map/ppermute | solution.py:311
  15.4 8.5 %collective-permute-start.8 = (bf16[8,16,384]{2,1,0:T(8,128)(2,1)S(1)}, bf16[8,16,384]{2,1,0:T(8,128)(2,1)S(1)}, u32[]{:S(2)}, u32[]{:S(2)}) collective-permute-start(bf16[8,16,384]{2,1,0:T(8,128)(2,1)S(1)} %get-tuple-element.39), channel_id=1, source_target_pairs={{0,4},{4,8},{8,12},{12,16},{16,20},{20,24},{24,28},{28,0},{1,5},{5... | collective-permute-start | bytes 294920 | tf_op jit(solution)/shard_map/ppermute | solution.py:322
  17.2 6.7 %collective-permute-start.6 = (bf16[16,384]{1,0:T(8,128)(2,1)S(1)}, bf16[16,384]{1,0:T(8,128)(2,1)S(1)}, u32[]{:S(2)}, u32[]{:S(2)}) collective-permute-start(bf16[16,384]{1,0:T(8,128)(2,1)S(1)} %get-tuple-element.37), channel_id=1, source_target_pairs={{0,4},{4,8},{8,12},{12,16},{16,20},{20,24},{24,28},{28,0},{1,5},{5... | collective-permute-start | bytes 36872 | tf_op jit(solution)/shard_map/ppermute | solution.py:331
  17.9 6.3 %collective-permute-start.7 = (bf16[128,384]{1,0:T(8,128)(2,1)S(1)}, bf16[128,384]{1,0:T(8,128)(2,1)S(1)}, u32[]{:S(2)}, u32[]{:S(2)}) collective-permute-start(bf16[128,384]{1,0:T(8,128)(2,1)S(1)} %get-tuple-element.38), channel_id=1, source_target_pairs={{4,0},{8,4},{12,8},{16,12},{20,16},{24,20},{28,24},{0,28},{5,1},{9... | collective-permute-start | bytes 294920 | tf_op jit(solution)/shard_map/ppermute | solution.py:332
